TPU v7x, 32 devices: a whole 2x2x4 slice. The times are simulated.
32 devices in a mesh: row: 8 (over z, x), col: 4 (over y, core).
Axes of the slice: x: 2, y: 2, z: 4, core: 2. Of those that a mesh axis runs over, the one named last changes fastest.
Arguments:
- features: bfloat16 [2048, 512], P(('row', 'col')), may hold values from -0.5 to 0.5
- slot_of_ray: int32 [2048], P(('row', 'col')), may hold values from 0 to 63
- noise: float32 [2048], P(('row', 'col')), may hold values from 0.2 to 1
Outputs:
- front: float32 [2048, 4, 512], P('row', 'col')
- factor: float32 [2048, 1024], P('row')
All inputs are finite; a program needn't handle non-finite values.
Results may differ from a plain program's by a relative error of at most 0.0003.
Values may be sent and summed in bfloat16 or wider, within the bound.
No kernel may reach another device: no remote copies, remote signals or barrier semaphores. Data moves between devices by JAX's collectives and lax.ppermute only.
A program may use at most 64 MiB of HBM per device.

v0:
```python
import jax
import jax.numpy as jnp
from jax import lax
from jax.sharding import PartitionSpec as P

PANEL = 256
PANELS = 4
NT = 64


def broadcast(block, axis, holder):
    block = jnp.where(lax.axis_index(axis) == holder, block, jnp.zeros_like(block))
    return lax.psum(block, axis)


def time_rate():
    length = NT / 8.0
    return 1.0 / (2.0 * length * length)


def shards(features, slot_of_ray, noise):
    ray_dev = noise.shape[0]
    col_count = lax.axis_size("col")
    row_width = ray_dev * col_count
    col_width = ray_dev * lax.axis_size("row")
    row_index = lax.axis_index("row")
    col_index = lax.axis_index("col")
    own_slots = slot_of_ray.astype(jnp.bfloat16)
    row_feat, row_slot = (
        lax.all_gather(features, "col", axis=0, tiled=True),
        lax.all_gather(own_slots, "col", axis=0, tiled=True),
    )
    col_feat, col_slot = (
        lax.all_gather(features, "row", axis=0, tiled=True),
        lax.all_gather(own_slots, "row", axis=0, tiled=True),
    )
    gram_tile = lax.dot_general(
        row_feat, col_feat, (((1,), (1,)), ((), ())), preferred_element_type=jnp.float32
    )
    slot_gap = row_slot.astype(jnp.float32)[:, None] - col_slot.astype(jnp.float32)[None, :]
    row_ray = row_index * row_width + jnp.arange(row_width, dtype=jnp.int32)
    local_cols = jnp.arange(col_width, dtype=jnp.int32)
    col_ray = (local_cols // ray_dev * col_count + col_index) * ray_dev + local_cols % ray_dev
    noise_rows = lax.dynamic_update_slice_in_dim(
        jnp.zeros((row_width,), jnp.float32), noise, col_index * ray_dev, 0
    )
    diagonal = row_ray[:, None] == col_ray[None, :]
    complement = gram_tile * jnp.exp(-slot_gap * slot_gap * time_rate()) + jnp.where(
        diagonal, noise_rows[:, None], 0.0
    )
    identity = jnp.eye(PANEL, dtype=jnp.float32)
    panel_offsets = jnp.arange(PANEL, dtype=jnp.int32)
    columns = []
    for panel_number in range(PANELS):
        panel_start = panel_number * PANEL
        owner_row = panel_start // row_width
        offset = panel_start % row_width
        block_cols = complement[:, owner_row * ray_dev : (owner_row + 1) * ray_dev]
        panel_top = complement[offset : offset + PANEL]
        diag_rows = lax.all_gather(block_cols[offset : offset + PANEL], "col", axis=1, tiled=True)
        corner = jnp.where(row_index == owner_row, diag_rows[:, offset : offset + PANEL], identity)
        triangle = jnp.linalg.cholesky(corner)
        solved = jax.scipy.linalg.solve_triangular(triangle, panel_top, lower=True)
        solved = broadcast(solved, "row", owner_row)
        mine_part = lax.dynamic_slice_in_dim(solved, row_index * ray_dev, ray_dev, 1)
        panel_cols = lax.all_gather(mine_part, "col", axis=1, tiled=True)
        complement = complement - lax.dot_general(
            panel_cols,
            solved,
            (((0,), (0,)), ((), ())),
            precision=lax.Precision.HIGHEST,
            preferred_element_type=jnp.float32,
        )
        below_mask = row_ray[:, None] >= panel_start + panel_offsets[None, :]
        columns.append(jnp.where(below_mask, panel_cols.T, 0.0))
    factor = jnp.concatenate(columns, axis=1)
    eliminated = PANELS * PANEL
    remaining = (row_ray[:, None] >= eliminated) & (col_ray[None, :] >= eliminated)
    front_out = jnp.where(remaining, complement, 0.0).reshape(row_width, 1, col_width)
    return (front_out, factor)


def solution(mesh):
    return jax.shard_map(
        shards,
        mesh=mesh,
        in_specs=(P(("row", "col"), None), P(("row", "col")), P(("row", "col"))),
        out_specs=(P("row", "col", None), P("row", None)),
        check_vma=False,
    )
```

profile of v0, /device:TPU:0, one launch (start us, length us, event | category | flops | bytes accessed | tf_op | source)
XLA Modules:
  0.0 693.0 jit_solution(1782419682293741497)
XLA Ops:
  7.3 7.6 %all_gather.36 = bf16[256,512]{1,0:T(8,128)(2,1)S(1)} all-gather(bf16[64,512]{1,0:T(8,128)(2,1)} %param.6), channel_id=1, replica_groups=mesh['row'=8,'col'=4] {'col'}, dimensions={0}, use_global_device_ids=true | all-gather | bytes 327680 | tf_op jit(solution)/shard_map/all_gather | solution.py:30
  14.9 31.9 %all_gather.37 = bf16[512,512]{1,0:T(8,128)(2,1)S(1)} all-gather(bf16[64,512]{1,0:T(8,128)(2,1)S(1)} %copy-done), channel_id=1, replica_groups=mesh['row'=8,'col'=4] {'row'}, dimensions={0}, use_global_device_ids=true | all-gather | bytes 589824 | tf_op jit(solution)/shard_map/all_gather | solution.py:34
  50.2 5.6 all-reduce.1
  56.1 21.2 %all-reduce.2 = bf16[512]{0:T(512)(128)(2,1)S(1)} all-reduce(bf16[512]{0:T(512)(128)(2,1)S(1)} %dynamic-update-slice.12), channel_id=1, replica_groups=mesh['row'=8,'col'=4] {'row'}, use_global_device_ids=true, to_apply=%add.2 | all-reduce | flops 512 | bytes 2048
  78.5 6.0 all_gather.40
  84.7 11.7 %cholesky.214 = f32[128,128]{1,0:T(8,128)S(1)} custom-call(f32[128,128]{1,0:T(8,128)S(1)} %cholesky.346), custom_call_target="Cholesky" | custom-call | tf_op jit(solution)/shard_map/jit(cholesky)/cholesky | solution.py:62
  96.5 9.8 %custom-call.17 = f32[1,128,128]{1,2,0:T(8,128)S(1)} custom-call(f32[1,128,128]{2,1,0:T(8,128)S(1)} %get-tuple-element.91), custom_call_target="InvertDiagBlocksLowerTriangular" | custom-call | tf_op jit(solution)/shard_map/jit(cholesky)/cholesky | solution.py:62
  106.8 11.7 %cholesky.231 = f32[128,128]{1,0:T(8,128)S(1)} custom-call(f32[128,128]{1,0:T(8,128)S(1)} %convolution_subtract_fusion.11), custom_call_target="Cholesky" | custom-call | tf_op jit(solution)/shard_map/jit(cholesky)/cholesky | solution.py:62
  120.5 4.1 while.8
  121.4 1.3 bitcast_dynamic-update-slice_fusion.8
  123.3 1.3 bitcast_dynamic-update-slice_fusion.8
  124.6 19.7 %custom-call.18 = f32[2,128,128]{1,2,0:T(8,128)S(1)} custom-call(f32[2,128,128]{2,1,0:T(8,128)S(1)} %get-tuple-element.30), custom_call_target="InvertDiagBlocksLowerTriangular" | custom-call | tf_op jit(solution)/shard_map/jit(_solve_triangular)/triangular_solve | solution.py:63
  146.7 70.1 %all-reduce.8.cloned.1.call-done = f32[256,512]{0,1:T(8,128)} async-done(((f32[256,512]{0,1:T(8,128)}), f32[256,512]{0,1:T(8,128)}) %all-reduce.8.cloned.1.call-update) | async-done | bytes 524304 | tf_op jit(solution)/shard_map/psum | solution.py:13
  217.7 5.8 all_gather.41
  223.4 1.7 convolution_subtract_fusion.3
  225.1 5.9 all_gather.42
  231.2 11.7 %cholesky.248 = f32[128,128]{1,0:T(8,128)S(1)} custom-call(f32[128,128]{1,0:T(8,128)S(1)} %cholesky.349), custom_call_target="Cholesky" | custom-call | tf_op jit(solution)/shard_map/jit(cholesky)/cholesky | solution.py:62
  243.6 9.8 %custom-call.19 = f32[1,128,128]{1,2,0:T(8,128)S(1)} custom-call(f32[1,128,128]{2,1,0:T(8,128)S(1)} %get-tuple-element.87), custom_call_target="InvertDiagBlocksLowerTriangular" | custom-call | tf_op jit(solution)/shard_map/jit(cholesky)/cholesky | solution.py:62
  253.9 11.7 %cholesky.265 = f32[128,128]{1,0:T(8,128)S(1)} custom-call(f32[128,128]{1,0:T(8,128)S(1)} %convolution_subtract_fusion.10), custom_call_target="Cholesky" | custom-call | tf_op jit(solution)/shard_map/jit(cholesky)/cholesky | solution.py:62
  267.8 14.9 %while.9 = (s32[]{:T(128)}, f32[256,256]{1,0:T(8,128)S(1)}, s32[2,2]{1,0:T(2,128)S(1)}, f32[2,128,128]{2,1,0:T(8,128)S(1)}, s32[]{:T(128)}) while((s32[]{:T(128)}, f32[256,256]{1,0:T(8,128)S(1)}, s32[2,2]{1,0:T(2,128)S(1)}, f32[2,128,128]{2,1,0:T(8,128)S(1)}, s32[]{:T(128)}) %tuple.106), condition=%wide.while_cond.clone, body=%wide.while_body.clone.sunk | while | flops 2 | bytes 131189 | solution.py:63
  279.1 1.4 bitcast_dynamic-update-slice_fusion.9
  281.2 1.4 bitcast_dynamic-update-slice_fusion.9
  282.6 19.7 %custom-call.20 = f32[2,128,128]{1,2,0:T(8,128)S(1)} custom-call(f32[2,128,128]{2,1,0:T(8,128)S(1)} %get-tuple-element.31), custom_call_target="InvertDiagBlocksLowerTriangular" | custom-call | tf_op jit(solution)/shard_map/jit(_solve_triangular)/triangular_solve | solution.py:63
  304.8 72.0 %all-reduce.10.cloned.1.call-done = f32[256,512]{0,1:T(8,128)} async-done(((f32[256,512]{0,1:T(8,128)}), f32[256,512]{0,1:T(8,128)}) %all-reduce.10.cloned.1.call-update) | async-done | bytes 524304 | tf_op jit(solution)/shard_map/psum | solution.py:13
  377.6 5.8 all_gather.43
  383.4 1.7 convolution_subtract_fusion.2
  385.1 5.9 all_gather.44
  391.1 11.7 %cholesky.282 = f32[128,128]{1,0:T(8,128)S(1)} custom-call(f32[128,128]{1,0:T(8,128)S(1)} %cholesky.352), custom_call_target="Cholesky" | custom-call | tf_op jit(solution)/shard_map/jit(cholesky)/cholesky | solution.py:62
  403.5 9.8 %custom-call.21 = f32[1,128,128]{1,2,0:T(8,128)S(1)} custom-call(f32[1,128,128]{2,1,0:T(8,128)S(1)} %get-tuple-element.83), custom_call_target="InvertDiagBlocksLowerTriangular" | custom-call | tf_op jit(solution)/shard_map/jit(cholesky)/cholesky | solution.py:62
  413.9 11.7 %cholesky.299 = f32[128,128]{1,0:T(8,128)S(1)} custom-call(f32[128,128]{1,0:T(8,128)S(1)} %convolution_subtract_fusion.9), custom_call_target="Cholesky" | custom-call | tf_op jit(solution)/shard_map/jit(cholesky)/cholesky | solution.py:62
  427.7 4.3 while.10
  428.6 1.4 bitcast_dynamic-update-slice_fusion.10
  430.6 1.4 bitcast_dynamic-update-slice_fusion.10
  432.1 19.7 %custom-call.22 = f32[2,128,128]{1,2,0:T(8,128)S(1)} custom-call(f32[2,128,128]{2,1,0:T(8,128)S(1)} %get-tuple-element.32), custom_call_target="InvertDiagBlocksLowerTriangular" | custom-call | tf_op jit(solution)/shard_map/jit(_solve_triangular)/triangular_solve | solution.py:63
  454.2 71.9 %all-reduce.12.cloned.1.call-done = f32[256,512]{0,1:T(8,128)} async-done(((f32[256,512]{0,1:T(8,128)}), f32[256,512]{0,1:T(8,128)}) %all-reduce.12.cloned.1.call-update) | async-done | bytes 524304 | tf_op jit(solution)/shard_map/psum | solution.py:13
  526.9 5.8 all_gather.45
  532.7 1.7 convolution_subtract_fusion.1
  534.4 5.8 all_gather.46
  540.5 11.7 %cholesky.316 = f32[128,128]{1,0:T(8,128)S(1)} custom-call(f32[128,128]{1,0:T(8,128)S(1)} %cholesky.355), custom_call_target="Cholesky" | custom-call | tf_op jit(solution)/shard_map/jit(cholesky)/cholesky | solution.py:62
  552.9 9.8 %custom-call.23 = f32[1,128,128]{1,2,0:T(8,128)S(1)} custom-call(f32[1,128,128]{2,1,0:T(8,128)S(1)} %get-tuple-element.79), custom_call_target="InvertDiagBlocksLowerTriangular" | custom-call | tf_op jit(solution)/shard_map/jit(cholesky)/cholesky | solution.py:62
  563.2 11.7 %cholesky.333 = f32[128,128]{1,0:T(8,128)S(1)} custom-call(f32[128,128]{1,0:T(8,128)S(1)} %convolution_subtract_fusion.8), custom_call_target="Cholesky" | custom-call | tf_op jit(solution)/shard_map/jit(cholesky)/cholesky | solution.py:62
  577.0 4.4 while.11
  577.9 1.4 bitcast_dynamic-update-slice_fusion.11
  580.0 1.4 bitcast_dynamic-update-slice_fusion.11
  581.4 19.7 %custom-call.24 = f32[2,128,128]{1,2,0:T(8,128)S(1)} custom-call(f32[2,128,128]{2,1,0:T(8,128)S(1)} %get-tuple-element.33), custom_call_target="InvertDiagBlocksLowerTriangular" | custom-call | tf_op jit(solution)/shard_map/jit(_solve_triangular)/triangular_solve | solution.py:63
  603.5 71.9 %all-reduce.14.cloned.1.call-done = f32[256,512]{0,1:T(8,128)} async-done(((f32[256,512]{0,1:T(8,128)}), f32[256,512]{0,1:T(8,128)}) %all-reduce.14.cloned.1.call-update) | async-done | bytes 524304 | tf_op jit(solution)/shard_map/psum | solution.py:13
  676.3 5.8 all_gather.47
  682.1 1.7 fusion.1
  (136 shorter events, 31.8 us)
Async XLA Ops:
  7.2 209.7 %all-reduce.8.cloned.1.call-start = ((), (), s32[]{:S(2)}) async-start(), calls=%async_computation | async-start | bytes 1048576 | tf_op jit(solution)/shard_map/psum | solution.py:13
  7.2 7.6 %copy-start = (bf16[64,512]{1,0:T(8,128)(2,1)S(1)}, bf16[64,512]{1,0:T(8,128)(2,1)}, u32[]{:S(2)}) copy-start(bf16[64,512]{1,0:T(8,128)(2,1)} %param.6) | copy-start | bytes 196612
  46.7 0.7 copy-start.4
  47.4 0.7 copy-start.3
  49.2 0.7 copy-start.1
  77.3 0.7 copy-start.2
  146.7 230.1 %all-reduce.10.cloned.1.call-start = ((), (), s32[]{:S(2)}) async-start(), calls=%async_computation.1 | async-start | bytes 1048576 | tf_op jit(solution)/shard_map/psum | solution.py:13
  304.7 221.4 %all-reduce.12.cloned.1.call-start = ((), (), s32[]{:S(2)}) async-start(), calls=%async_computation.2 | async-start | bytes 1048576 | tf_op jit(solution)/shard_map/psum | solution.py:13
  454.1 221.3 %all-reduce.14.cloned.1.call-start = ((), (), s32[]{:S(2)}) async-start(), calls=%async_computation.3 | async-start | bytes 1048576 | tf_op jit(solution)/shard_map/psum | solution.py:13
Sparse Core Ops, SparseCore 0:
  146.8 69.9 all-reduce.7
  304.9 71.8 all-reduce.9
  454.2 71.8 all-reduce.11
  603.6 71.8 all-reduce.13
where the time goes:
time: 703 us; the launch traced here: 693 us
  waiting for transfers between devices  286 us (41%)
  other arithmetic  222 us (32%)
  blocking collectives  113 us (16%)
  local copies, waits for them, and re-layouts  24.9 us (4%)
  between operations  21.3 us (3%)
  matrix products  14.3 us (2%)
  loops' own time  11.7 us (2%)
    psum x4, waiting for transfers between devices, broadcast(): return lax.psum(block, axis)  286 us
    another operation x27, other arithmetic, shards(): triangle = jnp.linalg.cholesky(corner)  138 us
    another operation x9, other arithmetic, shards(): solved = jax.scipy.linalg.solve_triangular(triangle, panel_top, lower=True)  78.8 us
    all_gather x1, blocking collectives, shards(): lax.all_gather(features, 'row', axis=0, tiled=True)  31.9 us
    unnamed x2, blocking collectives  26.9 us
    all_gather x4, blocking collectives, shards(): lax.all_gather(block_cols[offset:offset + PANEL], 'col', axis=1, tiled=True)  23.6 us
    all_gather x4, blocking collectives, shards(): panel_cols = lax.all_gather(mine_part, 'col', axis=1, tiled=True)  23.1 us
    another operation x33, local copies, waits for them, and re-layouts, shards(): solved = jax.scipy.linalg.solve_triangular(triangle, panel_top, lower=True)  16.5 us
  transfers between devices with their start and end apart: 4, of which 4 were waited for; matrix products, arithmetic and copies ran while one was open for 0% of the time, Pallas kernels for 0%

commit v1 on v0

v1 whole, which is shorter than its diff:
```python
import functools

import jax
import jax.numpy as jnp
from jax import lax
from jax.experimental import pallas as pl
from jax.experimental.pallas import tpu as pltpu
from jax.sharding import PartitionSpec as P

PANEL = 256
PANELS = 4
NT = 64
LANES = 128
SUBS = 8
HALF = PANEL // 2
HIGH = lax.Precision.HIGHEST


def time_rate():
    length = NT / 8.0
    return 1.0 / (2.0 * length * length)


def dot(a, b, ca, cb, precision=HIGH):
    return lax.dot_general(
        a, b, (((ca,), (cb,)), ((), ())), precision=precision, preferred_element_type=jnp.float32
    )


def inverse_factor(block):
    count = block.shape[0] // SUBS
    strips = [block[SUBS * t : SUBS * (t + 1), :] for t in range(count)]
    shape = (SUBS, LANES)
    lane = lax.broadcasted_iota(jnp.int32, shape, 1)
    sub = lax.broadcasted_iota(jnp.int32, shape, 0)

    def over_subs(x, k):
        return jnp.broadcast_to(x[k : k + 1, :], shape)

    def over_lanes(x, j):
        return jnp.broadcast_to(x[:, j : j + 1], shape)

    result = []
    for s in range(count):
        base = SUBS * s
        corner = [over_lanes(strips[s], base + j) for j in range(SUBS)]
        own = (lane >= base) & (lane < base + SUBS)
        rows = jnp.where(own, jnp.where(lane - base == sub, 1.0, 0.0), strips[s])
        scaled = rows
        pivots = rows
        for k in range(SUBS):
            pivot = over_subs(corner[k], k)
            inverse = 1.0 / pivot
            lead_row = over_subs(rows, k) * inverse
            here = sub == k
            scaled = jnp.where(here, lead_row, scaled)
            pivots = jnp.where(here, pivot, pivots)
            rows = jnp.where(here, lead_row, rows - corner[k] * lead_row)
            for j in range(k + 1, SUBS):
                entry = over_subs(corner[k], j) * inverse
                corner[j] = jnp.where(here, entry, corner[j] - corner[k] * entry)
        result.append(jnp.where(lane - base <= sub, scaled * jnp.sqrt(pivots), 0.0))
        lead_rows = [over_subs(rows, k) for k in range(SUBS)]
        for t in range(s + 1, count):
            terms = [over_lanes(strips[t], base + k) * lead_rows[k] for k in range(SUBS)]
            while len(terms) > 1:
                terms = [a + b for a, b in zip(terms[::2], terms[1::2])]
            strips[t] = jnp.where(own, 0.0, strips[t]) - terms[0]
    return jnp.concatenate(result, axis=0)


def covariance(feat_a, feat_b, slot_a, slot_b, ray_a, ray_b, noise_b):
    gram = dot(feat_a, feat_b, 1, 1, None)
    gap = slot_a - slot_b
    tile = gram * jnp.exp(-gap * gap * time_rate())
    return tile + jnp.where(ray_a == ray_b, noise_b, 0.0)


def as_column(row):
    return jnp.broadcast_to(row, (LANES, row.shape[1])).T


def kernel(
    lead_feat, row_feat, col_feat, lead_aux, row_aux, col_aux, front, factor, mat, upper, inv
):
    lead = lead_feat.shape[0]
    rows, cols = row_feat.shape[0], col_feat.shape[0]
    row_tiles, col_tiles = rows // PANEL, cols // LANES
    skipped = front.shape[1] - cols

    def fill(feat_ref, aux_ref, count, start):
        @pl.loop(0, count)
        def _(i):
            at = pl.multiple_of(i * LANES, LANES)
            a = feat_ref[pl.ds(at, LANES), :]
            slot_a = as_column(aux_ref[0:1, pl.ds(at, LANES)])
            ray_a = as_column(aux_ref[2:3, pl.ds(at, LANES)])
            to = pl.multiple_of(start + at, LANES)

            @pl.loop(0, lead // LANES)
            def _(j):
                b = pl.multiple_of(j * LANES, LANES)
                mat[pl.ds(to, LANES), pl.ds(b, LANES)] = covariance(
                    a,
                    lead_feat[pl.ds(b, LANES), :],
                    slot_a,
                    lead_aux[0:1, pl.ds(b, LANES)],
                    ray_a,
                    lead_aux[2:3, pl.ds(b, LANES)],
                    lead_aux[1:2, pl.ds(b, LANES)],
                )

            @pl.loop(0, col_tiles)
            def _(j):
                b = pl.multiple_of(j * LANES, LANES)
                mat[pl.ds(to, LANES), pl.ds(pl.multiple_of(lead + b, LANES), LANES)] = covariance(
                    a,
                    col_feat[pl.ds(b, LANES), :],
                    slot_a,
                    col_aux[0:1, pl.ds(b, LANES)],
                    ray_a,
                    col_aux[2:3, pl.ds(b, LANES)],
                    col_aux[1:2, pl.ds(b, LANES)],
                )

    fill(lead_feat, lead_aux, lead // LANES, 0)
    fill(row_feat, row_aux, rows // LANES, lead)

    panels = lead // PANEL
    width = lead + cols

    @pl.loop(0, panels)
    def _(p):
        at = pl.multiple_of(p * PANEL, PANEL)
        mid = pl.multiple_of(at + HALF, HALF)
        inv_a = inverse_factor(mat[pl.ds(at, HALF), pl.ds(at, HALF)])
        cross = dot(inv_a, mat[pl.ds(at, HALF), pl.ds(mid, HALF)], 1, 0)
        inv_b = inverse_factor(
            mat[pl.ds(mid, HALF), pl.ds(mid, HALF)] - dot(cross, cross, 0, 0)
        )
        inv[0:HALF, 0:HALF] = inv_a
        inv[0:HALF, HALF:PANEL] = jnp.zeros((HALF, HALF), jnp.float32)
        inv[HALF:PANEL, HALF:PANEL] = inv_b
        inv[HALF:PANEL, 0:HALF] = -dot(inv_b, dot(cross, inv_a, 0, 0), 1, 0)

        first = (at + PANEL) // LANES

        @pl.loop(first, width // LANES)
        def _(j):
            b = pl.multiple_of(j * LANES, LANES)
            upper[:, pl.ds(b, LANES)] = dot(
                inv[...], mat[pl.ds(at, PANEL), pl.ds(b, LANES)], 1, 0
            )

        @pl.loop(p + 1, panels)
        def _(q):
            row = pl.multiple_of(q * PANEL, PANEL)
            lower = upper[:, pl.ds(row, PANEL)]

            @pl.loop(row // LANES, width // LANES)
            def _(j):
                b = pl.multiple_of(j * LANES, LANES)
                mat[pl.ds(row, PANEL), pl.ds(b, LANES)] -= dot(
                    lower, upper[:, pl.ds(b, LANES)], 0, 0
                )

        @pl.loop(0, row_tiles)
        def _(i):
            here = pl.multiple_of(i * PANEL, PANEL)
            row = pl.multiple_of(lead + here, PANEL)
            solved = dot(mat[pl.ds(row, PANEL), pl.ds(at, PANEL)], inv[...], 1, 1)
            ray = as_column(row_aux[2:3, pl.ds(here, PANEL)])
            for half in range(2):
                offset = at + half * LANES
                lanes = lax.broadcasted_iota(jnp.int32, (PANEL, LANES), 1) + offset
                factor[pl.ds(here, PANEL), pl.ds(pl.multiple_of(offset, LANES), LANES)] = jnp.where(
                    ray >= lanes.astype(jnp.float32),
                    solved[:, half * LANES : (half + 1) * LANES],
                    0.0,
                )

            @pl.loop(first, width // LANES)
            def _(j):
                b = pl.multiple_of(j * LANES, LANES)
                mat[pl.ds(row, PANEL), pl.ds(b, LANES)] -= dot(
                    solved, upper[:, pl.ds(b, LANES)], 1, 0
                )

    if skipped:
        front[:, 0:skipped] = jnp.zeros((rows, skipped), jnp.float32)
    keep = row_aux[2, 0] >= lead

    @pl.loop(0, col_tiles)
    def _(j):
        b = pl.multiple_of(j * LANES, LANES)
        front[:, pl.ds(pl.multiple_of(skipped + b, LANES), LANES)] = jnp.where(
            keep, mat[pl.ds(lead, rows), pl.ds(pl.multiple_of(lead + b, LANES), LANES)], 0.0
        )


def shards(features, slot_of_ray, noise):
    ray_dev = noise.shape[0]
    row_count, col_count = lax.axis_size("row"), lax.axis_size("col")
    row_width, col_width = ray_dev * col_count, ray_dev * row_count
    row_index, col_index = lax.axis_index("row"), lax.axis_index("col")
    lead = PANELS * PANEL
    own = jnp.concatenate([slot_of_ray.astype(jnp.float32), noise])[None]
    every = lax.all_gather(features, ("row", "col"), axis=0, tiled=True)
    aux = lax.all_gather(own, ("row", "col"), axis=0, tiled=True)
    rays = row_count * row_width
    aux = aux.reshape(rays // ray_dev, 2, ray_dev).transpose(1, 0, 2).reshape(2, rays)
    aux = jnp.concatenate([aux, jnp.arange(rays, dtype=jnp.float32)[None]])
    skipped_blocks = lead // row_width
    row_feat = lax.dynamic_slice_in_dim(every, row_index * row_width, row_width, 0)
    row_aux = lax.dynamic_slice_in_dim(aux, row_index * row_width, row_width, 1)
    blocks = every.reshape(row_count, col_count, ray_dev, -1)[skipped_blocks:]
    col_feat = lax.dynamic_index_in_dim(blocks, col_index, 1, False).reshape(-1, features.shape[1])
    aux_blocks = aux.reshape(3, row_count, col_count, ray_dev)[:, skipped_blocks:]
    col_aux = lax.dynamic_index_in_dim(aux_blocks, col_index, 2, False).reshape(3, -1)
    cols = col_feat.shape[0]
    front, factor = pl.pallas_call(
        kernel,
        out_shape=(
            jax.ShapeDtypeStruct((row_width, col_width), jnp.float32),
            jax.ShapeDtypeStruct((row_width, lead), jnp.float32),
        ),
        scratch_shapes=[
            pltpu.VMEM((lead + row_width, lead + cols), jnp.float32),
            pltpu.VMEM((PANEL, lead + cols), jnp.float32),
            pltpu.VMEM((PANEL, PANEL), jnp.float32),
        ],
        name="panels",
    )(every[:lead], row_feat, col_feat, aux[:, :lead], row_aux, col_aux)
    return front.reshape(row_width, 1, col_width), factor


def solution(mesh):
    return jax.shard_map(
        shards,
        mesh=mesh,
        in_specs=(P(("row", "col"), None), P(("row", "col")), P(("row", "col"))),
        out_specs=(P("row", "col", None), P("row", None)),
        check_vma=False,
    )
```

time: 703 us -> 179 us (0.25); the launches traced: 693 us -> 179 us
  waiting for transfers between devices: 286 us -> 14.6 us
  other arithmetic: 222 us -> 3.41 us
  Pallas kernels: 0 us -> 94.5 us
  blocking collectives: 113 us -> 43.3 us
  local copies, waits for them, and re-layouts: 24.9 us -> 8.8 us
  matrix products: 14.3 us -> 0 us
  loops' own time: 11.7 us -> 0 us
  between operations: 21.3 us -> 14.1 us
    psum x4 -> x0, waiting for transfers between devices: 286 us -> none  [broadcast(): return lax.psum(block, axis)]
    another operation x36 -> x0, other arithmetic: 217 us -> none  [the longest x27 138 us: shards(): triangle = jnp.linalg.cholesky(corner)]
    pallas_call x0 -> x1, Pallas kernels: none -> 94.5 us  [shards(): pl.pallas_call(kernel, out_shape=(jax.ShapeDtypeStruct((row_width, col_wi...]
    all_gather x10 -> x1, blocking collectives: 86.1 us -> 43.3 us  [shards(): aux = lax.all_gather(own, ('row', 'col'), axis=0, tiled=True)]
    unnamed x2 -> x0, blocking collectives: 26.9 us -> none
    another operation x41 -> x0, local copies, waits for them, and re-layouts: 16.7 us -> none  [the longest x33 16.5 us: shards(): solved = jax.scipy.linalg.solve_triangular(triangle, panel_top, lower=True)]
    all_gather x0 -> x1, waiting for transfers between devices: none -> 13.9 us  [shards(): every = lax.all_gather(features, ('row', 'col'), axis=0, tiled=True)]
    another operation x4 -> x0, loops' own time: 11.7 us -> none  [shards(): solved = jax.scipy.linalg.solve_triangular(triangle, panel_top, lower=True)]
  transfers between devices with their start and end apart: 4 -> 1, of which waited for: 4 -> 1; matrix products, arithmetic and copies ran while one was open for 0% -> 3% of each run, Pallas kernels for 0% -> 0%
where the time goes in v1:
time: 179 us
  Pallas kernels  94.5 us (53%)
  blocking collectives  43.3 us (24%)
  waiting for transfers between devices  14.6 us (8%)
  between operations  14.1 us (8%)
  local copies, waits for them, and re-layouts  8.8 us (5%)
  other arithmetic  3.41 us (2%)
    pallas_call x1, Pallas kernels, shards(): pl.pallas_call(kernel, out_shape=(jax.ShapeDtypeStruct((row_width, col_wi...  94.5 us
    all_gather x1, blocking collectives, shards(): aux = lax.all_gather(own, ('row', 'col'), axis=0, tiled=True)  43.3 us
    all_gather x1, waiting for transfers between devices, shards(): every = lax.all_gather(features, ('row', 'col'), axis=0, tiled=True)  13.9 us
  transfers between devices with their start and end apart: 1, of which 1 were waited for; matrix products, arithmetic and copies ran while one was open for 3% of the time, Pallas kernels for 0%

profile of v1, /device:TPU:0, one launch (start us, length us, event | category | flops | bytes accessed | tf_op | source)
XLA Modules:
  0.0 178.7 jit_solution(12011408889978044315)
XLA Ops:
  7.2 0.0 all-gather.4.cloned.1.call-start
  7.2 0.7 all-gather.4.cloned.1.call-update
  7.9 0.7 convert_element_type.3
  8.6 0.7 maximum_bitcast_fusion
  9.3 43.3 %all-gather.1 = f32[32,1,128]{2,1,0:T(1,128)S(1)} all-gather(f32[1,1,128]{2,1,0:T(1,128)S(1)} %maximum_bitcast_fusion), channel_id=2, replica_groups=mesh['row'=8,'col'=4] {'row','col'}, dimensions={0}, use_global_device_ids=true | all-gather | bytes 16896 | tf_op jit(solution)/shard_map/all_gather | solution.py:209
  52.6 0.5 broadcast.20
  53.1 0.7 reduce.7
  53.8 0.1 reshape.49
  53.9 0.1 reshape.50
  54.0 0.7 reshape.51.col_aux
  54.7 0.7 fusion.3.row_aux
  55.4 0.6 fusion.lead_aux
  56.0 13.9 %all-gather.4.cloned.1.call-done = bf16[2048,512]{1,0:T(8,128)(2,1)} async-done(((bf16[64,512]{1,0:T(8,128)(2,1)}), bf16[2048,512]{1,0:T(8,128)(2,1)}) %all-gather.4.cloned.1.call-update) | async-done | bytes 2097168 | tf_op jit(solution)/shard_map/all_gather | solution.py:208
  69.9 2.7 %fusion.4 = (bf16[1024,512]{1,0:T(8,128)(2,1)S(1)}, bf16[1024,512]{1,0:T(8,128)(2,1)}) fusion(bf16[2048,512]{1,0:T(8,128)(2,1)} %all-gather.4.cloned.1.call-done), kind=kLoop, calls=%fused_computation.14 | loop fusion | bytes 4194304 | tf_op jit(solution)/shard_map/slice | solution.py:216
  72.5 0.7 constant_dynamic-slice_fusion
  73.3 1.7 constant_dynamic-slice_fusion.1.row_feat
  75.0 94.5 %panels.1 = (f32[256,512]{1,0:T(8,128)}, f32[256,1024]{1,0:T(8,128)}) custom-call(bf16[1024,512]{1,0:T(8,128)(2,1)} %get-tuple-element.15.lead_feat, bf16[256,512]{1,0:T(8,128)(2,1)} %constant_dynamic-slice_fusion.1.row_feat, bf16[256,512]{1,0:T(8,128)(2,1)} %bitcast.10, f32[3,1024]{1,0:T(4,128)} %fusion.lead_aux, f32[3,256]{1,0:T(4,128)} %fusion.3.row_aux, ...), custom_call_target="tpu_custom_call" | custom-call | tf_op jit(solution)/shard_map/panels/pallas_call | solution.py:221
  169.5 2.4 %copy.16 = f32[256,1,512]{2,1,0:T(1,128)} copy(f32[256,1,512]{2,0,1:T(8,128)} %bitcast.11) | data formatting | bytes 1048576
  (3 shorter events, 0.1 us)
Async XLA Ops:
  7.2 62.7 %all-gather.4.cloned.1.call-start = ((), (), s32[]{:S(2)}) async-start(), calls=%async_computation | async-start | bytes 2162688 | tf_op jit(solution)/shard_map/all_gather | solution.py:208
Sparse Core Ops, SparseCore 0:
  10.8 59.0 all-gather.3

commit v2 on v1

v2 whole, which is shorter than its diff:
```python
import functools

import jax
import jax.numpy as jnp
from jax import lax
from jax.experimental import pallas as pl
from jax.experimental.pallas import tpu as pltpu
from jax.sharding import PartitionSpec as P

PANEL = 256
PANELS = 4
NT = 64
LANES = 128
SUBS = 8
HALF = PANEL // 2


def time_rate():
    length = NT / 8.0
    return 1.0 / (2.0 * length * length)


def dot(a, b, ca, cb):
    return lax.dot_general(
        a,
        b,
        (((ca,), (cb,)), ((), ())),
        precision=lax.Precision.HIGHEST,
        preferred_element_type=jnp.float32,
    )


def inverse_factor(block):
    count = block.shape[0] // SUBS
    strips = [block[SUBS * t : SUBS * (t + 1), :] for t in range(count)]
    shape = (SUBS, LANES)
    lane = lax.broadcasted_iota(jnp.int32, shape, 1)
    sub = lax.broadcasted_iota(jnp.int32, shape, 0)

    def over_subs(x, k):
        return jnp.broadcast_to(x[k : k + 1, :], shape)

    def over_lanes(x, j):
        return jnp.broadcast_to(x[:, j : j + 1], shape)

    result = []
    for s in range(count):
        base = SUBS * s
        corner = [over_lanes(strips[s], base + j) for j in range(SUBS)]
        own = (lane >= base) & (lane < base + SUBS)
        rows = jnp.where(own, jnp.where(lane - base == sub, 1.0, 0.0), strips[s])
        scaled = rows
        pivots = rows
        for k in range(SUBS):
            pivot = over_subs(corner[k], k)
            inverse = 1.0 / pivot
            lead_row = over_subs(rows, k) * inverse
            here = sub == k
            scaled = jnp.where(here, lead_row, scaled)
            pivots = jnp.where(here, pivot, pivots)
            rows = jnp.where(here, lead_row, rows - corner[k] * lead_row)
            for j in range(k + 1, SUBS):
                entry = over_subs(corner[k], j) * inverse
                corner[j] = jnp.where(here, entry, corner[j] - corner[k] * entry)
        result.append(jnp.where(lane - base <= sub, scaled * jnp.sqrt(pivots), 0.0))
        lead_rows = [over_subs(rows, k) for k in range(SUBS)]
        for t in range(s + 1, count):
            terms = [over_lanes(strips[t], base + k) * lead_rows[k] for k in range(SUBS)]
            while len(terms) > 1:
                terms = [a + b for a, b in zip(terms[::2], terms[1::2])]
            strips[t] = jnp.where(own, 0.0, strips[t]) - terms[0]
    return jnp.concatenate(result, axis=0)


def as_column(row):
    return jnp.broadcast_to(row, (LANES, LANES)).T


def reversed_bits(value, bits):
    out = 0
    for k in range(bits):
        out = out | (((value >> k) & 1) << (bits - 1 - k))
    return out


def bits_of(count):
    return count.bit_length() - 1


def kernel(*refs, ray_dev, row_count, col_count, lead, tops):
    near, near_x = refs[:2]
    lists = [refs[2 + k * tops : 2 + (k + 1) * tops] for k in range(4)]
    side, side_x, core, core_x = lists
    front, factor, feat, slot, noise, ray, mat, upper, inv = refs[2 + 4 * tops :]
    row_index, col_index = lax.axis_index("row"), lax.axis_index("col")
    rows = ray_dev * col_count
    pair_count = near.shape[0]
    lead_pairs = lead // rows // 2
    cols = (pair_count - lead_pairs) * 2 * ray_dev
    row_pair, odd_row = row_index // 2, row_index % 2
    col_pair, odd_col = col_index // 2, col_index % 2
    lanes = lax.broadcasted_iota(jnp.int32, (1, LANES), 1)

    def aux_of(block):
        line = block[ray_dev : ray_dev + SUBS, :].astype(jnp.float32)[0:1]
        parts = [line[:, LANES * k : LANES * (k + 1)] for k in range(4)]
        return parts[0], parts[1] + parts[2] + parts[3]

    def put(mine, other, odd, to, numbers):
        here = pl.multiple_of(to + odd * ray_dev, ray_dev)
        there = pl.multiple_of(to + (1 - odd) * ray_dev, ray_dev)
        feat[pl.ds(here, ray_dev), :] = mine[:ray_dev, :]
        feat[pl.ds(there, ray_dev), :] = other[:ray_dev, :]
        tile = to // LANES
        for out, a, b in zip((slot, noise), aux_of(mine), aux_of(other)):
            even, late = jnp.where(odd == 0, a, b), jnp.where(odd == 0, b, a)
            out[pl.ds(tile, 1), :] = even + pltpu.roll(late, ray_dev, 1)
        ray[pl.ds(tile, 1), :] = numbers.astype(jnp.float32)

    low_bits = bits_of(lead_pairs)
    for k in range(lead_pairs):
        pair = (row_pair % lead_pairs) ^ reversed_bits(k, low_bits)
        for bit in range(2):
            row = pair * 2 + (odd_row if bit == 0 else 1 - odd_row)
            for top in range(tops):
                at = (col_pair ^ reversed_bits(top, bits_of(tops))) * LANES + row * rows
                mine, other = (side, core) if bit == 0 else (side_x, core_x)
                put(mine[top][k], other[top][k], odd_col, at, lanes + at)
    for top in range(tops):
        at = (col_pair ^ reversed_bits(top, bits_of(tops))) * LANES
        numbers = lanes + (row_index * rows + at)
        put(side[top][lead_pairs], core[top][lead_pairs], odd_col, lead + at, numbers)
    for place in range(pair_count):
        pair = row_pair ^ reversed_bits(place, bits_of(pair_count))

        @pl.when(pair >= lead_pairs)
        def _():
            numbers = ((pair * 2 + lanes // ray_dev) * col_count + col_index) * ray_dev
            numbers = numbers + lanes % ray_dev
            at = lead + rows + (pair - lead_pairs) * LANES
            put(near[place], near_x[place], odd_row, at, numbers)

    if cols % PANEL:
        feat[lead + rows + cols :, :] = jnp.zeros((PANEL - cols % PANEL, feat.shape[1]), feat.dtype)
        for out in (slot, noise, ray):
            out[(lead + rows + cols) // LANES :, :] = jnp.full((1, LANES), -1.0, jnp.float32)

    panels, row_tiles = lead // PANEL, rows // PANEL
    col_tiles = (cols + PANEL - 1) // PANEL
    wide = panels + col_tiles

    def tile(i):
        return pl.ds(pl.multiple_of(i * PANEL, PANEL), PANEL)

    def column(source, i):
        return jnp.concatenate([as_column(source[pl.ds(2 * i + k, 1), :]) for k in range(2)], axis=0)

    def line(source, i):
        return [source[pl.ds(2 * i + k, 1), :] for k in range(2)]

    def spot(j):
        return jnp.where(j < panels, j, j + row_tiles)

    def tile_of(i, j, slot_a, ray_a):
        gram = lax.dot_general(
            feat[tile(i), :],
            feat[tile(j), :],
            (((1,), (1,)), ((), ())),
            preferred_element_type=jnp.float32,
        )
        halves = []
        slots, noises, rays = line(slot, j), line(noise, j), line(ray, j)
        for k in range(2):
            gap = slot_a - slots[k]
            part = gram[:, k * LANES : (k + 1) * LANES] * jnp.exp(-gap * gap * time_rate())
            halves.append(part + jnp.where(ray_a == rays[k], noises[k], 0.0))
        return jnp.concatenate(halves, axis=1)

    @pl.loop(0, panels + row_tiles)
    def _(i):
        slot_a, ray_a = column(slot, i), column(ray, i)

        @pl.loop(jnp.where(i < panels, i, 0), wide)
        def _(j):
            mat[tile(i), tile(j)] = tile_of(i, spot(j), slot_a, ray_a)

    @pl.loop(0, panels)
    def _(p):
        at = pl.multiple_of(p * PANEL, PANEL)
        mid = pl.multiple_of(at + HALF, HALF)
        inv_a = inverse_factor(mat[pl.ds(at, HALF), pl.ds(at, HALF)])
        cross = dot(inv_a, mat[pl.ds(at, HALF), pl.ds(mid, HALF)], 1, 0)
        inv_b = inverse_factor(mat[pl.ds(mid, HALF), pl.ds(mid, HALF)] - dot(cross, cross, 0, 0))
        inv[0:HALF, 0:HALF] = inv_a
        inv[0:HALF, HALF:PANEL] = jnp.zeros((HALF, HALF), jnp.float32)
        inv[HALF:PANEL, HALF:PANEL] = inv_b
        inv[HALF:PANEL, 0:HALF] = -dot(inv_b, dot(cross, inv_a, 0, 0), 1, 0)

        @pl.loop(p + 1, wide)
        def _(j):
            upper[:, tile(j)] = dot(inv[...], mat[tile(p), tile(j)], 1, 0)

        @pl.loop(p + 1, panels)
        def _(q):
            @pl.loop(q, wide)
            def _(j):
                mat[tile(q), tile(j)] -= dot(upper[:, tile(q)], upper[:, tile(j)], 0, 0)

        @pl.loop(0, row_tiles)
        def _(i):
            solved = dot(mat[tile(panels + i), tile(p)], inv[...], 1, 1)
            ray_a = column(ray, panels + i)
            kept = [
                jnp.where(ray_a >= line_k, solved[:, k * LANES : (k + 1) * LANES], 0.0)
                for k, line_k in enumerate(line(ray, p))
            ]
            factor[tile(i), tile(p)] = jnp.concatenate(kept, axis=1)

            @pl.loop(p + 1, wide)
            def _(j):
                mat[tile(panels + i), tile(j)] -= dot(solved, upper[:, tile(j)], 1, 0)

    skipped = front.shape[1] - cols
    front[:, 0:skipped] = jnp.zeros((rows, skipped), jnp.float32)
    front[:, skipped:] = jnp.where(
        row_index * rows >= lead, mat[lead : lead + rows, lead : lead + cols], 0.0
    )


def packed(features, slot_of_ray, noise):
    high = lax.reduce_precision(noise, 8, 7)
    middle = lax.reduce_precision(noise - high, 8, 7)
    terms = jnp.stack([slot_of_ray.astype(jnp.float32), high, middle, noise - high - middle])
    ray_dev, width = features.shape
    aux = jnp.pad(terms, ((0, 0), (0, LANES - ray_dev))).reshape(1, 4 * LANES)
    aux = jnp.pad(aux, ((0, SUBS - 1), (0, width - 4 * LANES))).astype(features.dtype)
    return jnp.concatenate([features, aux])


def shards(features, slot_of_ray, noise):
    ray_dev = noise.shape[0]
    row_count, col_count = lax.axis_size("row"), lax.axis_size("col")
    rows, col_width = ray_dev * col_count, ray_dev * row_count
    row_index = lax.axis_index("row")
    lead = PANELS * PANEL
    row_bits, col_bits = bits_of(row_count), bits_of(col_count)
    tops = col_count // 2
    lead_pairs = lead // rows // 2

    def other(value, axis, bit):
        count = lax.axis_size(axis)
        return lax.ppermute(value, axis, [(k, k ^ (1 << bit)) for k in range(count)])

    near = packed(features, slot_of_ray, noise)[None]
    own = near
    for bit in reversed(range(1, row_bits)):
        near = jnp.concatenate([near, other(near, "row", bit)])
    high_bits = row_bits - 1 - bits_of(lead_pairs)
    group = reversed_bits(row_index >> (row_bits - high_bits), high_bits)

    def leading(blocks):
        split = blocks.reshape(lead_pairs, 1 << high_bits, *blocks.shape[1:])
        return lax.dynamic_index_in_dim(split, group, 1, False)

    near_x = other(near, "row", 0)
    side = [jnp.concatenate([leading(near), own])]
    side_x = [leading(near_x)]
    for bit in reversed(range(1, col_bits)):
        side += [other(value, "col", bit) for value in side]
        side_x += [other(value, "col", bit) for value in side_x]
    core = [other(value, "col", 0) for value in side]
    core_x = [other(value, "col", 0) for value in side_x]

    cols = col_width - lead // col_count
    padded = -(-cols // PANEL) * PANEL
    rays = lead + rows + padded
    front, factor = pl.pallas_call(
        functools.partial(
            kernel, ray_dev=ray_dev, row_count=row_count, col_count=col_count, lead=lead, tops=tops
        ),
        out_shape=(
            jax.ShapeDtypeStruct((rows, col_width), jnp.float32),
            jax.ShapeDtypeStruct((rows, lead), jnp.float32),
        ),
        scratch_shapes=[
            pltpu.VMEM((rays, features.shape[1]), features.dtype),
            *[pltpu.VMEM((rays // LANES, LANES), jnp.float32)] * 3,
            pltpu.VMEM((lead + rows, lead + padded), jnp.float32),
            pltpu.VMEM((PANEL, lead + padded), jnp.float32),
            pltpu.VMEM((PANEL, PANEL), jnp.float32),
        ],
        name="panels",
    )(near, near_x, *side, *side_x, *core, *core_x)
    return front.reshape(rows, 1, col_width), factor


def solution(mesh):
    return jax.shard_map(
        shards,
        mesh=mesh,
        in_specs=(P(("row", "col"), None), P(("row", "col")), P(("row", "col"))),
        out_specs=(P("row", "col", None), P("row", None)),
        check_vma=False,
    )
```

time: 179 us -> 98.1 us (0.55)
  blocking collectives: 43.3 us -> 0 us
  Pallas kernels: 94.5 us -> 65.7 us
  between operations: 14.1 us -> 0.81 us
  starting transfers between devices: 0.04 us -> 10.5 us
  local copies, waits for them, and re-layouts: 8.8 us -> 3.09 us
  other arithmetic: 3.41 us -> 1.61 us
    all_gather x1 -> x0, blocking collectives: 43.3 us -> none  [shards(): aux = lax.all_gather(own, ('row', 'col'), axis=0, tiled=True)]
    pallas_call x1, Pallas kernels: 94.5 us -> 65.7 us  [shards(): pl.pallas_call(functools.partial(kernel, ray_dev=ray_dev, row_count=row_c...]
    ppermute x0 -> x9, waiting for transfers between devices: none -> 16 us  [other(): return lax.ppermute(value, axis, [(k, k ^ 1 << bit) for k in range(count)])]
    all_gather x1 -> x0, waiting for transfers between devices: 13.9 us -> none  [shards(): every = lax.all_gather(features, ('row', 'col'), axis=0, tiled=True)]
    ppermute x0 -> x9, starting transfers between devices: none -> 10.5 us  [other(): return lax.ppermute(value, axis, [(k, k ^ 1 << bit) for k in range(count)])]
    slice x1 -> x0, local copies, waits for them, and re-layouts: 2.66 us -> none  [shards(): blocks = every.reshape(row_count, col_count, ray_dev, -1)[skipped_blocks:]]
    dynamic_slice x2 -> x0, local copies, waits for them, and re-layouts: 2.41 us -> none  [the longest x1 1.67 us: shards(): lax.dynamic_slice_in_dim(every, row_index * row_width, row_width, 0)]
  transfers between devices with their start and end apart: 1 -> 9, of which waited for: 1 -> 6; matrix products, arithmetic and copies ran while one was open for 3% -> 0% of each run, Pallas kernels for 0% -> 0%
where the time goes in v2:
time: 98.1 us; the launch traced here: 97.6 us
  Pallas kernels  65.7 us (67%)
  waiting for transfers between devices  16 us (16%)
  starting transfers between devices  10.5 us (11%)
  local copies, waits for them, and re-layouts  3.09 us (3%)
  other arithmetic  1.61 us (2%)
    pallas_call x1, Pallas kernels, shards(): pl.pallas_call(functools.partial(kernel, ray_dev=ray_dev, row_count=row_c...  65.7 us
    ppermute x9, waiting for transfers between devices, other(): return lax.ppermute(value, axis, [(k, k ^ 1 << bit) for k in range(count)])  16 us
    ppermute x9, starting transfers between devices, other(): return lax.ppermute(value, axis, [(k, k ^ 1 << bit) for k in range(count)])  10.5 us
    unnamed x24, local copies, waits for them, and re-layouts  3.07 us
  transfers between devices with their start and end apart: 9, of which 6 were waited for; matrix products, arithmetic and copies ran while one was open for 0% of the time, Pallas kernels for 0%

profile of v2, /device:TPU:0, one launch (start us, length us, event | category | flops | bytes accessed | tf_op | source)
XLA Modules:
  0.0 97.6 jit_solution(13898792819742603978)
XLA Ops:
  0.6 0.0 copy-start.10
  0.6 0.7 convert_bitcast_fusion
  1.3 0.0 copy-done.10
  1.3 0.8 fusion.2
  2.2 4.1 %collective-permute-start = (bf16[1,72,512]{2,1,0:T(8,128)(2,1)S(1)}, bf16[1,72,512]{2,1,0:T(8,128)(2,1)S(1)}, u32[]{:S(2)}, u32[]{:S(2)}) collective-permute-start(bf16[1,72,512]{2,1,0:T(8,128)(2,1)S(1)} %fusion.2), channel_id=1, source_target_pairs={{0,16},{4,20},{8,24},{12,28},{16,0},{20,4},{24,8},{28,12},{1,17},{... | collective-permute-start | bytes 221192 | tf_op jit(solution)/shard_map/ppermute | solution.py:252
  6.3 3.9 %collective-permute-done = bf16[1,72,512]{2,1,0:T(8,128)(2,1)S(1)} collective-permute-done((bf16[1,72,512]{2,1,0:T(8,128)(2,1)S(1)}, bf16[1,72,512]{2,1,0:T(8,128)(2,1)S(1)}, u32[]{:S(2)}, u32[]{:S(2)}) %collective-permute-start) | collective-permute-done | bytes 73760 | tf_op jit(solution)/shard_map/ppermute | solution.py:252
  10.2 0.7 collective-permute-start.1
  10.9 4.5 %collective-permute-done.1 = bf16[2,72,512]{2,1,0:T(8,128)(2,1)S(1)} collective-permute-done((bf16[2,72,512]{2,1,0:T(8,128)(2,1)S(1)}, bf16[2,72,512]{2,1,0:T(8,128)(2,1)S(1)}, u32[]{:S(2)}, u32[]{:S(2)}) %collective-permute-start.1) | collective-permute-done | bytes 147488 | tf_op jit(solution)/shard_map/ppermute | solution.py:252
  15.4 0.0 copy-start
  15.4 1.8 %collective-permute-start.2 = (bf16[4,72,512]{2,1,0:T(8,128)(2,1)S(1)}, bf16[4,72,512]{2,1,0:T(8,128)(2,1)S(1)}, u32[]{:S(2)}, u32[]{:S(2)}) collective-permute-start(bf16[4,72,512]{2,1,0:T(8,128)(2,1)S(1)} %pad_maximum_fusion.refs_0_), channel_id=1, source_target_pairs={{0,4},{4,0},{8,12},{12,8},{16,20},{20,16},{24,28},{28,24},{1,5},{5... | collective-permute-start | bytes 884744 | tf_op jit(solution)/shard_map/ppermute | solution.py:252
  17.3 0.0 copy-done
  17.3 0.0 copy-start.1
  17.3 1.6 %collective-permute-start.3 = (bf16[3,72,512]{2,1,0:T(8,128)(2,1)S(1)}, bf16[3,72,512]{2,1,0:T(8,128)(2,1)S(1)}, u32[]{:S(2)}, u32[]{:S(2)}) collective-permute-start(bf16[3,72,512]{2,1,0:T(8,128)(2,1)S(1)} %pad_maximum_fusion.1.refs_2_), channel_id=1, source_target_pairs={{0,2},{1,3},{2,0},{3,1},{4,6},{5,7},{6,4},{7,5},{8,10},{9,11},{10,... | collective-permute-start | bytes 663560 | tf_op jit(solution)/shard_map/ppermute | solution.py:252
  18.9 3.4 %collective-permute-done.2.refs_1_ = bf16[4,72,512]{2,1,0:T(8,128)(2,1)S(1)} collective-permute-done((bf16[4,72,512]{2,1,0:T(8,128)(2,1)S(1)}, bf16[4,72,512]{2,1,0:T(8,128)(2,1)S(1)}, u32[]{:S(2)}, u32[]{:S(2)}) %collective-permute-start.2) | collective-permute-done | bytes 294944 | tf_op jit(solution)/shard_map/ppermute | solution.py:252
  22.2 0.0 copy-start.2
  22.2 0.0 copy-start.3
  22.3 1.8 %collective-permute-start.4 = (bf16[2,72,512]{2,1,0:T(8,128)(2,1)S(1)}, bf16[2,72,512]{2,1,0:T(8,128)(2,1)S(1)}, u32[]{:S(2)}, u32[]{:S(2)}) collective-permute-start(bf16[2,72,512]{2,1,0:T(8,128)(2,1)S(1)} %dynamic-slice_bitcast_fusion.refs_4_), channel_id=1, source_target_pairs={{0,2},{1,3},{2,0},{3,1},{4,6},{5,7},{6,4},{7,5},{8,10},{9,11},{10,... | collective-permute-start | bytes 442376 | tf_op jit(solution)/shard_map/ppermute | solution.py:252
  24.1 0.0 collective-permute-start.5
  24.1 0.8 collective-permute-done.3.refs_3_
  24.9 0.0 copy-start.4
  24.9 0.0 collective-permute-start.6
  24.9 0.5 collective-permute-start.7
  25.4 2.1 %collective-permute-done.4.refs_5_ = bf16[2,72,512]{2,1,0:T(8,128)(2,1)S(1)} collective-permute-done((bf16[2,72,512]{2,1,0:T(8,128)(2,1)S(1)}, bf16[2,72,512]{2,1,0:T(8,128)(2,1)S(1)}, u32[]{:S(2)}, u32[]{:S(2)}) %collective-permute-start.4) | collective-permute-done | bytes 147488 | tf_op jit(solution)/shard_map/ppermute | solution.py:252
  27.5 0.0 copy-start.7
  27.5 0.0 collective-permute-start.8
  27.5 0.0 collective-permute-done.5.refs_6_
  27.5 0.0 copy-start.5
  27.5 0.0 collective-permute-done.6.refs_7_
  27.5 0.0 copy-start.6
  27.5 0.0 collective-permute-done.7.refs_8_
  27.5 0.0 copy-start.8
  27.5 1.3 %collective-permute-done.8.refs_9_ = bf16[2,72,512]{2,1,0:T(8,128)(2,1)S(1)} collective-permute-done((bf16[2,72,512]{2,1,0:T(8,128)(2,1)S(1)}, bf16[2,72,512]{2,1,0:T(8,128)(2,1)S(1)}, u32[]{:S(2)}, u32[]{:S(2)}) %collective-permute-start.8) | collective-permute-done | bytes 147488 | tf_op jit(solution)/shard_map/ppermute | solution.py:252
  28.8 0.0 copy-done.1
  28.8 0.0 copy-done.2
  28.8 0.0 copy-done.3
  28.9 0.0 copy-done.4
  28.9 0.0 copy-done.7
  28.9 0.0 copy-done.5
  28.9 0.0 copy-done.6
  28.9 0.0 copy-done.8
  28.9 0.0 copy-start.9
  28.9 0.6 copy-done.9
  29.6 65.7 %panels.1 = (f32[256,512]{1,0:T(8,128)}, f32[256,1024]{1,0:T(8,128)}) custom-call(bf16[4,72,512]{2,1,0:T(8,128)(2,1)} %copy-done, bf16[4,72,512]{2,1,0:T(8,128)(2,1)} %copy-done.2, bf16[3,72,512]{2,1,0:T(8,128)(2,1)} %copy-done.1, bf16[3,72,512]{2,1,0:T(8,128)(2,1)} %copy-done.4, bf16[2,72,512]{2,1,0:T(8,128)(2,1)} %copy-done.3, ...), custom_call_target="tpu_custom_call" | custom-call | tf_op jit(solution)/shard_map/panels/pallas_call | solution.py:277
  95.2 2.4 %copy.6 = f32[256,1,512]{2,1,0:T(1,128)} copy(f32[256,1,512]{2,0,1:T(8,128)} %bitcast.27) | data formatting | bytes 1048576
  (8 shorter events, 0.1 us)
Async XLA Ops:
  0.6 0.7 copy-start.10
  2.2 8.0 %collective-permute-start = (bf16[1,72,512]{2,1,0:T(8,128)(2,1)S(1)}, bf16[1,72,512]{2,1,0:T(8,128)(2,1)S(1)}, u32[]{:S(2)}, u32[]{:S(2)}) collective-permute-start(bf16[1,72,512]{2,1,0:T(8,128)(2,1)S(1)} %fusion.2), channel_id=1, source_target_pairs={{0,16},{4,20},{8,24},{12,28},{16,0},{20,4},{24,8},{28,12},{1,17},{... | collective-permute-start | bytes 221192 | tf_op jit(solution)/shard_map/ppermute | solution.py:252
  10.2 5.2 %collective-permute-start.1 = (bf16[2,72,512]{2,1,0:T(8,128)(2,1)S(1)}, bf16[2,72,512]{2,1,0:T(8,128)(2,1)S(1)}, u32[]{:S(2)}, u32[]{:S(2)}) collective-permute-start(bf16[2,72,512]{2,1,0:T(8,128)(2,1)S(1)} %pad_maximum_fusion.2), channel_id=1, source_target_pairs={{0,8},{4,12},{8,0},{12,4},{16,24},{20,28},{24,16},{28,20},{1,9},{5... | collective-permute-start | bytes 442376 | tf_op jit(solution)/shard_map/ppermute | solution.py:252
  15.4 1.8 %copy-start = (bf16[4,72,512]{2,1,0:T(8,128)(2,1)}, bf16[4,72,512]{2,1,0:T(8,128)(2,1)S(1)}, u32[]{:S(2)}) copy-start(bf16[4,72,512]{2,1,0:T(8,128)(2,1)S(1)} %pad_maximum_fusion.refs_0_) | copy-start | bytes 884740
  15.4 6.8 %collective-permute-start.2 = (bf16[4,72,512]{2,1,0:T(8,128)(2,1)S(1)}, bf16[4,72,512]{2,1,0:T(8,128)(2,1)S(1)}, u32[]{:S(2)}, u32[]{:S(2)}) collective-permute-start(bf16[4,72,512]{2,1,0:T(8,128)(2,1)S(1)} %pad_maximum_fusion.refs_0_), channel_id=1, source_target_pairs={{0,4},{4,0},{8,12},{12,8},{16,20},{20,16},{24,28},{28,24},{1,5},{5... | collective-permute-start | bytes 884744 | tf_op jit(solution)/shard_map/ppermute | solution.py:252
  17.3 11.6 %copy-start.1 = (bf16[3,72,512]{2,1,0:T(8,128)(2,1)}, bf16[3,72,512]{2,1,0:T(8,128)(2,1)S(1)}, u32[]{:S(2)}) copy-start(bf16[3,72,512]{2,1,0:T(8,128)(2,1)S(1)} %pad_maximum_fusion.1.refs_2_) | copy-start | bytes 663556
  17.3 7.6 %collective-permute-start.3 = (bf16[3,72,512]{2,1,0:T(8,128)(2,1)S(1)}, bf16[3,72,512]{2,1,0:T(8,128)(2,1)S(1)}, u32[]{:S(2)}, u32[]{:S(2)}) collective-permute-start(bf16[3,72,512]{2,1,0:T(8,128)(2,1)S(1)} %pad_maximum_fusion.1.refs_2_), channel_id=1, source_target_pairs={{0,2},{1,3},{2,0},{3,1},{4,6},{5,7},{6,4},{7,5},{8,10},{9,11},{10,... | collective-permute-start | bytes 663560 | tf_op jit(solution)/shard_map/ppermute | solution.py:252
  22.2 6.6 %copy-start.2 = (bf16[4,72,512]{2,1,0:T(8,128)(2,1)}, bf16[4,72,512]{2,1,0:T(8,128)(2,1)S(1)}, u32[]{:S(2)}) copy-start(bf16[4,72,512]{2,1,0:T(8,128)(2,1)S(1)} %collective-permute-done.2.refs_1_) | copy-start | bytes 884740
  22.2 6.6 %copy-start.3 = (bf16[2,72,512]{2,1,0:T(8,128)(2,1)}, bf16[2,72,512]{2,1,0:T(8,128)(2,1)S(1)}, u32[]{:S(2)}) copy-start(bf16[2,72,512]{2,1,0:T(8,128)(2,1)S(1)} %dynamic-slice_bitcast_fusion.refs_4_) | copy-start | bytes 442372
  22.3 5.2 %collective-permute-start.4 = (bf16[2,72,512]{2,1,0:T(8,128)(2,1)S(1)}, bf16[2,72,512]{2,1,0:T(8,128)(2,1)S(1)}, u32[]{:S(2)}, u32[]{:S(2)}) collective-permute-start(bf16[2,72,512]{2,1,0:T(8,128)(2,1)S(1)} %dynamic-slice_bitcast_fusion.refs_4_), channel_id=1, source_target_pairs={{0,2},{1,3},{2,0},{3,1},{4,6},{5,7},{6,4},{7,5},{8,10},{9,11},{10,... | collective-permute-start | bytes 442376 | tf_op jit(solution)/shard_map/ppermute | solution.py:252
  24.1 3.4 %collective-permute-start.5 = (bf16[3,72,512]{2,1,0:T(8,128)(2,1)S(1)}, bf16[3,72,512]{2,1,0:T(8,128)(2,1)S(1)}, u32[]{:S(2)}, u32[]{:S(2)}) collective-permute-start(bf16[3,72,512]{2,1,0:T(8,128)(2,1)S(1)} %pad_maximum_fusion.1.refs_2_), channel_id=1, source_target_pairs={{0,1},{1,0},{2,3},{3,2},{4,5},{5,4},{6,7},{7,6},{8,9},{9,8},{10,11... | collective-permute-start | bytes 663560 | tf_op jit(solution)/shard_map/ppermute | solution.py:252
  24.9 4.0 %copy-start.4 = (bf16[3,72,512]{2,1,0:T(8,128)(2,1)}, bf16[3,72,512]{2,1,0:T(8,128)(2,1)S(1)}, u32[]{:S(2)}) copy-start(bf16[3,72,512]{2,1,0:T(8,128)(2,1)S(1)} %collective-permute-done.3.refs_3_) | copy-start | bytes 663556
  24.9 2.6 %collective-permute-start.6 = (bf16[3,72,512]{2,1,0:T(8,128)(2,1)S(1)}, bf16[3,72,512]{2,1,0:T(8,128)(2,1)S(1)}, u32[]{:S(2)}, u32[]{:S(2)}) collective-permute-start(bf16[3,72,512]{2,1,0:T(8,128)(2,1)S(1)} %collective-permute-done.3.refs_3_), channel_id=1, source_target_pairs={{0,1},{1,0},{2,3},{3,2},{4,5},{5,4},{6,7},{7,6},{8,9},{9,8},{10,11... | collective-permute-start | bytes 663560 | tf_op jit(solution)/shard_map/ppermute | solution.py:252
  24.9 2.7 %collective-permute-start.7 = (bf16[2,72,512]{2,1,0:T(8,128)(2,1)S(1)}, bf16[2,72,512]{2,1,0:T(8,128)(2,1)S(1)}, u32[]{:S(2)}, u32[]{:S(2)}) collective-permute-start(bf16[2,72,512]{2,1,0:T(8,128)(2,1)S(1)} %dynamic-slice_bitcast_fusion.refs_4_), channel_id=1, source_target_pairs={{0,1},{1,0},{2,3},{3,2},{4,5},{5,4},{6,7},{7,6},{8,9},{9,8},{10,11... | collective-permute-start | bytes 442376 | tf_op jit(solution)/shard_map/ppermute | solution.py:252
  27.5 1.4 %copy-start.7 = (bf16[2,72,512]{2,1,0:T(8,128)(2,1)}, bf16[2,72,512]{2,1,0:T(8,128)(2,1)S(1)}, u32[]{:S(2)}) copy-start(bf16[2,72,512]{2,1,0:T(8,128)(2,1)S(1)} %collective-permute-done.4.refs_5_) | copy-start | bytes 442372
  27.5 1.4 %collective-permute-start.8 = (bf16[2,72,512]{2,1,0:T(8,128)(2,1)S(1)}, bf16[2,72,512]{2,1,0:T(8,128)(2,1)S(1)}, u32[]{:S(2)}, u32[]{:S(2)}) collective-permute-start(bf16[2,72,512]{2,1,0:T(8,128)(2,1)S(1)} %collective-permute-done.4.refs_5_), channel_id=1, source_target_pairs={{0,1},{1,0},{2,3},{3,2},{4,5},{5,4},{6,7},{7,6},{8,9},{9,8},{10,11... | collective-permute-start | bytes 442376 | tf_op jit(solution)/shard_map/ppermute | solution.py:252
  27.5 1.4 %copy-start.5 = (bf16[3,72,512]{2,1,0:T(8,128)(2,1)}, bf16[3,72,512]{2,1,0:T(8,128)(2,1)S(1)}, u32[]{:S(2)}) copy-start(bf16[3,72,512]{2,1,0:T(8,128)(2,1)S(1)} %collective-permute-done.5.refs_6_) | copy-start | bytes 663556
  27.5 1.4 %copy-start.6 = (bf16[3,72,512]{2,1,0:T(8,128)(2,1)}, bf16[3,72,512]{2,1,0:T(8,128)(2,1)S(1)}, u32[]{:S(2)}) copy-start(bf16[3,72,512]{2,1,0:T(8,128)(2,1)S(1)} %collective-permute-done.6.refs_7_) | copy-start | bytes 663556
  27.5 1.4 %copy-start.8 = (bf16[2,72,512]{2,1,0:T(8,128)(2,1)}, bf16[2,72,512]{2,1,0:T(8,128)(2,1)S(1)}, u32[]{:S(2)}) copy-start(bf16[2,72,512]{2,1,0:T(8,128)(2,1)S(1)} %collective-permute-done.7.refs_8_) | copy-start | bytes 442372
  28.9 0.7 copy-start.9

commit v3 on v2

--- a/solution.py
+++ b/solution.py
@@ -20,14 +20,26 @@
     return 1.0 / (2.0 * length * length)
 
 
-def dot(a, b, ca, cb):
-    return lax.dot_general(
-        a,
-        b,
-        (((ca,), (cb,)), ((), ())),
-        precision=lax.Precision.HIGHEST,
-        preferred_element_type=jnp.float32,
-    )
+def terms_of(value):
+    high = value.astype(jnp.bfloat16)
+    rest = value - high.astype(jnp.float32)
+    middle = rest.astype(jnp.bfloat16)
+    low = (rest - middle.astype(jnp.float32)).astype(jnp.bfloat16)
+    return high, middle, low
+
+
+def left(value):
+    high, middle, low = terms_of(value)
+    return jnp.concatenate([low, high, middle, middle, high, high], axis=1)
+
+
+def right(value):
+    high, middle, low = terms_of(value)
+    return jnp.concatenate([high, low, middle, high, middle, high], axis=0)
+
+
+def product(a, b):
+    return jnp.dot(a, b, preferred_element_type=jnp.float32)
 
 
 def inverse_factor(block):
@@ -43,32 +55,60 @@
     def over_lanes(x, j):
         return jnp.broadcast_to(x[:, j : j + 1], shape)
 
+    per = count // 2
     result = []
     for s in range(count):
         base = SUBS * s
-        corner = [over_lanes(strips[s], base + j) for j in range(SUBS)]
+        raw = [over_lanes(strips[s], base + j) for j in range(SUBS)]
+        corner = list(raw)
         own = (lane >= base) & (lane < base + SUBS)
         rows = jnp.where(own, jnp.where(lane - base == sub, 1.0, 0.0), strips[s])
         scaled = rows
         pivots = rows
-        for k in range(SUBS):
-            pivot = over_subs(corner[k], k)
-            inverse = 1.0 / pivot
-            lead_row = over_subs(rows, k) * inverse
-            here = sub == k
-            scaled = jnp.where(here, lead_row, scaled)
-            pivots = jnp.where(here, pivot, pivots)
-            rows = jnp.where(here, lead_row, rows - corner[k] * lead_row)
-            for j in range(k + 1, SUBS):
-                entry = over_subs(corner[k], j) * inverse
-                corner[j] = jnp.where(here, entry, corner[j] - corner[k] * entry)
-        result.append(jnp.where(lane - base <= sub, scaled * jnp.sqrt(pivots), 0.0))
+        for k in range(0, SUBS, 2):
+            here, after = sub == k, sub == k + 1
+            a, b, c = over_subs(raw[k], k), over_subs(raw[k], k + 1), over_subs(raw[k + 1], k + 1)
+            det = a * c - b * b
+            inv_a, inv_det = 1.0 / a, 1.0 / det
+            ratio = b * inv_a
+            plain = corner[k + 1] - corner[k] * ratio
+            second = jnp.where(here, ratio, plain)
+            row = over_subs(rows, k) * inv_a
+            rows = jnp.where(here, row, rows - corner[k] * row)
+            row_2 = over_subs(rows, k + 1) * (a * inv_det)
+            rows = jnp.where(after, row_2, rows - second * row_2)
+            scaled = jnp.where(here, row, jnp.where(after, row_2, scaled))
+            pivots = jnp.where(here, a, jnp.where(after, det * inv_a, pivots))
+            for j in range(k + 2, SUBS):
+                entry = over_subs(raw[k], j) * inv_a
+                entry_2 = over_subs(plain, j) * a
+                first = jnp.where(here, entry, corner[j] - corner[k] * entry)
+                raw[j] = first - (second * entry_2) * inv_det
+                corner[j] = jnp.where(after, entry_2 * inv_det, raw[j])
+        result.append(scaled * jnp.sqrt(pivots))
         lead_rows = [over_subs(rows, k) for k in range(SUBS)]
-        for t in range(s + 1, count):
-            terms = [over_lanes(strips[t], base + k) * lead_rows[k] for k in range(SUBS)]
-            while len(terms) > 1:
-                terms = [a + b for a, b in zip(terms[::2], terms[1::2])]
-            strips[t] = jnp.where(own, 0.0, strips[t]) - terms[0]
+        end = (s // per + 1) * per
+        for t in range(s + 1, end):
+            parts = [over_lanes(strips[t], base + k) * lead_rows[k] for k in range(SUBS)]
+            while len(parts) > 1:
+                parts = [x + y for x, y in zip(parts[::2], parts[1::2])]
+            strips[t] = jnp.where(own, 0.0, strips[t]) - parts[0]
+        if s + 1 == end < count:
+            solved = jnp.concatenate(result, axis=0)
+            lanes = lax.broadcasted_iota(jnp.int32, solved.shape, 1)
+            subs = lax.broadcasted_iota(jnp.int32, solved.shape, 0)
+            clean = jnp.where((lanes < SUBS * end) & (lanes > subs), 0.0, solved)
+            change = lax.dot_general(
+                solved,
+                clean,
+                (((0,), (0,)), ((), ())),
+                precision=lax.Precision.HIGHEST,
+                preferred_element_type=jnp.float32,
+            )
+            for t in range(end, count):
+                keep = jnp.where(lane < SUBS * end, 0.0, strips[t])
+                strips[t] = keep - change[SUBS * t : SUBS * (t + 1), :]
+    result = [jnp.where(lane - SUBS * s <= sub, result[s], 0.0) for s in range(count)]
     return jnp.concatenate(result, axis=0)
 
 
@@ -91,7 +131,7 @@
     near, near_x = refs[:2]
     lists = [refs[2 + k * tops : 2 + (k + 1) * tops] for k in range(4)]
     side, side_x, core, core_x = lists
-    front, factor, feat, slot, noise, ray, mat, upper, inv = refs[2 + 4 * tops :]
+    front, factor, feat, slot, noise, ray, mat, upper, lowers = refs[2 + 4 * tops :]
     row_index, col_index = lax.axis_index("row"), lax.axis_index("col")
     rows = ray_dev * col_count
     pair_count = near.shape[0]
@@ -147,10 +187,20 @@
 
     panels, row_tiles = lead // PANEL, rows // PANEL
     col_tiles = (cols + PANEL - 1) // PANEL
-    wide = panels + col_tiles
 
     def tile(i):
-        return pl.ds(pl.multiple_of(i * PANEL, PANEL), PANEL)
+        start = i * PANEL
+        return pl.ds(start if isinstance(start, int) else pl.multiple_of(start, PANEL), PANEL)
+
+    def each(start, count, body):
+        if count <= 2:
+            for i in range(start, start + count):
+                body(i)
+        else:
+
+            @pl.loop(start, start + count)
+            def _(i):
+                body(i)
 
     def column(source, i):
         return jnp.concatenate([as_column(source[pl.ds(2 * i + k, 1), :]) for k in range(2)], axis=0)
@@ -158,67 +208,86 @@
     def line(source, i):
         return [source[pl.ds(2 * i + k, 1), :] for k in range(2)]
 
-    def spot(j):
-        return jnp.where(j < panels, j, j + row_tiles)
-
-    def tile_of(i, j, slot_a, ray_a):
+    def fill(i, j, slot_a, ray_a=None):
+        at = j if isinstance(j, int) and j < panels else j + row_tiles
         gram = lax.dot_general(
             feat[tile(i), :],
-            feat[tile(j), :],
+            feat[tile(at), :],
             (((1,), (1,)), ((), ())),
             preferred_element_type=jnp.float32,
         )
         halves = []
-        slots, noises, rays = line(slot, j), line(noise, j), line(ray, j)
-        for k in range(2):
-            gap = slot_a - slots[k]
+        for k, (slot_b, noise_b, ray_b) in enumerate(
+            zip(line(slot, at), line(noise, at), line(ray, at))
+        ):
+            gap = slot_a - slot_b
             part = gram[:, k * LANES : (k + 1) * LANES] * jnp.exp(-gap * gap * time_rate())
-            halves.append(part + jnp.where(ray_a == rays[k], noises[k], 0.0))
-        return jnp.concatenate(halves, axis=1)
-
-    @pl.loop(0, panels + row_tiles)
-    def _(i):
+            if ray_a is not None:
+                part = part + jnp.where(ray_a == ray_b, noise_b, 0.0)
+            halves.append(part)
+        mat[tile(i), tile(j)] = jnp.concatenate(halves, axis=1)
+
+    for i in range(panels):
+        slot_a = column(slot, i)
+        fill(i, i, slot_a, column(ray, i))
+        for j in range(i + 1, panels):
+            fill(i, j, slot_a)
+        each(panels, col_tiles, lambda j: fill(i, j, slot_a))
+
+    def fill_row(i):
         slot_a, ray_a = column(slot, i), column(ray, i)
-
-        @pl.loop(jnp.where(i < panels, i, 0), wide)
-        def _(j):
-            mat[tile(i), tile(j)] = tile_of(i, spot(j), slot_a, ray_a)
-
-    @pl.loop(0, panels)
-    def _(p):
-        at = pl.multiple_of(p * PANEL, PANEL)
-        mid = pl.multiple_of(at + HALF, HALF)
-        inv_a = inverse_factor(mat[pl.ds(at, HALF), pl.ds(at, HALF)])
-        cross = dot(inv_a, mat[pl.ds(at, HALF), pl.ds(mid, HALF)], 1, 0)
-        inv_b = inverse_factor(mat[pl.ds(mid, HALF), pl.ds(mid, HALF)] - dot(cross, cross, 0, 0))
-        inv[0:HALF, 0:HALF] = inv_a
-        inv[0:HALF, HALF:PANEL] = jnp.zeros((HALF, HALF), jnp.float32)
-        inv[HALF:PANEL, HALF:PANEL] = inv_b
-        inv[HALF:PANEL, 0:HALF] = -dot(inv_b, dot(cross, inv_a, 0, 0), 1, 0)
-
-        @pl.loop(p + 1, wide)
-        def _(j):
-            upper[:, tile(j)] = dot(inv[...], mat[tile(p), tile(j)], 1, 0)
-
-        @pl.loop(p + 1, panels)
-        def _(q):
-            @pl.loop(q, wide)
-            def _(j):
-                mat[tile(q), tile(j)] -= dot(upper[:, tile(q)], upper[:, tile(j)], 0, 0)
-
-        @pl.loop(0, row_tiles)
-        def _(i):
-            solved = dot(mat[tile(panels + i), tile(p)], inv[...], 1, 1)
+        for j in range(panels):
+            fill(i, j, slot_a, ray_a)
+        each(panels, col_tiles, lambda j: fill(i, j, slot_a, ray_a))
+
+    each(panels, row_tiles, fill_row)
+
+    for p in range(panels):
+        at = p * PANEL
+        mid = at + HALF
+        inv_a = inverse_factor(mat[at:mid, at:mid])
+        cross = product(left(inv_a), right(mat[at:mid, mid : mid + HALF]))
+        cross_left, cross_right = left(cross.T), right(cross)
+        corner = mat[mid : mid + HALF, mid : mid + HALF] - product(cross_left, cross_right)
+        inv_b = inverse_factor(corner)
+        below = product(left(-inv_b), right(product(cross_left, right(inv_a))))
+        zero = jnp.zeros((HALF, HALF), jnp.float32)
+        inv = jnp.concatenate(
+            [jnp.concatenate([inv_a, zero], axis=1), jnp.concatenate([below, inv_b], axis=1)], axis=0
+        )
+        inv_left, inv_right = left(inv), right(inv.T)
+
+        def solve(j):
+            found = product(inv_left, right(mat[tile(p), tile(j)]))
+            upper[:, tile(j)] = right(found)
+            return found
+
+        def update(i, j, lower):
+            mat[tile(i), tile(j)] -= product(lower, upper[:, tile(j)])
+
+        for j in range(p + 1, panels):
+            lowers[tile(j), :] = left(solve(j).T)
+            update(j, j, lowers[tile(j), :])
+        each(panels, col_tiles, solve)
+        for q in range(p + 1, panels):
+            for j in range(q + 1, panels):
+                update(q, j, lowers[tile(q), :])
+            each(panels, col_tiles, lambda j: update(q, j, lowers[tile(q), :]))
+
+        def solve_row(i):
+            found = product(left(mat[tile(panels + i), tile(p)]), inv_right)
             ray_a = column(ray, panels + i)
             kept = [
-                jnp.where(ray_a >= line_k, solved[:, k * LANES : (k + 1) * LANES], 0.0)
-                for k, line_k in enumerate(line(ray, p))
+                jnp.where(ray_a >= ray_b, found[:, k * LANES : (k + 1) * LANES], 0.0)
+                for k, ray_b in enumerate(line(ray, p))
             ]
             factor[tile(i), tile(p)] = jnp.concatenate(kept, axis=1)
-
-            @pl.loop(p + 1, wide)
-            def _(j):
-                mat[tile(panels + i), tile(j)] -= dot(solved, upper[:, tile(j)], 1, 0)
+            lower = left(found)
+            for j in range(p + 1, panels):
+                update(panels + i, j, lower)
+            each(panels, col_tiles, lambda j: update(panels + i, j, lower))
+
+        each(0, row_tiles, solve_row)
 
     skipped = front.shape[1] - cols
     front[:, 0:skipped] = jnp.zeros((rows, skipped), jnp.float32)
@@ -286,8 +355,8 @@
             pltpu.VMEM((rays, features.shape[1]), features.dtype),
             *[pltpu.VMEM((rays // LANES, LANES), jnp.float32)] * 3,
             pltpu.VMEM((lead + rows, lead + padded), jnp.float32),
-            pltpu.VMEM((PANEL, lead + padded), jnp.float32),
-            pltpu.VMEM((PANEL, PANEL), jnp.float32),
+            pltpu.VMEM((6 * PANEL, lead + padded), jnp.bfloat16),
+            pltpu.VMEM((lead, 6 * PANEL), jnp.bfloat16),
         ],
         name="panels",
     )(near, near_x, *side, *side_x, *core, *core_x)

time: 98.1 us -> 77.3 us (0.79)
  Pallas kernels: 65.7 us -> 44.8 us
    pallas_call x1, Pallas kernels: 65.7 us -> 44.8 us  [shards(): pl.pallas_call(functools.partial(kernel, ray_dev=ray_dev, row_count=row_c...]
where the time goes in v3:
time: 77.3 us; the launch traced here: 76.7 us
  Pallas kernels  44.8 us (58%)
  waiting for transfers between devices  16 us (21%)
  starting transfers between devices  10.5 us (14%)
  local copies, waits for them, and re-layouts  3.09 us (4%)
  other arithmetic  1.61 us (2%)
  between operations  0.81 us (1%)
    pallas_call x1, Pallas kernels, shards(): pl.pallas_call(functools.partial(kernel, ray_dev=ray_dev, row_count=row_c...  44.8 us
    ppermute x9, waiting for transfers between devices, other(): return lax.ppermute(value, axis, [(k, k ^ 1 << bit) for k in range(count)])  16 us
    ppermute x9, starting transfers between devices, other(): return lax.ppermute(value, axis, [(k, k ^ 1 << bit) for k in range(count)])  10.5 us
    unnamed x24, local copies, waits for them, and re-layouts  3.07 us
  transfers between devices with their start and end apart: 9, of which 6 were waited for; matrix products, arithmetic and copies ran while one was open for 0% of the time, Pallas kernels for 0%

profile of v3, /device:TPU:0, one launch (start us, length us, event | category | flops | bytes accessed | tf_op | source)
XLA Modules:
  0.0 76.7 jit_solution(16637711889212023432)
XLA Ops:
  0.6 0.0 copy-start.10
  0.6 0.7 convert_bitcast_fusion
  1.3 0.0 copy-done.10
  1.3 0.8 %fusion.2 = bf16[1,72,512]{2,1,0:T(8,128)(2,1)S(1)} fusion(bf16[1,512]{1,0:T(2,128)(2,1)S(1)} %bitcast.28, bf16[64,512]{1,0:T(8,128)(2,1)} %param.3), kind=kLoop, calls=%fused_computation.8 | loop fusion | flops 221184 | bytes 140288 | tf_op jit(solution)/shard_map/broadcast_in_dim | solution.py:323
  2.2 4.1 %collective-permute-start = (bf16[1,72,512]{2,1,0:T(8,128)(2,1)S(1)}, bf16[1,72,512]{2,1,0:T(8,128)(2,1)S(1)}, u32[]{:S(2)}, u32[]{:S(2)}) collective-permute-start(bf16[1,72,512]{2,1,0:T(8,128)(2,1)S(1)} %fusion.2), channel_id=1, source_target_pairs={{0,16},{4,20},{8,24},{12,28},{16,0},{20,4},{24,8},{28,12},{1,17},{... | collective-permute-start | bytes 221192 | tf_op jit(solution)/shard_map/ppermute | solution.py:321
  6.3 3.9 %collective-permute-done = bf16[1,72,512]{2,1,0:T(8,128)(2,1)S(1)} collective-permute-done((bf16[1,72,512]{2,1,0:T(8,128)(2,1)S(1)}, bf16[1,72,512]{2,1,0:T(8,128)(2,1)S(1)}, u32[]{:S(2)}, u32[]{:S(2)}) %collective-permute-start) | collective-permute-done | bytes 73760 | tf_op jit(solution)/shard_map/ppermute | solution.py:321
  10.2 0.7 collective-permute-start.1
  10.9 4.5 %collective-permute-done.1 = bf16[2,72,512]{2,1,0:T(8,128)(2,1)S(1)} collective-permute-done((bf16[2,72,512]{2,1,0:T(8,128)(2,1)S(1)}, bf16[2,72,512]{2,1,0:T(8,128)(2,1)S(1)}, u32[]{:S(2)}, u32[]{:S(2)}) %collective-permute-start.1) | collective-permute-done | bytes 147488 | tf_op jit(solution)/shard_map/ppermute | solution.py:321
  15.4 0.0 copy-start
  15.4 1.8 %collective-permute-start.2 = (bf16[4,72,512]{2,1,0:T(8,128)(2,1)S(1)}, bf16[4,72,512]{2,1,0:T(8,128)(2,1)S(1)}, u32[]{:S(2)}, u32[]{:S(2)}) collective-permute-start(bf16[4,72,512]{2,1,0:T(8,128)(2,1)S(1)} %pad_maximum_fusion.refs_0_), channel_id=1, source_target_pairs={{0,4},{4,0},{8,12},{12,8},{16,20},{20,16},{24,28},{28,24},{1,5},{5... | collective-permute-start | bytes 884744 | tf_op jit(solution)/shard_map/ppermute | solution.py:321
  17.3 0.0 copy-done
  17.3 0.0 copy-start.1
  17.3 1.6 %collective-permute-start.3 = (bf16[3,72,512]{2,1,0:T(8,128)(2,1)S(1)}, bf16[3,72,512]{2,1,0:T(8,128)(2,1)S(1)}, u32[]{:S(2)}, u32[]{:S(2)}) collective-permute-start(bf16[3,72,512]{2,1,0:T(8,128)(2,1)S(1)} %pad_maximum_fusion.1.refs_2_), channel_id=1, source_target_pairs={{0,2},{1,3},{2,0},{3,1},{4,6},{5,7},{6,4},{7,5},{8,10},{9,11},{10,... | collective-permute-start | bytes 663560 | tf_op jit(solution)/shard_map/ppermute | solution.py:321
  18.9 3.4 %collective-permute-done.2.refs_1_ = bf16[4,72,512]{2,1,0:T(8,128)(2,1)S(1)} collective-permute-done((bf16[4,72,512]{2,1,0:T(8,128)(2,1)S(1)}, bf16[4,72,512]{2,1,0:T(8,128)(2,1)S(1)}, u32[]{:S(2)}, u32[]{:S(2)}) %collective-permute-start.2) | collective-permute-done | bytes 294944 | tf_op jit(solution)/shard_map/ppermute | solution.py:321
  22.2 0.0 copy-start.2
  22.2 0.0 copy-start.3
  22.3 1.8 %collective-permute-start.4 = (bf16[2,72,512]{2,1,0:T(8,128)(2,1)S(1)}, bf16[2,72,512]{2,1,0:T(8,128)(2,1)S(1)}, u32[]{:S(2)}, u32[]{:S(2)}) collective-permute-start(bf16[2,72,512]{2,1,0:T(8,128)(2,1)S(1)} %dynamic-slice_bitcast_fusion.refs_4_), channel_id=1, source_target_pairs={{0,2},{1,3},{2,0},{3,1},{4,6},{5,7},{6,4},{7,5},{8,10},{9,11},{10,... | collective-permute-start | bytes 442376 | tf_op jit(solution)/shard_map/ppermute | solution.py:321
  24.1 0.0 collective-permute-start.5
  24.1 0.8 %collective-permute-done.3.refs_3_ = bf16[3,72,512]{2,1,0:T(8,128)(2,1)S(1)} collective-permute-done((bf16[3,72,512]{2,1,0:T(8,128)(2,1)S(1)}, bf16[3,72,512]{2,1,0:T(8,128)(2,1)S(1)}, u32[]{:S(2)}, u32[]{:S(2)}) %collective-permute-start.3) | collective-permute-done | bytes 221216 | tf_op jit(solution)/shard_map/ppermute | solution.py:321
  24.9 0.0 copy-start.4
  24.9 0.0 collective-permute-start.6
  24.9 0.5 collective-permute-start.7
  25.4 2.1 %collective-permute-done.4.refs_5_ = bf16[2,72,512]{2,1,0:T(8,128)(2,1)S(1)} collective-permute-done((bf16[2,72,512]{2,1,0:T(8,128)(2,1)S(1)}, bf16[2,72,512]{2,1,0:T(8,128)(2,1)S(1)}, u32[]{:S(2)}, u32[]{:S(2)}) %collective-permute-start.4) | collective-permute-done | bytes 147488 | tf_op jit(solution)/shard_map/ppermute | solution.py:321
  27.5 0.0 copy-start.7
  27.5 0.0 collective-permute-start.8
  27.5 0.0 collective-permute-done.5.refs_6_
  27.5 0.0 copy-start.5
  27.5 0.0 collective-permute-done.6.refs_7_
  27.5 0.0 copy-start.6
  27.5 0.0 collective-permute-done.7.refs_8_
  27.5 0.0 copy-start.8
  27.5 1.3 %collective-permute-done.8.refs_9_ = bf16[2,72,512]{2,1,0:T(8,128)(2,1)S(1)} collective-permute-done((bf16[2,72,512]{2,1,0:T(8,128)(2,1)S(1)}, bf16[2,72,512]{2,1,0:T(8,128)(2,1)S(1)}, u32[]{:S(2)}, u32[]{:S(2)}) %collective-permute-start.8) | collective-permute-done | bytes 147488 | tf_op jit(solution)/shard_map/ppermute | solution.py:321
  28.8 0.0 copy-done.1
  28.8 0.0 copy-done.2
  28.8 0.0 copy-done.3
  28.9 0.0 copy-done.4
  28.9 0.0 copy-done.7
  28.9 0.0 copy-done.5
  28.9 0.0 copy-done.6
  28.9 0.0 copy-done.8
  28.9 0.0 copy-start.9
  28.9 0.6 copy-done.9
  29.6 44.8 %panels.1 = (f32[256,512]{1,0:T(8,128)}, f32[256,1024]{1,0:T(8,128)}) custom-call(bf16[4,72,512]{2,1,0:T(8,128)(2,1)} %copy-done, bf16[4,72,512]{2,1,0:T(8,128)(2,1)} %copy-done.2, bf16[3,72,512]{2,1,0:T(8,128)(2,1)} %copy-done.1, bf16[3,72,512]{2,1,0:T(8,128)(2,1)} %copy-done.4, bf16[2,72,512]{2,1,0:T(8,128)(2,1)} %copy-done.3, ...), custom_call_target="tpu_custom_call" | custom-call | tf_op jit(solution)/shard_map/panels/pallas_call | solution.py:346
  74.3 2.4 %copy.6 = f32[256,1,512]{2,1,0:T(1,128)} copy(f32[256,1,512]{2,0,1:T(8,128)} %bitcast.27) | data formatting | bytes 1048576
  (8 shorter events, 0.1 us)
Async XLA Ops:
  0.6 0.7 copy-start.10
  2.2 8.0 %collective-permute-start = (bf16[1,72,512]{2,1,0:T(8,128)(2,1)S(1)}, bf16[1,72,512]{2,1,0:T(8,128)(2,1)S(1)}, u32[]{:S(2)}, u32[]{:S(2)}) collective-permute-start(bf16[1,72,512]{2,1,0:T(8,128)(2,1)S(1)} %fusion.2), channel_id=1, source_target_pairs={{0,16},{4,20},{8,24},{12,28},{16,0},{20,4},{24,8},{28,12},{1,17},{... | collective-permute-start | bytes 221192 | tf_op jit(solution)/shard_map/ppermute | solution.py:321
  10.2 5.2 %collective-permute-start.1 = (bf16[2,72,512]{2,1,0:T(8,128)(2,1)S(1)}, bf16[2,72,512]{2,1,0:T(8,128)(2,1)S(1)}, u32[]{:S(2)}, u32[]{:S(2)}) collective-permute-start(bf16[2,72,512]{2,1,0:T(8,128)(2,1)S(1)} %pad_maximum_fusion.2), channel_id=1, source_target_pairs={{0,8},{4,12},{8,0},{12,4},{16,24},{20,28},{24,16},{28,20},{1,9},{5... | collective-permute-start | bytes 442376 | tf_op jit(solution)/shard_map/ppermute | solution.py:321
  15.4 1.8 %copy-start = (bf16[4,72,512]{2,1,0:T(8,128)(2,1)}, bf16[4,72,512]{2,1,0:T(8,128)(2,1)S(1)}, u32[]{:S(2)}) copy-start(bf16[4,72,512]{2,1,0:T(8,128)(2,1)S(1)} %pad_maximum_fusion.refs_0_) | copy-start | bytes 884740
  15.4 6.8 %collective-permute-start.2 = (bf16[4,72,512]{2,1,0:T(8,128)(2,1)S(1)}, bf16[4,72,512]{2,1,0:T(8,128)(2,1)S(1)}, u32[]{:S(2)}, u32[]{:S(2)}) collective-permute-start(bf16[4,72,512]{2,1,0:T(8,128)(2,1)S(1)} %pad_maximum_fusion.refs_0_), channel_id=1, source_target_pairs={{0,4},{4,0},{8,12},{12,8},{16,20},{20,16},{24,28},{28,24},{1,5},{5... | collective-permute-start | bytes 884744 | tf_op jit(solution)/shard_map/ppermute | solution.py:321
  17.3 11.6 %copy-start.1 = (bf16[3,72,512]{2,1,0:T(8,128)(2,1)}, bf16[3,72,512]{2,1,0:T(8,128)(2,1)S(1)}, u32[]{:S(2)}) copy-start(bf16[3,72,512]{2,1,0:T(8,128)(2,1)S(1)} %pad_maximum_fusion.1.refs_2_) | copy-start | bytes 663556
  17.3 7.6 %collective-permute-start.3 = (bf16[3,72,512]{2,1,0:T(8,128)(2,1)S(1)}, bf16[3,72,512]{2,1,0:T(8,128)(2,1)S(1)}, u32[]{:S(2)}, u32[]{:S(2)}) collective-permute-start(bf16[3,72,512]{2,1,0:T(8,128)(2,1)S(1)} %pad_maximum_fusion.1.refs_2_), channel_id=1, source_target_pairs={{0,2},{1,3},{2,0},{3,1},{4,6},{5,7},{6,4},{7,5},{8,10},{9,11},{10,... | collective-permute-start | bytes 663560 | tf_op jit(solution)/shard_map/ppermute | solution.py:321
  22.2 6.6 %copy-start.2 = (bf16[4,72,512]{2,1,0:T(8,128)(2,1)}, bf16[4,72,512]{2,1,0:T(8,128)(2,1)S(1)}, u32[]{:S(2)}) copy-start(bf16[4,72,512]{2,1,0:T(8,128)(2,1)S(1)} %collective-permute-done.2.refs_1_) | copy-start | bytes 884740
  22.2 6.6 %copy-start.3 = (bf16[2,72,512]{2,1,0:T(8,128)(2,1)}, bf16[2,72,512]{2,1,0:T(8,128)(2,1)S(1)}, u32[]{:S(2)}) copy-start(bf16[2,72,512]{2,1,0:T(8,128)(2,1)S(1)} %dynamic-slice_bitcast_fusion.refs_4_) | copy-start | bytes 442372
  22.3 5.2 %collective-permute-start.4 = (bf16[2,72,512]{2,1,0:T(8,128)(2,1)S(1)}, bf16[2,72,512]{2,1,0:T(8,128)(2,1)S(1)}, u32[]{:S(2)}, u32[]{:S(2)}) collective-permute-start(bf16[2,72,512]{2,1,0:T(8,128)(2,1)S(1)} %dynamic-slice_bitcast_fusion.refs_4_), channel_id=1, source_target_pairs={{0,2},{1,3},{2,0},{3,1},{4,6},{5,7},{6,4},{7,5},{8,10},{9,11},{10,... | collective-permute-start | bytes 442376 | tf_op jit(solution)/shard_map/ppermute | solution.py:321
  24.1 3.4 %collective-permute-start.5 = (bf16[3,72,512]{2,1,0:T(8,128)(2,1)S(1)}, bf16[3,72,512]{2,1,0:T(8,128)(2,1)S(1)}, u32[]{:S(2)}, u32[]{:S(2)}) collective-permute-start(bf16[3,72,512]{2,1,0:T(8,128)(2,1)S(1)} %pad_maximum_fusion.1.refs_2_), channel_id=1, source_target_pairs={{0,1},{1,0},{2,3},{3,2},{4,5},{5,4},{6,7},{7,6},{8,9},{9,8},{10,11... | collective-permute-start | bytes 663560 | tf_op jit(solution)/shard_map/ppermute | solution.py:321
  24.9 4.0 %copy-start.4 = (bf16[3,72,512]{2,1,0:T(8,128)(2,1)}, bf16[3,72,512]{2,1,0:T(8,128)(2,1)S(1)}, u32[]{:S(2)}) copy-start(bf16[3,72,512]{2,1,0:T(8,128)(2,1)S(1)} %collective-permute-done.3.refs_3_) | copy-start | bytes 663556
  24.9 2.6 %collective-permute-start.6 = (bf16[3,72,512]{2,1,0:T(8,128)(2,1)S(1)}, bf16[3,72,512]{2,1,0:T(8,128)(2,1)S(1)}, u32[]{:S(2)}, u32[]{:S(2)}) collective-permute-start(bf16[3,72,512]{2,1,0:T(8,128)(2,1)S(1)} %collective-permute-done.3.refs_3_), channel_id=1, source_target_pairs={{0,1},{1,0},{2,3},{3,2},{4,5},{5,4},{6,7},{7,6},{8,9},{9,8},{10,11... | collective-permute-start | bytes 663560 | tf_op jit(solution)/shard_map/ppermute | solution.py:321
  24.9 2.7 %collective-permute-start.7 = (bf16[2,72,512]{2,1,0:T(8,128)(2,1)S(1)}, bf16[2,72,512]{2,1,0:T(8,128)(2,1)S(1)}, u32[]{:S(2)}, u32[]{:S(2)}) collective-permute-start(bf16[2,72,512]{2,1,0:T(8,128)(2,1)S(1)} %dynamic-slice_bitcast_fusion.refs_4_), channel_id=1, source_target_pairs={{0,1},{1,0},{2,3},{3,2},{4,5},{5,4},{6,7},{7,6},{8,9},{9,8},{10,11... | collective-permute-start | bytes 442376 | tf_op jit(solution)/shard_map/ppermute | solution.py:321
  27.5 1.4 %copy-start.7 = (bf16[2,72,512]{2,1,0:T(8,128)(2,1)}, bf16[2,72,512]{2,1,0:T(8,128)(2,1)S(1)}, u32[]{:S(2)}) copy-start(bf16[2,72,512]{2,1,0:T(8,128)(2,1)S(1)} %collective-permute-done.4.refs_5_) | copy-start | bytes 442372
  27.5 1.4 %collective-permute-start.8 = (bf16[2,72,512]{2,1,0:T(8,128)(2,1)S(1)}, bf16[2,72,512]{2,1,0:T(8,128)(2,1)S(1)}, u32[]{:S(2)}, u32[]{:S(2)}) collective-permute-start(bf16[2,72,512]{2,1,0:T(8,128)(2,1)S(1)} %collective-permute-done.4.refs_5_), channel_id=1, source_target_pairs={{0,1},{1,0},{2,3},{3,2},{4,5},{5,4},{6,7},{7,6},{8,9},{9,8},{10,11... | collective-permute-start | bytes 442376 | tf_op jit(solution)/shard_map/ppermute | solution.py:321
  27.5 1.4 %copy-start.5 = (bf16[3,72,512]{2,1,0:T(8,128)(2,1)}, bf16[3,72,512]{2,1,0:T(8,128)(2,1)S(1)}, u32[]{:S(2)}) copy-start(bf16[3,72,512]{2,1,0:T(8,128)(2,1)S(1)} %collective-permute-done.5.refs_6_) | copy-start | bytes 663556
  27.5 1.4 %copy-start.6 = (bf16[3,72,512]{2,1,0:T(8,128)(2,1)}, bf16[3,72,512]{2,1,0:T(8,128)(2,1)S(1)}, u32[]{:S(2)}) copy-start(bf16[3,72,512]{2,1,0:T(8,128)(2,1)S(1)} %collective-permute-done.6.refs_7_) | copy-start | bytes 663556
  27.5 1.4 %copy-start.8 = (bf16[2,72,512]{2,1,0:T(8,128)(2,1)}, bf16[2,72,512]{2,1,0:T(8,128)(2,1)S(1)}, u32[]{:S(2)}) copy-start(bf16[2,72,512]{2,1,0:T(8,128)(2,1)S(1)} %collective-permute-done.7.refs_8_) | copy-start | bytes 442372
  28.9 0.7 copy-start.9

commit v4 on v3

--- a/solution.py
+++ b/solution.py
@@ -44,6 +44,7 @@
 
 def inverse_factor(block):
     count = block.shape[0] // SUBS
+    per, ahead = count // 2, SUBS // 2
     strips = [block[SUBS * t : SUBS * (t + 1), :] for t in range(count)]
     shape = (SUBS, LANES)
     lane = lax.broadcasted_iota(jnp.int32, shape, 1)
@@ -55,16 +56,23 @@
     def over_lanes(x, j):
         return jnp.broadcast_to(x[:, j : j + 1], shape)
 
-    per = count // 2
     result = []
+    early = []
     for s in range(count):
         base = SUBS * s
-        raw = [over_lanes(strips[s], base + j) for j in range(SUBS)]
+        end = (s // per + 1) * per
+        raw = early + [over_lanes(strips[s], base + j) for j in range(len(early), SUBS)]
         corner = list(raw)
         own = (lane >= base) & (lane < base + SUBS)
         rows = jnp.where(own, jnp.where(lane - base == sub, 1.0, 0.0), strips[s])
         scaled = rows
         pivots = rows
+        near = s + 1 < end
+        early = []
+        if near:
+            cols = [over_lanes(strips[s + 1], base + k) for k in range(SUBS)]
+            early = [over_lanes(strips[s + 1], base + SUBS + j) for j in range(ahead)]
+            following = jnp.where(own, 0.0, strips[s + 1])
         for k in range(0, SUBS, 2):
             here, after = sub == k, sub == k + 1
             a, b, c = over_subs(raw[k], k), over_subs(raw[k], k + 1), over_subs(raw[k + 1], k + 1)
@@ -75,20 +83,33 @@
             second = jnp.where(here, ratio, plain)
             row = over_subs(rows, k) * inv_a
             rows = jnp.where(here, row, rows - corner[k] * row)
-            row_2 = over_subs(rows, k + 1) * (a * inv_det)
+            row_2 = (over_subs(rows, k + 1) * a) * inv_det
             rows = jnp.where(after, row_2, rows - second * row_2)
             scaled = jnp.where(here, row, jnp.where(after, row_2, scaled))
             pivots = jnp.where(here, a, jnp.where(after, det * inv_a, pivots))
+            entries = []
             for j in range(k + 2, SUBS):
                 entry = over_subs(raw[k], j) * inv_a
                 entry_2 = over_subs(plain, j) * a
+                entries.append((entry, entry_2))
                 first = jnp.where(here, entry, corner[j] - corner[k] * entry)
                 raw[j] = first - (second * entry_2) * inv_det
                 corner[j] = jnp.where(after, entry_2 * inv_det, raw[j])
+            if near:
+                col = cols[k]
+                col_2 = cols[k + 1] - col * ratio
+                for j, (entry, entry_2) in zip(range(k + 2, SUBS), entries):
+                    cols[j] = (cols[j] - col * entry) - (col_2 * entry_2) * inv_det
+                following = (following - col * row) - col_2 * row_2
+                for j in range(ahead):
+                    part = early[j] - col * (over_subs(col, j) * inv_a)
+                    early[j] = part - (col_2 * (over_subs(col_2, j) * a)) * inv_det
         result.append(scaled * jnp.sqrt(pivots))
-        lead_rows = [over_subs(rows, k) for k in range(SUBS)]
-        end = (s // per + 1) * per
-        for t in range(s + 1, end):
+        if near:
+            strips[s + 1] = following
+        if s + 2 < end:
+            lead_rows = [over_subs(rows, k) for k in range(SUBS)]
+        for t in range(s + 2, end):
             parts = [over_lanes(strips[t], base + k) * lead_rows[k] for k in range(SUBS)]
             while len(parts) > 1:
                 parts = [x + y for x, y in zip(parts[::2], parts[1::2])]
@@ -242,52 +263,73 @@
 
     each(panels, row_tiles, fill_row)
 
+    half = 6 * HALF
+
     for p in range(panels):
-        at = p * PANEL
-        mid = at + HALF
-        inv_a = inverse_factor(mat[at:mid, at:mid])
-        cross = product(left(inv_a), right(mat[at:mid, mid : mid + HALF]))
+        top, low = pl.ds(p * PANEL, HALF), pl.ds(p * PANEL + HALF, HALF)
+        inv_a = inverse_factor(mat[top, top])
+        left_a = left(inv_a)
+        cross = product(left_a, right(mat[top, low]))
         cross_left, cross_right = left(cross.T), right(cross)
-        corner = mat[mid : mid + HALF, mid : mid + HALF] - product(cross_left, cross_right)
+        corner = mat[low, low] - product(cross_left, cross_right)
+
+        def solve_top(j):
+            found = product(left_a, right(mat[top, tile(j)]))
+            terms = right(found)
+            upper[0:half, tile(j)] = terms
+            mat[low, tile(j)] -= product(cross_left, terms)
+            return found
+
+        def solve_low(j):
+            found = product(left_b, right(mat[low, tile(j)]))
+            upper[half:, tile(j)] = right(found)
+            return found
+
+        for j in range(p + 1, panels):
+            lowers[tile(j), 0:half] = left(solve_top(j).T)
+        if p + 1 < panels:
+            mat[tile(p + 1), tile(p + 1)] -= product(
+                lowers[tile(p + 1), 0:half], upper[0:half, tile(p + 1)]
+            )
         inv_b = inverse_factor(corner)
-        below = product(left(-inv_b), right(product(cross_left, right(inv_a))))
-        zero = jnp.zeros((HALF, HALF), jnp.float32)
-        inv = jnp.concatenate(
-            [jnp.concatenate([inv_a, zero], axis=1), jnp.concatenate([below, inv_b], axis=1)], axis=0
-        )
-        inv_left, inv_right = left(inv), right(inv.T)
+        left_b = left(inv_b)
+        for j in range(p + 1, panels):
+            lowers[tile(j), half:] = left(solve_low(j).T)
+            if j == p + 1:
+                mat[tile(j), tile(j)] -= product(lowers[tile(j), half:], upper[half:, tile(j)])
 
         def solve(j):
-            found = product(inv_left, right(mat[tile(p), tile(j)]))
-            upper[:, tile(j)] = right(found)
-            return found
-
-        def update(i, j, lower):
-            mat[tile(i), tile(j)] -= product(lower, upper[:, tile(j)])
-
-        for j in range(p + 1, panels):
-            lowers[tile(j), :] = left(solve(j).T)
-            update(j, j, lowers[tile(j), :])
+            solve_top(j)
+            solve_low(j)
+
         each(panels, col_tiles, solve)
-        for q in range(p + 1, panels):
-            for j in range(q + 1, panels):
-                update(q, j, lowers[tile(q), :])
-            each(panels, col_tiles, lambda j: update(q, j, lowers[tile(q), :]))
+        right_a, right_b = right(inv_a.T), right(inv_b.T)
 
         def solve_row(i):
-            found = product(left(mat[tile(panels + i), tile(p)]), inv_right)
+            row = tile(panels + i)
+            first = product(left(mat[row, top]), right_a)
+            first_left = left(first)
+            second = product(left(mat[row, low] - product(first_left, cross_right)), right_b)
             ray_a = column(ray, panels + i)
             kept = [
-                jnp.where(ray_a >= ray_b, found[:, k * LANES : (k + 1) * LANES], 0.0)
-                for k, ray_b in enumerate(line(ray, p))
+                jnp.where(ray_a >= ray_b, part, 0.0)
+                for part, ray_b in zip((first, second), line(ray, p))
             ]
             factor[tile(i), tile(p)] = jnp.concatenate(kept, axis=1)
-            lower = left(found)
-            for j in range(p + 1, panels):
-                update(panels + i, j, lower)
-            each(panels, col_tiles, lambda j: update(panels + i, j, lower))
+            lowers[row, 0:half] = first_left
+            lowers[row, half:] = left(second)
 
         each(0, row_tiles, solve_row)
+
+        def update(start, count, j):
+            some = pl.ds(start * PANEL, count * PANEL)
+            mat[some, tile(j)] -= product(lowers[some, :], upper[:, tile(j)])
+
+        for j in range(p + 1, panels):
+            if j > p + 1:
+                update(p + 1, j - p, j)
+            update(panels, row_tiles, j)
+        each(panels, col_tiles, lambda j: update(p + 1, panels + row_tiles - p - 1, j))
 
     skipped = front.shape[1] - cols
     front[:, 0:skipped] = jnp.zeros((rows, skipped), jnp.float32)
@@ -356,7 +398,7 @@
             *[pltpu.VMEM((rays // LANES, LANES), jnp.float32)] * 3,
             pltpu.VMEM((lead + rows, lead + padded), jnp.float32),
             pltpu.VMEM((6 * PANEL, lead + padded), jnp.bfloat16),
-            pltpu.VMEM((lead, 6 * PANEL), jnp.bfloat16),
+            pltpu.VMEM((lead + rows, 6 * PANEL), jnp.bfloat16),
         ],
         name="panels",
     )(near, near_x, *side, *side_x, *core, *core_x)

time: 77.3 us -> 64.3 us (0.83)
  Pallas kernels: 44.8 us -> 31.8 us
    pallas_call x1, Pallas kernels: 44.8 us -> 31.8 us  [shards(): pl.pallas_call(functools.partial(kernel, ray_dev=ray_dev, row_count=row_c...]
where the time goes in v4:
time: 64.3 us; the launch traced here: 63.8 us
  Pallas kernels  31.8 us (49%)
  waiting for transfers between devices  16 us (25%)
  starting transfers between devices  10.5 us (16%)
  local copies, waits for them, and re-layouts  3.09 us (5%)
  other arithmetic  1.61 us (3%)
  between operations  0.81 us (1%)
    pallas_call x1, Pallas kernels, shards(): pl.pallas_call(functools.partial(kernel, ray_dev=ray_dev, row_count=row_c...  31.8 us
    ppermute x9, waiting for transfers between devices, other(): return lax.ppermute(value, axis, [(k, k ^ 1 << bit) for k in range(count)])  16 us
    ppermute x9, starting transfers between devices, other(): return lax.ppermute(value, axis, [(k, k ^ 1 << bit) for k in range(count)])  10.5 us
    unnamed x24, local copies, waits for them, and re-layouts  3.07 us
  transfers between devices with their start and end apart: 9, of which 6 were waited for; matrix products, arithmetic and copies ran while one was open for 0% of the time, Pallas kernels for 0%

profile of v4, /device:TPU:0, one launch (start us, length us, event | category | flops | bytes accessed | tf_op | source)
XLA Modules:
  0.0 63.8 jit_solution(15347557760593045859)
XLA Ops:
  0.6 0.0 copy-start.10
  0.6 0.7 %convert_bitcast_fusion = bf16[1,64]{1,0:T(2,128)(2,1)S(1)} fusion(s32[64]{0:T(128)} %param.4), kind=kLoop, calls=%fused_computation.27 | loop fusion | flops 128 | bytes 384 | tf_op jit(solution)/shard_map/stack | solution.py:344
  1.3 0.0 copy-done.10
  1.3 0.8 %fusion.2 = bf16[1,72,512]{2,1,0:T(8,128)(2,1)S(1)} fusion(bf16[1,512]{1,0:T(2,128)(2,1)S(1)} %bitcast.28, bf16[64,512]{1,0:T(8,128)(2,1)} %param.3), kind=kLoop, calls=%fused_computation.8 | loop fusion | flops 221184 | bytes 140288 | tf_op jit(solution)/shard_map/broadcast_in_dim | solution.py:365
  2.2 4.1 %collective-permute-start = (bf16[1,72,512]{2,1,0:T(8,128)(2,1)S(1)}, bf16[1,72,512]{2,1,0:T(8,128)(2,1)S(1)}, u32[]{:S(2)}, u32[]{:S(2)}) collective-permute-start(bf16[1,72,512]{2,1,0:T(8,128)(2,1)S(1)} %fusion.2), channel_id=1, source_target_pairs={{0,16},{4,20},{8,24},{12,28},{16,0},{20,4},{24,8},{28,12},{1,17},{... | collective-permute-start | bytes 221192 | tf_op jit(solution)/shard_map/ppermute | solution.py:363
  6.3 3.9 %collective-permute-done = bf16[1,72,512]{2,1,0:T(8,128)(2,1)S(1)} collective-permute-done((bf16[1,72,512]{2,1,0:T(8,128)(2,1)S(1)}, bf16[1,72,512]{2,1,0:T(8,128)(2,1)S(1)}, u32[]{:S(2)}, u32[]{:S(2)}) %collective-permute-start) | collective-permute-done | bytes 73760 | tf_op jit(solution)/shard_map/ppermute | solution.py:363
  10.2 0.7 %collective-permute-start.1 = (bf16[2,72,512]{2,1,0:T(8,128)(2,1)S(1)}, bf16[2,72,512]{2,1,0:T(8,128)(2,1)S(1)}, u32[]{:S(2)}, u32[]{:S(2)}) collective-permute-start(bf16[2,72,512]{2,1,0:T(8,128)(2,1)S(1)} %pad_maximum_fusion.2), channel_id=1, source_target_pairs={{0,8},{4,12},{8,0},{12,4},{16,24},{20,28},{24,16},{28,20},{1,9},{5... | collective-permute-start | bytes 442376 | tf_op jit(solution)/shard_map/ppermute | solution.py:363
  10.9 4.5 %collective-permute-done.1 = bf16[2,72,512]{2,1,0:T(8,128)(2,1)S(1)} collective-permute-done((bf16[2,72,512]{2,1,0:T(8,128)(2,1)S(1)}, bf16[2,72,512]{2,1,0:T(8,128)(2,1)S(1)}, u32[]{:S(2)}, u32[]{:S(2)}) %collective-permute-start.1) | collective-permute-done | bytes 147488 | tf_op jit(solution)/shard_map/ppermute | solution.py:363
  15.4 0.0 copy-start
  15.4 1.8 %collective-permute-start.2 = (bf16[4,72,512]{2,1,0:T(8,128)(2,1)S(1)}, bf16[4,72,512]{2,1,0:T(8,128)(2,1)S(1)}, u32[]{:S(2)}, u32[]{:S(2)}) collective-permute-start(bf16[4,72,512]{2,1,0:T(8,128)(2,1)S(1)} %pad_maximum_fusion.refs_0_), channel_id=1, source_target_pairs={{0,4},{4,0},{8,12},{12,8},{16,20},{20,16},{24,28},{28,24},{1,5},{5... | collective-permute-start | bytes 884744 | tf_op jit(solution)/shard_map/ppermute | solution.py:363
  17.3 0.0 copy-done
  17.3 0.0 copy-start.1
  17.3 1.6 %collective-permute-start.3 = (bf16[3,72,512]{2,1,0:T(8,128)(2,1)S(1)}, bf16[3,72,512]{2,1,0:T(8,128)(2,1)S(1)}, u32[]{:S(2)}, u32[]{:S(2)}) collective-permute-start(bf16[3,72,512]{2,1,0:T(8,128)(2,1)S(1)} %pad_maximum_fusion.1.refs_2_), channel_id=1, source_target_pairs={{0,2},{1,3},{2,0},{3,1},{4,6},{5,7},{6,4},{7,5},{8,10},{9,11},{10,... | collective-permute-start | bytes 663560 | tf_op jit(solution)/shard_map/ppermute | solution.py:363
  18.9 3.4 %collective-permute-done.2.refs_1_ = bf16[4,72,512]{2,1,0:T(8,128)(2,1)S(1)} collective-permute-done((bf16[4,72,512]{2,1,0:T(8,128)(2,1)S(1)}, bf16[4,72,512]{2,1,0:T(8,128)(2,1)S(1)}, u32[]{:S(2)}, u32[]{:S(2)}) %collective-permute-start.2) | collective-permute-done | bytes 294944 | tf_op jit(solution)/shard_map/ppermute | solution.py:363
  22.2 0.0 copy-start.2
  22.2 0.0 copy-start.3
  22.3 1.8 %collective-permute-start.4 = (bf16[2,72,512]{2,1,0:T(8,128)(2,1)S(1)}, bf16[2,72,512]{2,1,0:T(8,128)(2,1)S(1)}, u32[]{:S(2)}, u32[]{:S(2)}) collective-permute-start(bf16[2,72,512]{2,1,0:T(8,128)(2,1)S(1)} %dynamic-slice_bitcast_fusion.refs_4_), channel_id=1, source_target_pairs={{0,2},{1,3},{2,0},{3,1},{4,6},{5,7},{6,4},{7,5},{8,10},{9,11},{10,... | collective-permute-start | bytes 442376 | tf_op jit(solution)/shard_map/ppermute | solution.py:363
  24.1 0.0 collective-permute-start.5
  24.1 0.8 %collective-permute-done.3.refs_3_ = bf16[3,72,512]{2,1,0:T(8,128)(2,1)S(1)} collective-permute-done((bf16[3,72,512]{2,1,0:T(8,128)(2,1)S(1)}, bf16[3,72,512]{2,1,0:T(8,128)(2,1)S(1)}, u32[]{:S(2)}, u32[]{:S(2)}) %collective-permute-start.3) | collective-permute-done | bytes 221216 | tf_op jit(solution)/shard_map/ppermute | solution.py:363
  24.9 0.0 copy-start.4
  24.9 0.0 collective-permute-start.6
  24.9 0.5 collective-permute-start.7
  25.4 2.1 %collective-permute-done.4.refs_5_ = bf16[2,72,512]{2,1,0:T(8,128)(2,1)S(1)} collective-permute-done((bf16[2,72,512]{2,1,0:T(8,128)(2,1)S(1)}, bf16[2,72,512]{2,1,0:T(8,128)(2,1)S(1)}, u32[]{:S(2)}, u32[]{:S(2)}) %collective-permute-start.4) | collective-permute-done | bytes 147488 | tf_op jit(solution)/shard_map/ppermute | solution.py:363
  27.5 0.0 copy-start.7
  27.5 0.0 collective-permute-start.8
  27.5 0.0 collective-permute-done.5.refs_6_
  27.5 0.0 copy-start.5
  27.5 0.0 collective-permute-done.6.refs_7_
  27.5 0.0 copy-start.6
  27.5 0.0 collective-permute-done.7.refs_8_
  27.5 0.0 copy-start.8
  27.5 1.3 %collective-permute-done.8.refs_9_ = bf16[2,72,512]{2,1,0:T(8,128)(2,1)S(1)} collective-permute-done((bf16[2,72,512]{2,1,0:T(8,128)(2,1)S(1)}, bf16[2,72,512]{2,1,0:T(8,128)(2,1)S(1)}, u32[]{:S(2)}, u32[]{:S(2)}) %collective-permute-start.8) | collective-permute-done | bytes 147488 | tf_op jit(solution)/shard_map/ppermute | solution.py:363
  28.8 0.0 copy-done.1
  28.8 0.0 copy-done.2
  28.8 0.0 copy-done.3
  28.9 0.0 copy-done.4
  28.9 0.0 copy-done.7
  28.9 0.0 copy-done.5
  28.9 0.0 copy-done.6
  28.9 0.0 copy-done.8
  28.9 0.0 copy-start.9
  28.9 0.6 %copy-done.9 = bf16[2,72,512]{2,1,0:T(8,128)(2,1)} copy-done((bf16[2,72,512]{2,1,0:T(8,128)(2,1)}, bf16[2,72,512]{2,1,0:T(8,128)(2,1)S(1)}, u32[]{:S(2)}) %copy-start.9) | copy-done | bytes 147480
  29.6 31.8 %panels.1 = (f32[256,512]{1,0:T(8,128)}, f32[256,1024]{1,0:T(8,128)}) custom-call(bf16[4,72,512]{2,1,0:T(8,128)(2,1)} %copy-done, bf16[4,72,512]{2,1,0:T(8,128)(2,1)} %copy-done.2, bf16[3,72,512]{2,1,0:T(8,128)(2,1)} %copy-done.1, bf16[3,72,512]{2,1,0:T(8,128)(2,1)} %copy-done.4, bf16[2,72,512]{2,1,0:T(8,128)(2,1)} %copy-done.3, ...), custom_call_target="tpu_custom_call" | custom-call | tf_op jit(solution)/shard_map/panels/pallas_call | solution.py:388
  61.4 2.4 %copy.6 = f32[256,1,512]{2,1,0:T(1,128)} copy(f32[256,1,512]{2,0,1:T(8,128)} %bitcast.27) | data formatting | bytes 1048576
  (8 shorter events, 0.1 us)
Async XLA Ops:
  0.6 0.7 %copy-start.10 = (f32[64]{0:T(128)S(1)}, f32[64]{0:T(128)}, u32[]{:S(2)}) copy-start(f32[64]{0:T(128)} %param.5) | copy-start | bytes 772
  2.2 8.0 %collective-permute-start = (bf16[1,72,512]{2,1,0:T(8,128)(2,1)S(1)}, bf16[1,72,512]{2,1,0:T(8,128)(2,1)S(1)}, u32[]{:S(2)}, u32[]{:S(2)}) collective-permute-start(bf16[1,72,512]{2,1,0:T(8,128)(2,1)S(1)} %fusion.2), channel_id=1, source_target_pairs={{0,16},{4,20},{8,24},{12,28},{16,0},{20,4},{24,8},{28,12},{1,17},{... | collective-permute-start | bytes 221192 | tf_op jit(solution)/shard_map/ppermute | solution.py:363
  10.2 5.2 %collective-permute-start.1 = (bf16[2,72,512]{2,1,0:T(8,128)(2,1)S(1)}, bf16[2,72,512]{2,1,0:T(8,128)(2,1)S(1)}, u32[]{:S(2)}, u32[]{:S(2)}) collective-permute-start(bf16[2,72,512]{2,1,0:T(8,128)(2,1)S(1)} %pad_maximum_fusion.2), channel_id=1, source_target_pairs={{0,8},{4,12},{8,0},{12,4},{16,24},{20,28},{24,16},{28,20},{1,9},{5... | collective-permute-start | bytes 442376 | tf_op jit(solution)/shard_map/ppermute | solution.py:363
  15.4 1.8 %copy-start = (bf16[4,72,512]{2,1,0:T(8,128)(2,1)}, bf16[4,72,512]{2,1,0:T(8,128)(2,1)S(1)}, u32[]{:S(2)}) copy-start(bf16[4,72,512]{2,1,0:T(8,128)(2,1)S(1)} %pad_maximum_fusion.refs_0_) | copy-start | bytes 884740
  15.4 6.8 %collective-permute-start.2 = (bf16[4,72,512]{2,1,0:T(8,128)(2,1)S(1)}, bf16[4,72,512]{2,1,0:T(8,128)(2,1)S(1)}, u32[]{:S(2)}, u32[]{:S(2)}) collective-permute-start(bf16[4,72,512]{2,1,0:T(8,128)(2,1)S(1)} %pad_maximum_fusion.refs_0_), channel_id=1, source_target_pairs={{0,4},{4,0},{8,12},{12,8},{16,20},{20,16},{24,28},{28,24},{1,5},{5... | collective-permute-start | bytes 884744 | tf_op jit(solution)/shard_map/ppermute | solution.py:363
  17.3 11.6 %copy-start.1 = (bf16[3,72,512]{2,1,0:T(8,128)(2,1)}, bf16[3,72,512]{2,1,0:T(8,128)(2,1)S(1)}, u32[]{:S(2)}) copy-start(bf16[3,72,512]{2,1,0:T(8,128)(2,1)S(1)} %pad_maximum_fusion.1.refs_2_) | copy-start | bytes 663556
  17.3 7.6 %collective-permute-start.3 = (bf16[3,72,512]{2,1,0:T(8,128)(2,1)S(1)}, bf16[3,72,512]{2,1,0:T(8,128)(2,1)S(1)}, u32[]{:S(2)}, u32[]{:S(2)}) collective-permute-start(bf16[3,72,512]{2,1,0:T(8,128)(2,1)S(1)} %pad_maximum_fusion.1.refs_2_), channel_id=1, source_target_pairs={{0,2},{1,3},{2,0},{3,1},{4,6},{5,7},{6,4},{7,5},{8,10},{9,11},{10,... | collective-permute-start | bytes 663560 | tf_op jit(solution)/shard_map/ppermute | solution.py:363
  22.2 6.6 %copy-start.2 = (bf16[4,72,512]{2,1,0:T(8,128)(2,1)}, bf16[4,72,512]{2,1,0:T(8,128)(2,1)S(1)}, u32[]{:S(2)}) copy-start(bf16[4,72,512]{2,1,0:T(8,128)(2,1)S(1)} %collective-permute-done.2.refs_1_) | copy-start | bytes 884740
  22.2 6.6 %copy-start.3 = (bf16[2,72,512]{2,1,0:T(8,128)(2,1)}, bf16[2,72,512]{2,1,0:T(8,128)(2,1)S(1)}, u32[]{:S(2)}) copy-start(bf16[2,72,512]{2,1,0:T(8,128)(2,1)S(1)} %dynamic-slice_bitcast_fusion.refs_4_) | copy-start | bytes 442372
  22.3 5.2 %collective-permute-start.4 = (bf16[2,72,512]{2,1,0:T(8,128)(2,1)S(1)}, bf16[2,72,512]{2,1,0:T(8,128)(2,1)S(1)}, u32[]{:S(2)}, u32[]{:S(2)}) collective-permute-start(bf16[2,72,512]{2,1,0:T(8,128)(2,1)S(1)} %dynamic-slice_bitcast_fusion.refs_4_), channel_id=1, source_target_pairs={{0,2},{1,3},{2,0},{3,1},{4,6},{5,7},{6,4},{7,5},{8,10},{9,11},{10,... | collective-permute-start | bytes 442376 | tf_op jit(solution)/shard_map/ppermute | solution.py:363
  24.1 3.4 %collective-permute-start.5 = (bf16[3,72,512]{2,1,0:T(8,128)(2,1)S(1)}, bf16[3,72,512]{2,1,0:T(8,128)(2,1)S(1)}, u32[]{:S(2)}, u32[]{:S(2)}) collective-permute-start(bf16[3,72,512]{2,1,0:T(8,128)(2,1)S(1)} %pad_maximum_fusion.1.refs_2_), channel_id=1, source_target_pairs={{0,1},{1,0},{2,3},{3,2},{4,5},{5,4},{6,7},{7,6},{8,9},{9,8},{10,11... | collective-permute-start | bytes 663560 | tf_op jit(solution)/shard_map/ppermute | solution.py:363
  24.9 4.0 %copy-start.4 = (bf16[3,72,512]{2,1,0:T(8,128)(2,1)}, bf16[3,72,512]{2,1,0:T(8,128)(2,1)S(1)}, u32[]{:S(2)}) copy-start(bf16[3,72,512]{2,1,0:T(8,128)(2,1)S(1)} %collective-permute-done.3.refs_3_) | copy-start | bytes 663556
  24.9 2.6 %collective-permute-start.6 = (bf16[3,72,512]{2,1,0:T(8,128)(2,1)S(1)}, bf16[3,72,512]{2,1,0:T(8,128)(2,1)S(1)}, u32[]{:S(2)}, u32[]{:S(2)}) collective-permute-start(bf16[3,72,512]{2,1,0:T(8,128)(2,1)S(1)} %collective-permute-done.3.refs_3_), channel_id=1, source_target_pairs={{0,1},{1,0},{2,3},{3,2},{4,5},{5,4},{6,7},{7,6},{8,9},{9,8},{10,11... | collective-permute-start | bytes 663560 | tf_op jit(solution)/shard_map/ppermute | solution.py:363
  24.9 2.7 %collective-permute-start.7 = (bf16[2,72,512]{2,1,0:T(8,128)(2,1)S(1)}, bf16[2,72,512]{2,1,0:T(8,128)(2,1)S(1)}, u32[]{:S(2)}, u32[]{:S(2)}) collective-permute-start(bf16[2,72,512]{2,1,0:T(8,128)(2,1)S(1)} %dynamic-slice_bitcast_fusion.refs_4_), channel_id=1, source_target_pairs={{0,1},{1,0},{2,3},{3,2},{4,5},{5,4},{6,7},{7,6},{8,9},{9,8},{10,11... | collective-permute-start | bytes 442376 | tf_op jit(solution)/shard_map/ppermute | solution.py:363
  27.5 1.4 %copy-start.7 = (bf16[2,72,512]{2,1,0:T(8,128)(2,1)}, bf16[2,72,512]{2,1,0:T(8,128)(2,1)S(1)}, u32[]{:S(2)}) copy-start(bf16[2,72,512]{2,1,0:T(8,128)(2,1)S(1)} %collective-permute-done.4.refs_5_) | copy-start | bytes 442372
  27.5 1.4 %collective-permute-start.8 = (bf16[2,72,512]{2,1,0:T(8,128)(2,1)S(1)}, bf16[2,72,512]{2,1,0:T(8,128)(2,1)S(1)}, u32[]{:S(2)}, u32[]{:S(2)}) collective-permute-start(bf16[2,72,512]{2,1,0:T(8,128)(2,1)S(1)} %collective-permute-done.4.refs_5_), channel_id=1, source_target_pairs={{0,1},{1,0},{2,3},{3,2},{4,5},{5,4},{6,7},{7,6},{8,9},{9,8},{10,11... | collective-permute-start | bytes 442376 | tf_op jit(solution)/shard_map/ppermute | solution.py:363
  27.5 1.4 %copy-start.5 = (bf16[3,72,512]{2,1,0:T(8,128)(2,1)}, bf16[3,72,512]{2,1,0:T(8,128)(2,1)S(1)}, u32[]{:S(2)}) copy-start(bf16[3,72,512]{2,1,0:T(8,128)(2,1)S(1)} %collective-permute-done.5.refs_6_) | copy-start | bytes 663556
  27.5 1.4 %copy-start.6 = (bf16[3,72,512]{2,1,0:T(8,128)(2,1)}, bf16[3,72,512]{2,1,0:T(8,128)(2,1)S(1)}, u32[]{:S(2)}) copy-start(bf16[3,72,512]{2,1,0:T(8,128)(2,1)S(1)} %collective-permute-done.6.refs_7_) | copy-start | bytes 663556
  27.5 1.4 %copy-start.8 = (bf16[2,72,512]{2,1,0:T(8,128)(2,1)}, bf16[2,72,512]{2,1,0:T(8,128)(2,1)S(1)}, u32[]{:S(2)}) copy-start(bf16[2,72,512]{2,1,0:T(8,128)(2,1)S(1)} %collective-permute-done.7.refs_8_) | copy-start | bytes 442372
  28.9 0.7 %copy-start.9 = (bf16[2,72,512]{2,1,0:T(8,128)(2,1)}, bf16[2,72,512]{2,1,0:T(8,128)(2,1)S(1)}, u32[]{:S(2)}) copy-start(bf16[2,72,512]{2,1,0:T(8,128)(2,1)S(1)} %collective-permute-done.8.refs_9_) | copy-start | bytes 442372

commit v5 on v4

--- a/solution.py
+++ b/solution.py
@@ -163,8 +163,8 @@
     lanes = lax.broadcasted_iota(jnp.int32, (1, LANES), 1)
 
     def aux_of(block):
-        line = block[ray_dev : ray_dev + SUBS, :].astype(jnp.float32)[0:1]
-        parts = [line[:, LANES * k : LANES * (k + 1)] for k in range(4)]
+        lines = block[ray_dev : ray_dev + SUBS, 0:LANES].astype(jnp.float32)
+        parts = [lines[k : k + 1] for k in range(4)]
         return parts[0], parts[1] + parts[2] + parts[3]
 
     def put(mine, other, odd, to, numbers):
@@ -208,6 +208,9 @@
 
     panels, row_tiles = lead // PANEL, rows // PANEL
     col_tiles = (cols + PANEL - 1) // PANEL
+
+    skipped = front.shape[2] - cols
+    front[:, 0, 0:skipped] = jnp.zeros((rows, skipped), jnp.float32)
 
     def tile(i):
         start = i * PANEL
@@ -331,9 +334,7 @@
             update(panels, row_tiles, j)
         each(panels, col_tiles, lambda j: update(p + 1, panels + row_tiles - p - 1, j))
 
-    skipped = front.shape[1] - cols
-    front[:, 0:skipped] = jnp.zeros((rows, skipped), jnp.float32)
-    front[:, skipped:] = jnp.where(
+    front[:, 0, skipped:] = jnp.where(
         row_index * rows >= lead, mat[lead : lead + rows, lead : lead + cols], 0.0
     )
 
@@ -343,8 +344,7 @@
     middle = lax.reduce_precision(noise - high, 8, 7)
     terms = jnp.stack([slot_of_ray.astype(jnp.float32), high, middle, noise - high - middle])
     ray_dev, width = features.shape
-    aux = jnp.pad(terms, ((0, 0), (0, LANES - ray_dev))).reshape(1, 4 * LANES)
-    aux = jnp.pad(aux, ((0, SUBS - 1), (0, width - 4 * LANES))).astype(features.dtype)
+    aux = jnp.pad(terms, ((0, SUBS - 4), (0, width - ray_dev))).astype(features.dtype)
     return jnp.concatenate([features, aux])
 
 
@@ -390,7 +390,7 @@
             kernel, ray_dev=ray_dev, row_count=row_count, col_count=col_count, lead=lead, tops=tops
         ),
         out_shape=(
-            jax.ShapeDtypeStruct((rows, col_width), jnp.float32),
+            jax.ShapeDtypeStruct((rows, 1, col_width), jnp.float32),
             jax.ShapeDtypeStruct((rows, lead), jnp.float32),
         ),
         scratch_shapes=[
@@ -402,7 +402,7 @@
         ],
         name="panels",
     )(near, near_x, *side, *side_x, *core, *core_x)
-    return front.reshape(rows, 1, col_width), factor
+    return front, factor
 
 
 def solution(mesh):

time: 64.3 us -> 61.9 us (0.963)
  local copies, waits for them, and re-layouts: 3.09 us -> 0.71 us
    unnamed x24 -> x22, local copies, waits for them, and re-layouts: 3.07 us -> 0.68 us
where the time goes in v5:
time: 61.9 us; the launch traced here: 61.4 us
  Pallas kernels  31.8 us (51%)
  waiting for transfers between devices  16 us (26%)
  starting transfers between devices  10.5 us (17%)
  other arithmetic  1.6 us (3%)
  between operations  0.8 us (1%)
  local copies, waits for them, and re-layouts  0.71 us (1%)
    pallas_call x1, Pallas kernels, shards(): pl.pallas_call(functools.partial(kernel, ray_dev=ray_dev, row_count=row_c...  31.8 us
    ppermute x9, waiting for transfers between devices, other(): return lax.ppermute(value, axis, [(k, k ^ 1 << bit) for k in range(count)])  16 us
    ppermute x9, starting transfers between devices, other(): return lax.ppermute(value, axis, [(k, k ^ 1 << bit) for k in range(count)])  10.5 us
  transfers between devices with their start and end apart: 9, of which 6 were waited for; matrix products, arithmetic and copies ran while one was open for 0% of the time, Pallas kernels for 0%

profile of v5, /device:TPU:0, one launch (start us, length us, event | category | flops | bytes accessed | tf_op | source)
XLA Modules:
  0.0 61.4 jit_solution(16278244971628158572)
XLA Ops:
  0.6 0.0 copy-start.10
  0.6 0.7 %convert_bitcast_fusion = bf16[1,64]{1,0:T(2,128)(2,1)S(1)} fusion(s32[64]{0:T(128)} %param.4), kind=kLoop, calls=%fused_computation.28 | loop fusion | flops 128 | bytes 384 | tf_op jit(solution)/shard_map/stack | solution.py:345
  1.3 0.0 copy-done.10
  1.3 0.8 %maximum_bitcast_fusion = bf16[1,72,512]{2,1,0:T(8,128)(2,1)S(1)} fusion(bf16[8,512]{1,0:T(8,128)(2,1)S(1)} %fusion.8, bf16[64,512]{1,0:T(8,128)(2,1)} %param.3), kind=kLoop, calls=%fused_computation.5 | loop fusion | flops 147456 | bytes 147456 | tf_op jit(solution)/shard_map/broadcast_in_dim | solution.py:365
  2.2 4.1 %collective-permute-start = (bf16[1,72,512]{2,1,0:T(8,128)(2,1)S(1)}, bf16[1,72,512]{2,1,0:T(8,128)(2,1)S(1)}, u32[]{:S(2)}, u32[]{:S(2)}) collective-permute-start(bf16[1,72,512]{2,1,0:T(8,128)(2,1)S(1)} %maximum_bitcast_fusion), channel_id=1, source_target_pairs={{0,16},{4,20},{8,24},{12,28},{16,0},{20,4},{24,8},{28,12},{1,17},{... | collective-permute-start | bytes 221192 | tf_op jit(solution)/shard_map/ppermute | solution.py:363
  6.2 3.9 %collective-permute-done = bf16[1,72,512]{2,1,0:T(8,128)(2,1)S(1)} collective-permute-done((bf16[1,72,512]{2,1,0:T(8,128)(2,1)S(1)}, bf16[1,72,512]{2,1,0:T(8,128)(2,1)S(1)}, u32[]{:S(2)}, u32[]{:S(2)}) %collective-permute-start) | collective-permute-done | bytes 73760 | tf_op jit(solution)/shard_map/ppermute | solution.py:363
  10.2 0.7 %collective-permute-start.1 = (bf16[2,72,512]{2,1,0:T(8,128)(2,1)S(1)}, bf16[2,72,512]{2,1,0:T(8,128)(2,1)S(1)}, u32[]{:S(2)}, u32[]{:S(2)}) collective-permute-start(bf16[2,72,512]{2,1,0:T(8,128)(2,1)S(1)} %pad_maximum_fusion.2), channel_id=1, source_target_pairs={{0,8},{4,12},{8,0},{12,4},{16,24},{20,28},{24,16},{28,20},{1,9},{5... | collective-permute-start | bytes 442376 | tf_op jit(solution)/shard_map/ppermute | solution.py:363
  10.9 4.5 %collective-permute-done.1 = bf16[2,72,512]{2,1,0:T(8,128)(2,1)S(1)} collective-permute-done((bf16[2,72,512]{2,1,0:T(8,128)(2,1)S(1)}, bf16[2,72,512]{2,1,0:T(8,128)(2,1)S(1)}, u32[]{:S(2)}, u32[]{:S(2)}) %collective-permute-start.1) | collective-permute-done | bytes 147488 | tf_op jit(solution)/shard_map/ppermute | solution.py:363
  15.4 0.0 copy-start
  15.4 1.8 %collective-permute-start.2 = (bf16[4,72,512]{2,1,0:T(8,128)(2,1)S(1)}, bf16[4,72,512]{2,1,0:T(8,128)(2,1)S(1)}, u32[]{:S(2)}, u32[]{:S(2)}) collective-permute-start(bf16[4,72,512]{2,1,0:T(8,128)(2,1)S(1)} %pad_maximum_fusion.refs_0_), channel_id=1, source_target_pairs={{0,4},{4,0},{8,12},{12,8},{16,20},{20,16},{24,28},{28,24},{1,5},{5... | collective-permute-start | bytes 884744 | tf_op jit(solution)/shard_map/ppermute | solution.py:363
  17.2 0.0 copy-done
  17.3 0.0 copy-start.1
  17.3 1.6 %collective-permute-start.3 = (bf16[3,72,512]{2,1,0:T(8,128)(2,1)S(1)}, bf16[3,72,512]{2,1,0:T(8,128)(2,1)S(1)}, u32[]{:S(2)}, u32[]{:S(2)}) collective-permute-start(bf16[3,72,512]{2,1,0:T(8,128)(2,1)S(1)} %pad_maximum_fusion.1.refs_2_), channel_id=1, source_target_pairs={{0,2},{1,3},{2,0},{3,1},{4,6},{5,7},{6,4},{7,5},{8,10},{9,11},{10,... | collective-permute-start | bytes 663560 | tf_op jit(solution)/shard_map/ppermute | solution.py:363
  18.8 3.4 %collective-permute-done.2.refs_1_ = bf16[4,72,512]{2,1,0:T(8,128)(2,1)S(1)} collective-permute-done((bf16[4,72,512]{2,1,0:T(8,128)(2,1)S(1)}, bf16[4,72,512]{2,1,0:T(8,128)(2,1)S(1)}, u32[]{:S(2)}, u32[]{:S(2)}) %collective-permute-start.2) | collective-permute-done | bytes 294944 | tf_op jit(solution)/shard_map/ppermute | solution.py:363
  22.2 0.0 copy-start.2
  22.2 0.0 copy-start.3
  22.2 1.8 %collective-permute-start.4 = (bf16[2,72,512]{2,1,0:T(8,128)(2,1)S(1)}, bf16[2,72,512]{2,1,0:T(8,128)(2,1)S(1)}, u32[]{:S(2)}, u32[]{:S(2)}) collective-permute-start(bf16[2,72,512]{2,1,0:T(8,128)(2,1)S(1)} %dynamic-slice_bitcast_fusion.refs_4_), channel_id=1, source_target_pairs={{0,2},{1,3},{2,0},{3,1},{4,6},{5,7},{6,4},{7,5},{8,10},{9,11},{10,... | collective-permute-start | bytes 442376 | tf_op jit(solution)/shard_map/ppermute | solution.py:363
  24.0 0.0 collective-permute-start.5
  24.0 0.8 %collective-permute-done.3.refs_3_ = bf16[3,72,512]{2,1,0:T(8,128)(2,1)S(1)} collective-permute-done((bf16[3,72,512]{2,1,0:T(8,128)(2,1)S(1)}, bf16[3,72,512]{2,1,0:T(8,128)(2,1)S(1)}, u32[]{:S(2)}, u32[]{:S(2)}) %collective-permute-start.3) | collective-permute-done | bytes 221216 | tf_op jit(solution)/shard_map/ppermute | solution.py:363
  24.8 0.0 copy-start.4
  24.8 0.0 collective-permute-start.6
  24.8 0.5 collective-permute-start.7
  25.4 2.1 %collective-permute-done.4.refs_5_ = bf16[2,72,512]{2,1,0:T(8,128)(2,1)S(1)} collective-permute-done((bf16[2,72,512]{2,1,0:T(8,128)(2,1)S(1)}, bf16[2,72,512]{2,1,0:T(8,128)(2,1)S(1)}, u32[]{:S(2)}, u32[]{:S(2)}) %collective-permute-start.4) | collective-permute-done | bytes 147488 | tf_op jit(solution)/shard_map/ppermute | solution.py:363
  27.5 0.0 copy-start.7
  27.5 0.0 collective-permute-start.8
  27.5 0.0 collective-permute-done.5.refs_6_
  27.5 0.0 copy-start.5
  27.5 0.0 collective-permute-done.6.refs_7_
  27.5 0.0 copy-start.6
  27.5 0.0 collective-permute-done.7.refs_8_
  27.5 0.0 copy-start.8
  27.5 1.3 %collective-permute-done.8.refs_9_ = bf16[2,72,512]{2,1,0:T(8,128)(2,1)S(1)} collective-permute-done((bf16[2,72,512]{2,1,0:T(8,128)(2,1)S(1)}, bf16[2,72,512]{2,1,0:T(8,128)(2,1)S(1)}, u32[]{:S(2)}, u32[]{:S(2)}) %collective-permute-start.8) | collective-permute-done | bytes 147488 | tf_op jit(solution)/shard_map/ppermute | solution.py:363
  28.8 0.0 copy-done.1
  28.8 0.0 copy-done.2
  28.8 0.0 copy-done.3
  28.8 0.0 copy-done.4
  28.8 0.0 copy-done.7
  28.9 0.0 copy-done.5
  28.9 0.0 copy-done.6
  28.9 0.0 copy-done.8
  28.9 0.0 copy-start.9
  28.9 0.6 %copy-done.9 = bf16[2,72,512]{2,1,0:T(8,128)(2,1)} copy-done((bf16[2,72,512]{2,1,0:T(8,128)(2,1)}, bf16[2,72,512]{2,1,0:T(8,128)(2,1)S(1)}, u32[]{:S(2)}) %copy-start.9) | copy-done | bytes 147480
  29.5 31.8 %panels.1 = (f32[256,1,512]{2,1,0:T(1,128)}, f32[256,1024]{1,0:T(8,128)}) custom-call(bf16[4,72,512]{2,1,0:T(8,128)(2,1)} %copy-done, bf16[4,72,512]{2,1,0:T(8,128)(2,1)} %copy-done.2, bf16[3,72,512]{2,1,0:T(8,128)(2,1)} %copy-done.1, bf16[3,72,512]{2,1,0:T(8,128)(2,1)} %copy-done.4, bf16[2,72,512]{2,1,0:T(8,128)(2,1)} %copy-done.3, ...), custom_call_target="tpu_custom_call" | custom-call | tf_op jit(solution)/shard_map/panels/pallas_call | solution.py:388
  (7 shorter events, 0.1 us)
Async XLA Ops:
  0.6 0.7 %copy-start.10 = (f32[64]{0:T(128)S(1)}, f32[64]{0:T(128)}, u32[]{:S(2)}) copy-start(f32[64]{0:T(128)} %param.5) | copy-start | bytes 772
  2.2 8.0 %collective-permute-start = (bf16[1,72,512]{2,1,0:T(8,128)(2,1)S(1)}, bf16[1,72,512]{2,1,0:T(8,128)(2,1)S(1)}, u32[]{:S(2)}, u32[]{:S(2)}) collective-permute-start(bf16[1,72,512]{2,1,0:T(8,128)(2,1)S(1)} %maximum_bitcast_fusion), channel_id=1, source_target_pairs={{0,16},{4,20},{8,24},{12,28},{16,0},{20,4},{24,8},{28,12},{1,17},{... | collective-permute-start | bytes 221192 | tf_op jit(solution)/shard_map/ppermute | solution.py:363
  10.2 5.2 %collective-permute-start.1 = (bf16[2,72,512]{2,1,0:T(8,128)(2,1)S(1)}, bf16[2,72,512]{2,1,0:T(8,128)(2,1)S(1)}, u32[]{:S(2)}, u32[]{:S(2)}) collective-permute-start(bf16[2,72,512]{2,1,0:T(8,128)(2,1)S(1)} %pad_maximum_fusion.2), channel_id=1, source_target_pairs={{0,8},{4,12},{8,0},{12,4},{16,24},{20,28},{24,16},{28,20},{1,9},{5... | collective-permute-start | bytes 442376 | tf_op jit(solution)/shard_map/ppermute | solution.py:363
  15.4 1.8 %copy-start = (bf16[4,72,512]{2,1,0:T(8,128)(2,1)}, bf16[4,72,512]{2,1,0:T(8,128)(2,1)S(1)}, u32[]{:S(2)}) copy-start(bf16[4,72,512]{2,1,0:T(8,128)(2,1)S(1)} %pad_maximum_fusion.refs_0_) | copy-start | bytes 884740
  15.4 6.8 %collective-permute-start.2 = (bf16[4,72,512]{2,1,0:T(8,128)(2,1)S(1)}, bf16[4,72,512]{2,1,0:T(8,128)(2,1)S(1)}, u32[]{:S(2)}, u32[]{:S(2)}) collective-permute-start(bf16[4,72,512]{2,1,0:T(8,128)(2,1)S(1)} %pad_maximum_fusion.refs_0_), channel_id=1, source_target_pairs={{0,4},{4,0},{8,12},{12,8},{16,20},{20,16},{24,28},{28,24},{1,5},{5... | collective-permute-start | bytes 884744 | tf_op jit(solution)/shard_map/ppermute | solution.py:363
  17.3 11.6 %copy-start.1 = (bf16[3,72,512]{2,1,0:T(8,128)(2,1)}, bf16[3,72,512]{2,1,0:T(8,128)(2,1)S(1)}, u32[]{:S(2)}) copy-start(bf16[3,72,512]{2,1,0:T(8,128)(2,1)S(1)} %pad_maximum_fusion.1.refs_2_) | copy-start | bytes 663556
  17.3 7.6 %collective-permute-start.3 = (bf16[3,72,512]{2,1,0:T(8,128)(2,1)S(1)}, bf16[3,72,512]{2,1,0:T(8,128)(2,1)S(1)}, u32[]{:S(2)}, u32[]{:S(2)}) collective-permute-start(bf16[3,72,512]{2,1,0:T(8,128)(2,1)S(1)} %pad_maximum_fusion.1.refs_2_), channel_id=1, source_target_pairs={{0,2},{1,3},{2,0},{3,1},{4,6},{5,7},{6,4},{7,5},{8,10},{9,11},{10,... | collective-permute-start | bytes 663560 | tf_op jit(solution)/shard_map/ppermute | solution.py:363
  22.2 6.6 %copy-start.2 = (bf16[4,72,512]{2,1,0:T(8,128)(2,1)}, bf16[4,72,512]{2,1,0:T(8,128)(2,1)S(1)}, u32[]{:S(2)}) copy-start(bf16[4,72,512]{2,1,0:T(8,128)(2,1)S(1)} %collective-permute-done.2.refs_1_) | copy-start | bytes 884740
  22.2 6.6 %copy-start.3 = (bf16[2,72,512]{2,1,0:T(8,128)(2,1)}, bf16[2,72,512]{2,1,0:T(8,128)(2,1)S(1)}, u32[]{:S(2)}) copy-start(bf16[2,72,512]{2,1,0:T(8,128)(2,1)S(1)} %dynamic-slice_bitcast_fusion.refs_4_) | copy-start | bytes 442372
  22.2 5.2 %collective-permute-start.4 = (bf16[2,72,512]{2,1,0:T(8,128)(2,1)S(1)}, bf16[2,72,512]{2,1,0:T(8,128)(2,1)S(1)}, u32[]{:S(2)}, u32[]{:S(2)}) collective-permute-start(bf16[2,72,512]{2,1,0:T(8,128)(2,1)S(1)} %dynamic-slice_bitcast_fusion.refs_4_), channel_id=1, source_target_pairs={{0,2},{1,3},{2,0},{3,1},{4,6},{5,7},{6,4},{7,5},{8,10},{9,11},{10,... | collective-permute-start | bytes 442376 | tf_op jit(solution)/shard_map/ppermute | solution.py:363
  24.0 3.4 %collective-permute-start.5 = (bf16[3,72,512]{2,1,0:T(8,128)(2,1)S(1)}, bf16[3,72,512]{2,1,0:T(8,128)(2,1)S(1)}, u32[]{:S(2)}, u32[]{:S(2)}) collective-permute-start(bf16[3,72,512]{2,1,0:T(8,128)(2,1)S(1)} %pad_maximum_fusion.1.refs_2_), channel_id=1, source_target_pairs={{0,1},{1,0},{2,3},{3,2},{4,5},{5,4},{6,7},{7,6},{8,9},{9,8},{10,11... | collective-permute-start | bytes 663560 | tf_op jit(solution)/shard_map/ppermute | solution.py:363
  24.8 4.0 %copy-start.4 = (bf16[3,72,512]{2,1,0:T(8,128)(2,1)}, bf16[3,72,512]{2,1,0:T(8,128)(2,1)S(1)}, u32[]{:S(2)}) copy-start(bf16[3,72,512]{2,1,0:T(8,128)(2,1)S(1)} %collective-permute-done.3.refs_3_) | copy-start | bytes 663556
  24.8 2.6 %collective-permute-start.6 = (bf16[3,72,512]{2,1,0:T(8,128)(2,1)S(1)}, bf16[3,72,512]{2,1,0:T(8,128)(2,1)S(1)}, u32[]{:S(2)}, u32[]{:S(2)}) collective-permute-start(bf16[3,72,512]{2,1,0:T(8,128)(2,1)S(1)} %collective-permute-done.3.refs_3_), channel_id=1, source_target_pairs={{0,1},{1,0},{2,3},{3,2},{4,5},{5,4},{6,7},{7,6},{8,9},{9,8},{10,11... | collective-permute-start | bytes 663560 | tf_op jit(solution)/shard_map/ppermute | solution.py:363
  24.8 2.7 %collective-permute-start.7 = (bf16[2,72,512]{2,1,0:T(8,128)(2,1)S(1)}, bf16[2,72,512]{2,1,0:T(8,128)(2,1)S(1)}, u32[]{:S(2)}, u32[]{:S(2)}) collective-permute-start(bf16[2,72,512]{2,1,0:T(8,128)(2,1)S(1)} %dynamic-slice_bitcast_fusion.refs_4_), channel_id=1, source_target_pairs={{0,1},{1,0},{2,3},{3,2},{4,5},{5,4},{6,7},{7,6},{8,9},{9,8},{10,11... | collective-permute-start | bytes 442376 | tf_op jit(solution)/shard_map/ppermute | solution.py:363
  27.5 1.4 %copy-start.7 = (bf16[2,72,512]{2,1,0:T(8,128)(2,1)}, bf16[2,72,512]{2,1,0:T(8,128)(2,1)S(1)}, u32[]{:S(2)}) copy-start(bf16[2,72,512]{2,1,0:T(8,128)(2,1)S(1)} %collective-permute-done.4.refs_5_) | copy-start | bytes 442372
  27.5 1.4 %collective-permute-start.8 = (bf16[2,72,512]{2,1,0:T(8,128)(2,1)S(1)}, bf16[2,72,512]{2,1,0:T(8,128)(2,1)S(1)}, u32[]{:S(2)}, u32[]{:S(2)}) collective-permute-start(bf16[2,72,512]{2,1,0:T(8,128)(2,1)S(1)} %collective-permute-done.4.refs_5_), channel_id=1, source_target_pairs={{0,1},{1,0},{2,3},{3,2},{4,5},{5,4},{6,7},{7,6},{8,9},{9,8},{10,11... | collective-permute-start | bytes 442376 | tf_op jit(solution)/shard_map/ppermute | solution.py:363
  27.5 1.4 %copy-start.5 = (bf16[3,72,512]{2,1,0:T(8,128)(2,1)}, bf16[3,72,512]{2,1,0:T(8,128)(2,1)S(1)}, u32[]{:S(2)}) copy-start(bf16[3,72,512]{2,1,0:T(8,128)(2,1)S(1)} %collective-permute-done.5.refs_6_) | copy-start | bytes 663556
  27.5 1.4 %copy-start.6 = (bf16[3,72,512]{2,1,0:T(8,128)(2,1)}, bf16[3,72,512]{2,1,0:T(8,128)(2,1)S(1)}, u32[]{:S(2)}) copy-start(bf16[3,72,512]{2,1,0:T(8,128)(2,1)S(1)} %collective-permute-done.6.refs_7_) | copy-start | bytes 663556
  27.5 1.4 %copy-start.8 = (bf16[2,72,512]{2,1,0:T(8,128)(2,1)}, bf16[2,72,512]{2,1,0:T(8,128)(2,1)S(1)}, u32[]{:S(2)}) copy-start(bf16[2,72,512]{2,1,0:T(8,128)(2,1)S(1)} %collective-permute-done.7.refs_8_) | copy-start | bytes 442372
  28.9 0.7 %copy-start.9 = (bf16[2,72,512]{2,1,0:T(8,128)(2,1)}, bf16[2,72,512]{2,1,0:T(8,128)(2,1)S(1)}, u32[]{:S(2)}) copy-start(bf16[2,72,512]{2,1,0:T(8,128)(2,1)S(1)} %collective-permute-done.8.refs_9_) | copy-start | bytes 442372

commit v6 on v5

--- a/solution.py
+++ b/solution.py
@@ -42,7 +42,7 @@
     return jnp.dot(a, b, preferred_element_type=jnp.float32)
 
 
-def inverse_factor(block):
+def inverse_factor(block, others=()):
     count = block.shape[0] // SUBS
     per, ahead = count // 2, SUBS // 2
     strips = [block[SUBS * t : SUBS * (t + 1), :] for t in range(count)]
@@ -59,6 +59,8 @@
     result = []
     early = []
     for s in range(count):
+        for work in others[len(others) * s // count : len(others) * (s + 1) // count]:
+            work()
         base = SUBS * s
         end = (s // per + 1) * per
         raw = early + [over_lanes(strips[s], base + j) for j in range(len(early), SUBS)]
@@ -152,7 +154,7 @@
     near, near_x = refs[:2]
     lists = [refs[2 + k * tops : 2 + (k + 1) * tops] for k in range(4)]
     side, side_x, core, core_x = lists
-    front, factor, feat, slot, noise, ray, mat, upper, lowers = refs[2 + 4 * tops :]
+    front, factor, feat, slot, noise, ray, mat, uppers, lowers_of = refs[2 + 4 * tops :]
     row_index, col_index = lax.axis_index("row"), lax.axis_index("col")
     rows = ray_dev * col_count
     pair_count = near.shape[0]
@@ -218,13 +220,14 @@
 
     def each(start, count, body):
         if count <= 2:
-            for i in range(start, start + count):
-                body(i)
-        else:
-
+            return [functools.partial(body, i) for i in range(start, start + count)]
+
+        def loop():
             @pl.loop(start, start + count)
             def _(i):
                 body(i)
+
+        return [loop]
 
     def column(source, i):
         return jnp.concatenate([as_column(source[pl.ds(2 * i + k, 1), :]) for k in range(2)], axis=0)
@@ -251,68 +254,88 @@
             halves.append(part)
         mat[tile(i), tile(j)] = jnp.concatenate(halves, axis=1)
 
-    for i in range(panels):
-        slot_a = column(slot, i)
-        fill(i, i, slot_a, column(ray, i))
-        for j in range(i + 1, panels):
-            fill(i, j, slot_a)
-        each(panels, col_tiles, lambda j: fill(i, j, slot_a))
-
-    def fill_row(i):
-        slot_a, ray_a = column(slot, i), column(ray, i)
-        for j in range(panels):
-            fill(i, j, slot_a, ray_a)
-        each(panels, col_tiles, lambda j: fill(i, j, slot_a, ray_a))
-
-    each(panels, row_tiles, fill_row)
+    columns = {}
+
+    def prepare(i):
+        columns[i] = column(slot, i), column(ray, i)
+
+    def fill_lead(i, j):
+        fill(i, j, columns[i][0])
+
+    def fill_own(i, j):
+        fill(i, j, *columns[i])
+
+    def fills(i):
+        found = [functools.partial(fill_lead, i, j) for j in range(i + 1, panels)]
+        return found + each(panels, col_tiles, functools.partial(fill_lead, i))
+
+    prepare(0)
+    fill_own(0, 0)
+    early, late = fills(0), []
+    for i in range(1, panels):
+        own = [functools.partial(prepare, i), functools.partial(fill_own, i, i)]
+        if i == 1:
+            early += own
+        else:
+            late += own
+        late += fills(i)
+    for i in range(panels, panels + row_tiles):
+        late += [functools.partial(prepare, i)]
+        late += [functools.partial(fill_own, i, j) for j in range(panels)]
+        late += each(panels, col_tiles, functools.partial(fill_own, i))
 
     half = 6 * HALF
 
     for p in range(panels):
+        upper, lowers = uppers.at[p % uppers.shape[0]], lowers_of.at[p % uppers.shape[0]]
         top, low = pl.ds(p * PANEL, HALF), pl.ds(p * PANEL + HALF, HALF)
-        inv_a = inverse_factor(mat[top, top])
+        inv_a = inverse_factor(mat[top, top], early)
         left_a = left(inv_a)
         cross = product(left_a, right(mat[top, low]))
         cross_left, cross_right = left(cross.T), right(cross)
         corner = mat[low, low] - product(cross_left, cross_right)
 
-        def solve_top(j):
+        def solve_top(j, upper=upper, left_a=left_a, cross_left=cross_left, top=top, low=low):
             found = product(left_a, right(mat[top, tile(j)]))
             terms = right(found)
             upper[0:half, tile(j)] = terms
             mat[low, tile(j)] -= product(cross_left, terms)
             return found
 
-        def solve_low(j):
+        if p + 1 < panels:
+            lowers[tile(p + 1), 0:half] = left(solve_top(p + 1).T)
+            mat[tile(p + 1), tile(p + 1)] -= product(
+                lowers[tile(p + 1), 0:half], upper[0:half, tile(p + 1)]
+            )
+
+        def top_of(j, lowers=lowers, solve_top=solve_top):
+            lowers[tile(j), 0:half] = left(solve_top(j).T)
+
+        late = late + [functools.partial(top_of, j) for j in range(p + 2, panels)]
+        inv_b = inverse_factor(corner, late + each(panels, col_tiles, solve_top))
+        left_b = left(inv_b)
+
+        def solve_low(j, upper=upper, left_b=left_b, low=low):
             found = product(left_b, right(mat[low, tile(j)]))
             upper[half:, tile(j)] = right(found)
             return found
 
-        for j in range(p + 1, panels):
-            lowers[tile(j), 0:half] = left(solve_top(j).T)
+        def low_of(j, lowers=lowers, solve_low=solve_low):
+            lowers[tile(j), half:] = left(solve_low(j).T)
+
         if p + 1 < panels:
+            low_of(p + 1)
             mat[tile(p + 1), tile(p + 1)] -= product(
-                lowers[tile(p + 1), 0:half], upper[0:half, tile(p + 1)]
+                lowers[tile(p + 1), half:], upper[half:, tile(p + 1)]
             )
-        inv_b = inverse_factor(corner)
-        left_b = left(inv_b)
-        for j in range(p + 1, panels):
-            lowers[tile(j), half:] = left(solve_low(j).T)
-            if j == p + 1:
-                mat[tile(j), tile(j)] -= product(lowers[tile(j), half:], upper[half:, tile(j)])
-
-        def solve(j):
-            solve_top(j)
-            solve_low(j)
-
-        each(panels, col_tiles, solve)
-        right_a, right_b = right(inv_a.T), right(inv_b.T)
-
-        def solve_row(i):
+
+        def solve_row(
+            i, p=p, top=top, low=low, inv_a=inv_a, inv_b=inv_b, cross_right=cross_right, lowers=lowers
+        ):
             row = tile(panels + i)
-            first = product(left(mat[row, top]), right_a)
+            first = product(left(mat[row, top]), right(inv_a.T))
             first_left = left(first)
-            second = product(left(mat[row, low] - product(first_left, cross_right)), right_b)
+            second = product(left(mat[row, low] - product(first_left, cross_right)), right(inv_b.T))
             ray_a = column(ray, panels + i)
             kept = [
                 jnp.where(ray_a >= ray_b, part, 0.0)
@@ -322,17 +345,27 @@
             lowers[row, 0:half] = first_left
             lowers[row, half:] = left(second)
 
-        each(0, row_tiles, solve_row)
-
-        def update(start, count, j):
+        def update(start, count, j, upper=upper, lowers=lowers):
             some = pl.ds(start * PANEL, count * PANEL)
             mat[some, tile(j)] -= product(lowers[some, :], upper[:, tile(j)])
 
-        for j in range(p + 1, panels):
-            if j > p + 1:
-                update(p + 1, j - p, j)
-            update(panels, row_tiles, j)
-        each(panels, col_tiles, lambda j: update(p + 1, panels + row_tiles - p - 1, j))
+        rest = panels + row_tiles
+        early = [functools.partial(low_of, j) for j in range(p + 2, panels)]
+        early += each(panels, col_tiles, solve_low)
+        late = each(0, row_tiles, solve_row)
+        if p + 1 < panels:
+            early += [functools.partial(update, p + 1, 1, j) for j in range(p + 2, panels)]
+            early += each(panels, col_tiles, functools.partial(update, p + 1, 1))
+            late += [
+                functools.partial(update, p + 2, j - p - 1, j) for j in range(p + 2, panels)
+            ]
+            late += [functools.partial(update, panels, row_tiles, j) for j in range(p + 1, panels)]
+        late += each(panels, col_tiles, functools.partial(update, p + 2, rest - p - 2) if p + 1 < panels
+            else functools.partial(update, panels, row_tiles))
+        if uppers.shape[0] == 1 and p + 1 < panels:
+            early, late = early + late, []
+    for work in early + late:
+        work()
 
     front[:, 0, skipped:] = jnp.where(
         row_index * rows >= lead, mat[lead : lead + rows, lead : lead + cols], 0.0
@@ -385,6 +418,7 @@
     cols = col_width - lead // col_count
     padded = -(-cols // PANEL) * PANEL
     rays = lead + rows + padded
+    sets = 2 if padded <= 2 * PANEL else 1
     front, factor = pl.pallas_call(
         functools.partial(
             kernel, ray_dev=ray_dev, row_count=row_count, col_count=col_count, lead=lead, tops=tops
@@ -397,8 +431,8 @@
             pltpu.VMEM((rays, features.shape[1]), features.dtype),
             *[pltpu.VMEM((rays // LANES, LANES), jnp.float32)] * 3,
             pltpu.VMEM((lead + rows, lead + padded), jnp.float32),
-            pltpu.VMEM((6 * PANEL, lead + padded), jnp.bfloat16),
-            pltpu.VMEM((lead + rows, 6 * PANEL), jnp.bfloat16),
+            pltpu.VMEM((sets, 6 * PANEL, lead + padded), jnp.bfloat16),
+            pltpu.VMEM((sets, lead + rows, 6 * PANEL), jnp.bfloat16),
         ],
         name="panels",
     )(near, near_x, *side, *side_x, *core, *core_x)

time: 61.9 us -> 60.2 us (0.973)
  Pallas kernels: 31.8 us -> 30.2 us
    pallas_call x1, Pallas kernels: 31.8 us -> 30.2 us  [shards(): pl.pallas_call(functools.partial(kernel, ray_dev=ray_dev, row_count=row_c...]
where the time goes in v6:
time: 60.2 us; the launch traced here: 59.7 us
  Pallas kernels  30.2 us (50%)
  waiting for transfers between devices  16 us (27%)
  starting transfers between devices  10.5 us (17%)
  other arithmetic  1.6 us (3%)
  between operations  0.8 us (1%)
  local copies, waits for them, and re-layouts  0.71 us (1%)
    pallas_call x1, Pallas kernels, shards(): pl.pallas_call(functools.partial(kernel, ray_dev=ray_dev, row_count=row_c...  30.2 us
    ppermute x9, waiting for transfers between devices, other(): return lax.ppermute(value, axis, [(k, k ^ 1 << bit) for k in range(count)])  16 us
    ppermute x9, starting transfers between devices, other(): return lax.ppermute(value, axis, [(k, k ^ 1 << bit) for k in range(count)])  10.5 us
  transfers between devices with their start and end apart: 9, of which 6 were waited for; matrix products, arithmetic and copies ran while one was open for 0% of the time, Pallas kernels for 0%

profile of v6, /device:TPU:0, one launch (start us, length us, event | category | flops | bytes accessed | tf_op | source)
XLA Modules:
  0.0 59.7 jit_solution(7831095055827068228)
XLA Ops:
  0.6 0.0 copy-start.10
  0.6 0.7 %convert_bitcast_fusion = bf16[1,64]{1,0:T(2,128)(2,1)S(1)} fusion(s32[64]{0:T(128)} %param.4), kind=kLoop, calls=%fused_computation.28 | loop fusion | flops 128 | bytes 384 | tf_op jit(solution)/shard_map/stack | solution.py:378
  1.3 0.0 copy-done.10
  1.3 0.8 %maximum_bitcast_fusion = bf16[1,72,512]{2,1,0:T(8,128)(2,1)S(1)} fusion(bf16[8,512]{1,0:T(8,128)(2,1)S(1)} %fusion.8, bf16[64,512]{1,0:T(8,128)(2,1)} %param.3), kind=kLoop, calls=%fused_computation.5 | loop fusion | flops 147456 | bytes 147456 | tf_op jit(solution)/shard_map/broadcast_in_dim | solution.py:398
  2.2 4.1 %collective-permute-start = (bf16[1,72,512]{2,1,0:T(8,128)(2,1)S(1)}, bf16[1,72,512]{2,1,0:T(8,128)(2,1)S(1)}, u32[]{:S(2)}, u32[]{:S(2)}) collective-permute-start(bf16[1,72,512]{2,1,0:T(8,128)(2,1)S(1)} %maximum_bitcast_fusion), channel_id=1, source_target_pairs={{0,16},{4,20},{8,24},{12,28},{16,0},{20,4},{24,8},{28,12},{1,17},{... | collective-permute-start | bytes 221192 | tf_op jit(solution)/shard_map/ppermute | solution.py:396
  6.2 3.9 %collective-permute-done = bf16[1,72,512]{2,1,0:T(8,128)(2,1)S(1)} collective-permute-done((bf16[1,72,512]{2,1,0:T(8,128)(2,1)S(1)}, bf16[1,72,512]{2,1,0:T(8,128)(2,1)S(1)}, u32[]{:S(2)}, u32[]{:S(2)}) %collective-permute-start) | collective-permute-done | bytes 73760 | tf_op jit(solution)/shard_map/ppermute | solution.py:396
  10.2 0.7 %collective-permute-start.1 = (bf16[2,72,512]{2,1,0:T(8,128)(2,1)S(1)}, bf16[2,72,512]{2,1,0:T(8,128)(2,1)S(1)}, u32[]{:S(2)}, u32[]{:S(2)}) collective-permute-start(bf16[2,72,512]{2,1,0:T(8,128)(2,1)S(1)} %pad_maximum_fusion.2), channel_id=1, source_target_pairs={{0,8},{4,12},{8,0},{12,4},{16,24},{20,28},{24,16},{28,20},{1,9},{5... | collective-permute-start | bytes 442376 | tf_op jit(solution)/shard_map/ppermute | solution.py:396
  10.9 4.5 %collective-permute-done.1 = bf16[2,72,512]{2,1,0:T(8,128)(2,1)S(1)} collective-permute-done((bf16[2,72,512]{2,1,0:T(8,128)(2,1)S(1)}, bf16[2,72,512]{2,1,0:T(8,128)(2,1)S(1)}, u32[]{:S(2)}, u32[]{:S(2)}) %collective-permute-start.1) | collective-permute-done | bytes 147488 | tf_op jit(solution)/shard_map/ppermute | solution.py:396
  15.4 0.0 copy-start
  15.4 1.8 %collective-permute-start.2 = (bf16[4,72,512]{2,1,0:T(8,128)(2,1)S(1)}, bf16[4,72,512]{2,1,0:T(8,128)(2,1)S(1)}, u32[]{:S(2)}, u32[]{:S(2)}) collective-permute-start(bf16[4,72,512]{2,1,0:T(8,128)(2,1)S(1)} %pad_maximum_fusion.refs_0_), channel_id=1, source_target_pairs={{0,4},{4,0},{8,12},{12,8},{16,20},{20,16},{24,28},{28,24},{1,5},{5... | collective-permute-start | bytes 884744 | tf_op jit(solution)/shard_map/ppermute | solution.py:396
  17.2 0.0 copy-done
  17.3 0.0 copy-start.1
  17.3 1.6 %collective-permute-start.3 = (bf16[3,72,512]{2,1,0:T(8,128)(2,1)S(1)}, bf16[3,72,512]{2,1,0:T(8,128)(2,1)S(1)}, u32[]{:S(2)}, u32[]{:S(2)}) collective-permute-start(bf16[3,72,512]{2,1,0:T(8,128)(2,1)S(1)} %pad_maximum_fusion.1.refs_2_), channel_id=1, source_target_pairs={{0,2},{1,3},{2,0},{3,1},{4,6},{5,7},{6,4},{7,5},{8,10},{9,11},{10,... | collective-permute-start | bytes 663560 | tf_op jit(solution)/shard_map/ppermute | solution.py:396
  18.8 3.4 %collective-permute-done.2.refs_1_ = bf16[4,72,512]{2,1,0:T(8,128)(2,1)S(1)} collective-permute-done((bf16[4,72,512]{2,1,0:T(8,128)(2,1)S(1)}, bf16[4,72,512]{2,1,0:T(8,128)(2,1)S(1)}, u32[]{:S(2)}, u32[]{:S(2)}) %collective-permute-start.2) | collective-permute-done | bytes 294944 | tf_op jit(solution)/shard_map/ppermute | solution.py:396
  22.2 0.0 copy-start.2
  22.2 0.0 copy-start.3
  22.2 1.8 %collective-permute-start.4 = (bf16[2,72,512]{2,1,0:T(8,128)(2,1)S(1)}, bf16[2,72,512]{2,1,0:T(8,128)(2,1)S(1)}, u32[]{:S(2)}, u32[]{:S(2)}) collective-permute-start(bf16[2,72,512]{2,1,0:T(8,128)(2,1)S(1)} %dynamic-slice_bitcast_fusion.refs_4_), channel_id=1, source_target_pairs={{0,2},{1,3},{2,0},{3,1},{4,6},{5,7},{6,4},{7,5},{8,10},{9,11},{10,... | collective-permute-start | bytes 442376 | tf_op jit(solution)/shard_map/ppermute | solution.py:396
  24.0 0.0 collective-permute-start.5
  24.0 0.8 %collective-permute-done.3.refs_3_ = bf16[3,72,512]{2,1,0:T(8,128)(2,1)S(1)} collective-permute-done((bf16[3,72,512]{2,1,0:T(8,128)(2,1)S(1)}, bf16[3,72,512]{2,1,0:T(8,128)(2,1)S(1)}, u32[]{:S(2)}, u32[]{:S(2)}) %collective-permute-start.3) | collective-permute-done | bytes 221216 | tf_op jit(solution)/shard_map/ppermute | solution.py:396
  24.8 0.0 copy-start.4
  24.8 0.0 collective-permute-start.6
  24.8 0.5 collective-permute-start.7
  25.4 2.1 %collective-permute-done.4.refs_5_ = bf16[2,72,512]{2,1,0:T(8,128)(2,1)S(1)} collective-permute-done((bf16[2,72,512]{2,1,0:T(8,128)(2,1)S(1)}, bf16[2,72,512]{2,1,0:T(8,128)(2,1)S(1)}, u32[]{:S(2)}, u32[]{:S(2)}) %collective-permute-start.4) | collective-permute-done | bytes 147488 | tf_op jit(solution)/shard_map/ppermute | solution.py:396
  27.5 0.0 copy-start.7
  27.5 0.0 collective-permute-start.8
  27.5 0.0 collective-permute-done.5.refs_6_
  27.5 0.0 copy-start.5
  27.5 0.0 collective-permute-done.6.refs_7_
  27.5 0.0 copy-start.6
  27.5 0.0 collective-permute-done.7.refs_8_
  27.5 0.0 copy-start.8
  27.5 1.3 %collective-permute-done.8.refs_9_ = bf16[2,72,512]{2,1,0:T(8,128)(2,1)S(1)} collective-permute-done((bf16[2,72,512]{2,1,0:T(8,128)(2,1)S(1)}, bf16[2,72,512]{2,1,0:T(8,128)(2,1)S(1)}, u32[]{:S(2)}, u32[]{:S(2)}) %collective-permute-start.8) | collective-permute-done | bytes 147488 | tf_op jit(solution)/shard_map/ppermute | solution.py:396
  28.8 0.0 copy-done.1
  28.8 0.0 copy-done.2
  28.8 0.0 copy-done.3
  28.8 0.0 copy-done.4
  28.8 0.0 copy-done.7
  28.9 0.0 copy-done.5
  28.9 0.0 copy-done.6
  28.9 0.0 copy-done.8
  28.9 0.0 copy-start.9
  28.9 0.6 %copy-done.9 = bf16[2,72,512]{2,1,0:T(8,128)(2,1)} copy-done((bf16[2,72,512]{2,1,0:T(8,128)(2,1)}, bf16[2,72,512]{2,1,0:T(8,128)(2,1)S(1)}, u32[]{:S(2)}) %copy-start.9) | copy-done | bytes 147480
  29.5 30.2 %panels.1 = (f32[256,1,512]{2,1,0:T(1,128)}, f32[256,1024]{1,0:T(8,128)}) custom-call(bf16[4,72,512]{2,1,0:T(8,128)(2,1)} %copy-done, bf16[4,72,512]{2,1,0:T(8,128)(2,1)} %copy-done.2, bf16[3,72,512]{2,1,0:T(8,128)(2,1)} %copy-done.1, bf16[3,72,512]{2,1,0:T(8,128)(2,1)} %copy-done.4, bf16[2,72,512]{2,1,0:T(8,128)(2,1)} %copy-done.3, ...), custom_call_target="tpu_custom_call" | custom-call | tf_op jit(solution)/shard_map/panels/pallas_call | solution.py:422
  (7 shorter events, 0.1 us)
Async XLA Ops:
  0.6 0.7 %copy-start.10 = (f32[64]{0:T(128)S(1)}, f32[64]{0:T(128)}, u32[]{:S(2)}) copy-start(f32[64]{0:T(128)} %param.5) | copy-start | bytes 772
  2.2 8.0 %collective-permute-start = (bf16[1,72,512]{2,1,0:T(8,128)(2,1)S(1)}, bf16[1,72,512]{2,1,0:T(8,128)(2,1)S(1)}, u32[]{:S(2)}, u32[]{:S(2)}) collective-permute-start(bf16[1,72,512]{2,1,0:T(8,128)(2,1)S(1)} %maximum_bitcast_fusion), channel_id=1, source_target_pairs={{0,16},{4,20},{8,24},{12,28},{16,0},{20,4},{24,8},{28,12},{1,17},{... | collective-permute-start | bytes 221192 | tf_op jit(solution)/shard_map/ppermute | solution.py:396
  10.2 5.2 %collective-permute-start.1 = (bf16[2,72,512]{2,1,0:T(8,128)(2,1)S(1)}, bf16[2,72,512]{2,1,0:T(8,128)(2,1)S(1)}, u32[]{:S(2)}, u32[]{:S(2)}) collective-permute-start(bf16[2,72,512]{2,1,0:T(8,128)(2,1)S(1)} %pad_maximum_fusion.2), channel_id=1, source_target_pairs={{0,8},{4,12},{8,0},{12,4},{16,24},{20,28},{24,16},{28,20},{1,9},{5... | collective-permute-start | bytes 442376 | tf_op jit(solution)/shard_map/ppermute | solution.py:396
  15.4 1.8 %copy-start = (bf16[4,72,512]{2,1,0:T(8,128)(2,1)}, bf16[4,72,512]{2,1,0:T(8,128)(2,1)S(1)}, u32[]{:S(2)}) copy-start(bf16[4,72,512]{2,1,0:T(8,128)(2,1)S(1)} %pad_maximum_fusion.refs_0_) | copy-start | bytes 884740
  15.4 6.8 %collective-permute-start.2 = (bf16[4,72,512]{2,1,0:T(8,128)(2,1)S(1)}, bf16[4,72,512]{2,1,0:T(8,128)(2,1)S(1)}, u32[]{:S(2)}, u32[]{:S(2)}) collective-permute-start(bf16[4,72,512]{2,1,0:T(8,128)(2,1)S(1)} %pad_maximum_fusion.refs_0_), channel_id=1, source_target_pairs={{0,4},{4,0},{8,12},{12,8},{16,20},{20,16},{24,28},{28,24},{1,5},{5... | collective-permute-start | bytes 884744 | tf_op jit(solution)/shard_map/ppermute | solution.py:396
  17.3 11.6 %copy-start.1 = (bf16[3,72,512]{2,1,0:T(8,128)(2,1)}, bf16[3,72,512]{2,1,0:T(8,128)(2,1)S(1)}, u32[]{:S(2)}) copy-start(bf16[3,72,512]{2,1,0:T(8,128)(2,1)S(1)} %pad_maximum_fusion.1.refs_2_) | copy-start | bytes 663556
  17.3 7.6 %collective-permute-start.3 = (bf16[3,72,512]{2,1,0:T(8,128)(2,1)S(1)}, bf16[3,72,512]{2,1,0:T(8,128)(2,1)S(1)}, u32[]{:S(2)}, u32[]{:S(2)}) collective-permute-start(bf16[3,72,512]{2,1,0:T(8,128)(2,1)S(1)} %pad_maximum_fusion.1.refs_2_), channel_id=1, source_target_pairs={{0,2},{1,3},{2,0},{3,1},{4,6},{5,7},{6,4},{7,5},{8,10},{9,11},{10,... | collective-permute-start | bytes 663560 | tf_op jit(solution)/shard_map/ppermute | solution.py:396
  22.2 6.6 %copy-start.2 = (bf16[4,72,512]{2,1,0:T(8,128)(2,1)}, bf16[4,72,512]{2,1,0:T(8,128)(2,1)S(1)}, u32[]{:S(2)}) copy-start(bf16[4,72,512]{2,1,0:T(8,128)(2,1)S(1)} %collective-permute-done.2.refs_1_) | copy-start | bytes 884740
  22.2 6.6 %copy-start.3 = (bf16[2,72,512]{2,1,0:T(8,128)(2,1)}, bf16[2,72,512]{2,1,0:T(8,128)(2,1)S(1)}, u32[]{:S(2)}) copy-start(bf16[2,72,512]{2,1,0:T(8,128)(2,1)S(1)} %dynamic-slice_bitcast_fusion.refs_4_) | copy-start | bytes 442372
  22.2 5.2 %collective-permute-start.4 = (bf16[2,72,512]{2,1,0:T(8,128)(2,1)S(1)}, bf16[2,72,512]{2,1,0:T(8,128)(2,1)S(1)}, u32[]{:S(2)}, u32[]{:S(2)}) collective-permute-start(bf16[2,72,512]{2,1,0:T(8,128)(2,1)S(1)} %dynamic-slice_bitcast_fusion.refs_4_), channel_id=1, source_target_pairs={{0,2},{1,3},{2,0},{3,1},{4,6},{5,7},{6,4},{7,5},{8,10},{9,11},{10,... | collective-permute-start | bytes 442376 | tf_op jit(solution)/shard_map/ppermute | solution.py:396
  24.0 3.4 %collective-permute-start.5 = (bf16[3,72,512]{2,1,0:T(8,128)(2,1)S(1)}, bf16[3,72,512]{2,1,0:T(8,128)(2,1)S(1)}, u32[]{:S(2)}, u32[]{:S(2)}) collective-permute-start(bf16[3,72,512]{2,1,0:T(8,128)(2,1)S(1)} %pad_maximum_fusion.1.refs_2_), channel_id=1, source_target_pairs={{0,1},{1,0},{2,3},{3,2},{4,5},{5,4},{6,7},{7,6},{8,9},{9,8},{10,11... | collective-permute-start | bytes 663560 | tf_op jit(solution)/shard_map/ppermute | solution.py:396
  24.8 4.0 %copy-start.4 = (bf16[3,72,512]{2,1,0:T(8,128)(2,1)}, bf16[3,72,512]{2,1,0:T(8,128)(2,1)S(1)}, u32[]{:S(2)}) copy-start(bf16[3,72,512]{2,1,0:T(8,128)(2,1)S(1)} %collective-permute-done.3.refs_3_) | copy-start | bytes 663556
  24.8 2.6 %collective-permute-start.6 = (bf16[3,72,512]{2,1,0:T(8,128)(2,1)S(1)}, bf16[3,72,512]{2,1,0:T(8,128)(2,1)S(1)}, u32[]{:S(2)}, u32[]{:S(2)}) collective-permute-start(bf16[3,72,512]{2,1,0:T(8,128)(2,1)S(1)} %collective-permute-done.3.refs_3_), channel_id=1, source_target_pairs={{0,1},{1,0},{2,3},{3,2},{4,5},{5,4},{6,7},{7,6},{8,9},{9,8},{10,11... | collective-permute-start | bytes 663560 | tf_op jit(solution)/shard_map/ppermute | solution.py:396
  24.8 2.7 %collective-permute-start.7 = (bf16[2,72,512]{2,1,0:T(8,128)(2,1)S(1)}, bf16[2,72,512]{2,1,0:T(8,128)(2,1)S(1)}, u32[]{:S(2)}, u32[]{:S(2)}) collective-permute-start(bf16[2,72,512]{2,1,0:T(8,128)(2,1)S(1)} %dynamic-slice_bitcast_fusion.refs_4_), channel_id=1, source_target_pairs={{0,1},{1,0},{2,3},{3,2},{4,5},{5,4},{6,7},{7,6},{8,9},{9,8},{10,11... | collective-permute-start | bytes 442376 | tf_op jit(solution)/shard_map/ppermute | solution.py:396
  27.5 1.4 %copy-start.7 = (bf16[2,72,512]{2,1,0:T(8,128)(2,1)}, bf16[2,72,512]{2,1,0:T(8,128)(2,1)S(1)}, u32[]{:S(2)}) copy-start(bf16[2,72,512]{2,1,0:T(8,128)(2,1)S(1)} %collective-permute-done.4.refs_5_) | copy-start | bytes 442372
  27.5 1.4 %collective-permute-start.8 = (bf16[2,72,512]{2,1,0:T(8,128)(2,1)S(1)}, bf16[2,72,512]{2,1,0:T(8,128)(2,1)S(1)}, u32[]{:S(2)}, u32[]{:S(2)}) collective-permute-start(bf16[2,72,512]{2,1,0:T(8,128)(2,1)S(1)} %collective-permute-done.4.refs_5_), channel_id=1, source_target_pairs={{0,1},{1,0},{2,3},{3,2},{4,5},{5,4},{6,7},{7,6},{8,9},{9,8},{10,11... | collective-permute-start | bytes 442376 | tf_op jit(solution)/shard_map/ppermute | solution.py:396
  27.5 1.4 %copy-start.5 = (bf16[3,72,512]{2,1,0:T(8,128)(2,1)}, bf16[3,72,512]{2,1,0:T(8,128)(2,1)S(1)}, u32[]{:S(2)}) copy-start(bf16[3,72,512]{2,1,0:T(8,128)(2,1)S(1)} %collective-permute-done.5.refs_6_) | copy-start | bytes 663556
  27.5 1.4 %copy-start.6 = (bf16[3,72,512]{2,1,0:T(8,128)(2,1)}, bf16[3,72,512]{2,1,0:T(8,128)(2,1)S(1)}, u32[]{:S(2)}) copy-start(bf16[3,72,512]{2,1,0:T(8,128)(2,1)S(1)} %collective-permute-done.6.refs_7_) | copy-start | bytes 663556
  27.5 1.4 %copy-start.8 = (bf16[2,72,512]{2,1,0:T(8,128)(2,1)}, bf16[2,72,512]{2,1,0:T(8,128)(2,1)S(1)}, u32[]{:S(2)}) copy-start(bf16[2,72,512]{2,1,0:T(8,128)(2,1)S(1)} %collective-permute-done.7.refs_8_) | copy-start | bytes 442372
  28.9 0.7 %copy-start.9 = (bf16[2,72,512]{2,1,0:T(8,128)(2,1)}, bf16[2,72,512]{2,1,0:T(8,128)(2,1)S(1)}, u32[]{:S(2)}) copy-start(bf16[2,72,512]{2,1,0:T(8,128)(2,1)S(1)} %collective-permute-done.8.refs_9_) | copy-start | bytes 442372

commit v7 on v6

--- a/solution.py
+++ b/solution.py
@@ -397,8 +397,17 @@
 
     near = packed(features, slot_of_ray, noise)[None]
     own = near
-    for bit in reversed(range(1, row_bits)):
-        near = jnp.concatenate([near, other(near, "row", bit)])
+    if row_bits <= 3:
+        pairs = row_count // 2
+        steps = [2 * reversed_bits(k, row_bits - 1) for k in range(1, pairs)]
+        direct = {
+            step: lax.ppermute(own, "row", [(k, k ^ step) for k in range(row_count)])
+            for step in sorted(steps, reverse=True)
+        }
+        near = jnp.concatenate([own] + [direct[step] for step in steps])
+    else:
+        for bit in reversed(range(1, row_bits)):
+            near = jnp.concatenate([near, other(near, "row", bit)])
     high_bits = row_bits - 1 - bits_of(lead_pairs)
     group = reversed_bits(row_index >> (row_bits - high_bits), high_bits)
 

time: 60.2 us -> 58.6 us (0.973)
  waiting for transfers between devices: 16 us -> 13.8 us
  starting transfers between devices: 10.5 us -> 11.3 us
    ppermute x9 -> x7, waiting for transfers between devices: 16 us -> 8.59 us  [other(): return lax.ppermute(value, axis, [(k, k ^ 1 << bit) for k in range(count)])]
    ppermute x0 -> x3, starting transfers between devices: none -> 5.7 us  [shards(): lax.ppermute(own, 'row', [(k, k ^ step) for k in range(row_count)])]
    ppermute x0 -> x3, waiting for transfers between devices: none -> 5.18 us  [shards(): lax.ppermute(own, 'row', [(k, k ^ step) for k in range(row_count)])]
    ppermute x9 -> x7, starting transfers between devices: 10.5 us -> 5.64 us  [other(): return lax.ppermute(value, axis, [(k, k ^ 1 << bit) for k in range(count)])]
  transfers between devices with their start and end apart: 9 -> 10, of which waited for: 6 -> 6; matrix products, arithmetic and copies ran while one was open for 0% -> 0% of each run, Pallas kernels for 0% -> 0%
where the time goes in v7:
time: 58.6 us; the launch traced here: 58.4 us
  Pallas kernels  30.2 us (52%)
  waiting for transfers between devices  13.8 us (24%)
  starting transfers between devices  11.3 us (19%)
  other arithmetic  1.6 us (3%)
  between operations  0.8 us (1%)
  local copies, waits for them, and re-layouts  0.71 us (1%)
    pallas_call x1, Pallas kernels, shards(): pl.pallas_call(functools.partial(kernel, ray_dev=ray_dev, row_count=row_c...  30.2 us
    ppermute x7, waiting for transfers between devices, other(): return lax.ppermute(value, axis, [(k, k ^ 1 << bit) for k in range(count)])  8.59 us
    ppermute x3, starting transfers between devices, shards(): lax.ppermute(own, 'row', [(k, k ^ step) for k in range(row_count)])  5.7 us
    ppermute x7, starting transfers between devices, other(): return lax.ppermute(value, axis, [(k, k ^ 1 << bit) for k in range(count)])  5.64 us
    ppermute x3, waiting for transfers between devices, shards(): lax.ppermute(own, 'row', [(k, k ^ step) for k in range(row_count)])  5.18 us
  transfers between devices with their start and end apart: 10, of which 6 were waited for; matrix products, arithmetic and copies ran while one was open for 0% of the time, Pallas kernels for 0%

profile of v7, /device:TPU:0, one launch (start us, length us, event | category | flops | bytes accessed | tf_op | source)
XLA Modules:
  0.0 58.4 jit_solution(6664591964260861135)
XLA Ops:
  0.6 0.0 copy-start.10
  0.6 0.7 %convert_bitcast_fusion = bf16[1,64]{1,0:T(2,128)(2,1)S(1)} fusion(s32[64]{0:T(128)} %param.4), kind=kLoop, calls=%fused_computation.27 | loop fusion | flops 128 | bytes 384 | tf_op jit(solution)/shard_map/stack | solution.py:378
  1.3 0.0 copy-done.10
  1.3 0.8 %maximum_bitcast_fusion = bf16[1,72,512]{2,1,0:T(8,128)(2,1)S(1)} fusion(bf16[8,512]{1,0:T(8,128)(2,1)S(1)} %fusion.8, bf16[64,512]{1,0:T(8,128)(2,1)} %param.3), kind=kLoop, calls=%fused_computation.4 | loop fusion | flops 147456 | bytes 147456 | tf_op jit(solution)/shard_map/broadcast_in_dim | solution.py:398
  2.2 5.1 %collective-permute-start.2 = (bf16[1,72,512]{2,1,0:T(8,128)(2,1)S(1)}, bf16[1,72,512]{2,1,0:T(8,128)(2,1)S(1)}, u32[]{:S(2)}, u32[]{:S(2)}) collective-permute-start(bf16[1,72,512]{2,1,0:T(8,128)(2,1)S(1)} %maximum_bitcast_fusion), channel_id=1, source_target_pairs={{0,24},{4,28},{8,16},{12,20},{16,8},{20,12},{24,0},{28,4},{1,25},{... | collective-permute-start | bytes 221192 | tf_op jit(solution)/shard_map/ppermute | solution.py:404
  7.3 0.0 collective-permute-start.1
  7.3 0.6 %collective-permute-start = (bf16[1,72,512]{2,1,0:T(8,128)(2,1)S(1)}, bf16[1,72,512]{2,1,0:T(8,128)(2,1)S(1)}, u32[]{:S(2)}, u32[]{:S(2)}) collective-permute-start(bf16[1,72,512]{2,1,0:T(8,128)(2,1)S(1)} %maximum_bitcast_fusion), channel_id=1, source_target_pairs={{0,16},{4,20},{8,24},{12,28},{16,0},{20,4},{24,8},{28,12},{1,17},{... | collective-permute-start | bytes 221192 | tf_op jit(solution)/shard_map/ppermute | solution.py:404
  7.9 2.5 %collective-permute-done.2 = bf16[1,72,512]{2,1,0:T(8,128)(2,1)S(1)} collective-permute-done((bf16[1,72,512]{2,1,0:T(8,128)(2,1)S(1)}, bf16[1,72,512]{2,1,0:T(8,128)(2,1)S(1)}, u32[]{:S(2)}, u32[]{:S(2)}) %collective-permute-start.2) | collective-permute-done | bytes 73760 | tf_op jit(solution)/shard_map/ppermute | solution.py:404
  10.4 1.9 %collective-permute-done.1 = bf16[1,72,512]{2,1,0:T(8,128)(2,1)S(1)} collective-permute-done((bf16[1,72,512]{2,1,0:T(8,128)(2,1)S(1)}, bf16[1,72,512]{2,1,0:T(8,128)(2,1)S(1)}, u32[]{:S(2)}, u32[]{:S(2)}) %collective-permute-start.1) | collective-permute-done | bytes 73760 | tf_op jit(solution)/shard_map/ppermute | solution.py:404
  12.3 0.8 %collective-permute-done = bf16[1,72,512]{2,1,0:T(8,128)(2,1)S(1)} collective-permute-done((bf16[1,72,512]{2,1,0:T(8,128)(2,1)S(1)}, bf16[1,72,512]{2,1,0:T(8,128)(2,1)S(1)}, u32[]{:S(2)}, u32[]{:S(2)}) %collective-permute-start) | collective-permute-done | bytes 73760 | tf_op jit(solution)/shard_map/ppermute | solution.py:404
  13.1 0.0 copy-start
  13.1 1.6 %collective-permute-start.3 = (bf16[4,72,512]{2,1,0:T(8,128)(2,1)S(1)}, bf16[4,72,512]{2,1,0:T(8,128)(2,1)S(1)}, u32[]{:S(2)}, u32[]{:S(2)}) collective-permute-start(bf16[4,72,512]{2,1,0:T(8,128)(2,1)S(1)} %pad_maximum_fusion.refs_0_), channel_id=1, source_target_pairs={{0,4},{4,0},{8,12},{12,8},{16,20},{20,16},{24,28},{28,24},{1,5},{5... | collective-permute-start | bytes 884744 | tf_op jit(solution)/shard_map/ppermute | solution.py:396
  14.8 0.0 copy-done
  14.8 0.0 copy-start.1
  14.8 1.6 %collective-permute-start.4 = (bf16[3,72,512]{2,1,0:T(8,128)(2,1)S(1)}, bf16[3,72,512]{2,1,0:T(8,128)(2,1)S(1)}, u32[]{:S(2)}, u32[]{:S(2)}) collective-permute-start(bf16[3,72,512]{2,1,0:T(8,128)(2,1)S(1)} %pad_maximum_fusion.1.refs_2_), channel_id=1, source_target_pairs={{0,2},{1,3},{2,0},{3,1},{4,6},{5,7},{6,4},{7,5},{8,10},{9,11},{10,... | collective-permute-start | bytes 663560 | tf_op jit(solution)/shard_map/ppermute | solution.py:396
  16.4 4.5 %collective-permute-done.3.refs_1_ = bf16[4,72,512]{2,1,0:T(8,128)(2,1)S(1)} collective-permute-done((bf16[4,72,512]{2,1,0:T(8,128)(2,1)S(1)}, bf16[4,72,512]{2,1,0:T(8,128)(2,1)S(1)}, u32[]{:S(2)}, u32[]{:S(2)}) %collective-permute-start.3) | collective-permute-done | bytes 294944 | tf_op jit(solution)/shard_map/ppermute | solution.py:396
  20.9 0.0 copy-start.2
  20.9 0.0 copy-start.3
  20.9 1.8 %collective-permute-start.5 = (bf16[2,72,512]{2,1,0:T(8,128)(2,1)S(1)}, bf16[2,72,512]{2,1,0:T(8,128)(2,1)S(1)}, u32[]{:S(2)}, u32[]{:S(2)}) collective-permute-start(bf16[2,72,512]{2,1,0:T(8,128)(2,1)S(1)} %dynamic-slice_bitcast_fusion.refs_4_), channel_id=1, source_target_pairs={{0,2},{1,3},{2,0},{3,1},{4,6},{5,7},{6,4},{7,5},{8,10},{9,11},{10,... | collective-permute-start | bytes 442376 | tf_op jit(solution)/shard_map/ppermute | solution.py:396
  22.7 0.0 collective-permute-start.6
  22.7 0.0 collective-permute-done.4.refs_3_
  22.8 0.0 copy-start.4
  22.8 0.5 collective-permute-start.7
  23.3 0.1 collective-permute-start.8
  23.3 2.8 %collective-permute-done.5.refs_5_ = bf16[2,72,512]{2,1,0:T(8,128)(2,1)S(1)} collective-permute-done((bf16[2,72,512]{2,1,0:T(8,128)(2,1)S(1)}, bf16[2,72,512]{2,1,0:T(8,128)(2,1)S(1)}, u32[]{:S(2)}, u32[]{:S(2)}) %collective-permute-start.5) | collective-permute-done | bytes 147488 | tf_op jit(solution)/shard_map/ppermute | solution.py:396
  26.1 0.0 copy-start.7
  26.1 0.0 collective-permute-start.9
  26.1 0.0 collective-permute-done.6.refs_6_
  26.1 0.0 copy-start.5
  26.1 0.0 collective-permute-done.7.refs_7_
  26.2 0.0 copy-start.6
  26.2 0.0 collective-permute-done.8.refs_8_
  26.2 0.0 copy-start.8
  26.2 1.3 %collective-permute-done.9.refs_9_ = bf16[2,72,512]{2,1,0:T(8,128)(2,1)S(1)} collective-permute-done((bf16[2,72,512]{2,1,0:T(8,128)(2,1)S(1)}, bf16[2,72,512]{2,1,0:T(8,128)(2,1)S(1)}, u32[]{:S(2)}, u32[]{:S(2)}) %collective-permute-start.9) | collective-permute-done | bytes 147488 | tf_op jit(solution)/shard_map/ppermute | solution.py:396
  27.5 0.0 copy-done.1
  27.5 0.0 copy-done.2
  27.5 0.0 copy-done.3
  27.5 0.0 copy-done.4
  27.5 0.0 copy-done.7
  27.5 0.0 copy-done.5
  27.5 0.0 copy-done.6
  27.6 0.0 copy-done.8
  27.6 0.0 copy-start.9
  27.6 0.6 %copy-done.9 = bf16[2,72,512]{2,1,0:T(8,128)(2,1)} copy-done((bf16[2,72,512]{2,1,0:T(8,128)(2,1)}, bf16[2,72,512]{2,1,0:T(8,128)(2,1)S(1)}, u32[]{:S(2)}) %copy-start.9) | copy-done | bytes 147480
  28.2 30.2 %panels.1 = (f32[256,1,512]{2,1,0:T(1,128)}, f32[256,1024]{1,0:T(8,128)}) custom-call(bf16[4,72,512]{2,1,0:T(8,128)(2,1)} %copy-done, bf16[4,72,512]{2,1,0:T(8,128)(2,1)} %copy-done.2, bf16[3,72,512]{2,1,0:T(8,128)(2,1)} %copy-done.1, bf16[3,72,512]{2,1,0:T(8,128)(2,1)} %copy-done.4, bf16[2,72,512]{2,1,0:T(8,128)(2,1)} %copy-done.3, ...), custom_call_target="tpu_custom_call" | custom-call | tf_op jit(solution)/shard_map/panels/pallas_call | solution.py:431
  (6 shorter events, 0.1 us)
Async XLA Ops:
  0.6 0.7 %copy-start.10 = (f32[64]{0:T(128)S(1)}, f32[64]{0:T(128)}, u32[]{:S(2)}) copy-start(f32[64]{0:T(128)} %param.5) | copy-start | bytes 772
  2.2 8.2 %collective-permute-start.2 = (bf16[1,72,512]{2,1,0:T(8,128)(2,1)S(1)}, bf16[1,72,512]{2,1,0:T(8,128)(2,1)S(1)}, u32[]{:S(2)}, u32[]{:S(2)}) collective-permute-start(bf16[1,72,512]{2,1,0:T(8,128)(2,1)S(1)} %maximum_bitcast_fusion), channel_id=1, source_target_pairs={{0,24},{4,28},{8,16},{12,20},{16,8},{20,12},{24,0},{28,4},{1,25},{... | collective-permute-start | bytes 221192 | tf_op jit(solution)/shard_map/ppermute | solution.py:404
  7.3 5.1 %collective-permute-start.1 = (bf16[1,72,512]{2,1,0:T(8,128)(2,1)S(1)}, bf16[1,72,512]{2,1,0:T(8,128)(2,1)S(1)}, u32[]{:S(2)}, u32[]{:S(2)}) collective-permute-start(bf16[1,72,512]{2,1,0:T(8,128)(2,1)S(1)} %maximum_bitcast_fusion), channel_id=1, source_target_pairs={{0,8},{4,12},{8,0},{12,4},{16,24},{20,28},{24,16},{28,20},{1,9},{5... | collective-permute-start | bytes 221192 | tf_op jit(solution)/shard_map/ppermute | solution.py:404
  7.3 5.8 %collective-permute-start = (bf16[1,72,512]{2,1,0:T(8,128)(2,1)S(1)}, bf16[1,72,512]{2,1,0:T(8,128)(2,1)S(1)}, u32[]{:S(2)}, u32[]{:S(2)}) collective-permute-start(bf16[1,72,512]{2,1,0:T(8,128)(2,1)S(1)} %maximum_bitcast_fusion), channel_id=1, source_target_pairs={{0,16},{4,20},{8,24},{12,28},{16,0},{20,4},{24,8},{28,12},{1,17},{... | collective-permute-start | bytes 221192 | tf_op jit(solution)/shard_map/ppermute | solution.py:404
  13.1 1.7 %copy-start = (bf16[4,72,512]{2,1,0:T(8,128)(2,1)}, bf16[4,72,512]{2,1,0:T(8,128)(2,1)S(1)}, u32[]{:S(2)}) copy-start(bf16[4,72,512]{2,1,0:T(8,128)(2,1)S(1)} %pad_maximum_fusion.refs_0_) | copy-start | bytes 884740
  13.1 7.8 %collective-permute-start.3 = (bf16[4,72,512]{2,1,0:T(8,128)(2,1)S(1)}, bf16[4,72,512]{2,1,0:T(8,128)(2,1)S(1)}, u32[]{:S(2)}, u32[]{:S(2)}) collective-permute-start(bf16[4,72,512]{2,1,0:T(8,128)(2,1)S(1)} %pad_maximum_fusion.refs_0_), channel_id=1, source_target_pairs={{0,4},{4,0},{8,12},{12,8},{16,20},{20,16},{24,28},{28,24},{1,5},{5... | collective-permute-start | bytes 884744 | tf_op jit(solution)/shard_map/ppermute | solution.py:396
  14.8 12.7 %copy-start.1 = (bf16[3,72,512]{2,1,0:T(8,128)(2,1)}, bf16[3,72,512]{2,1,0:T(8,128)(2,1)S(1)}, u32[]{:S(2)}) copy-start(bf16[3,72,512]{2,1,0:T(8,128)(2,1)S(1)} %pad_maximum_fusion.1.refs_2_) | copy-start | bytes 663556
  14.8 7.9 %collective-permute-start.4 = (bf16[3,72,512]{2,1,0:T(8,128)(2,1)S(1)}, bf16[3,72,512]{2,1,0:T(8,128)(2,1)S(1)}, u32[]{:S(2)}, u32[]{:S(2)}) collective-permute-start(bf16[3,72,512]{2,1,0:T(8,128)(2,1)S(1)} %pad_maximum_fusion.1.refs_2_), channel_id=1, source_target_pairs={{0,2},{1,3},{2,0},{3,1},{4,6},{5,7},{6,4},{7,5},{8,10},{9,11},{10,... | collective-permute-start | bytes 663560 | tf_op jit(solution)/shard_map/ppermute | solution.py:396
  20.9 6.6 %copy-start.2 = (bf16[4,72,512]{2,1,0:T(8,128)(2,1)}, bf16[4,72,512]{2,1,0:T(8,128)(2,1)S(1)}, u32[]{:S(2)}) copy-start(bf16[4,72,512]{2,1,0:T(8,128)(2,1)S(1)} %collective-permute-done.3.refs_1_) | copy-start | bytes 884740
  20.9 6.6 %copy-start.3 = (bf16[2,72,512]{2,1,0:T(8,128)(2,1)}, bf16[2,72,512]{2,1,0:T(8,128)(2,1)S(1)}, u32[]{:S(2)}) copy-start(bf16[2,72,512]{2,1,0:T(8,128)(2,1)S(1)} %dynamic-slice_bitcast_fusion.refs_4_) | copy-start | bytes 442372
  20.9 5.2 %collective-permute-start.5 = (bf16[2,72,512]{2,1,0:T(8,128)(2,1)S(1)}, bf16[2,72,512]{2,1,0:T(8,128)(2,1)S(1)}, u32[]{:S(2)}, u32[]{:S(2)}) collective-permute-start(bf16[2,72,512]{2,1,0:T(8,128)(2,1)S(1)} %dynamic-slice_bitcast_fusion.refs_4_), channel_id=1, source_target_pairs={{0,2},{1,3},{2,0},{3,1},{4,6},{5,7},{6,4},{7,5},{8,10},{9,11},{10,... | collective-permute-start | bytes 442376 | tf_op jit(solution)/shard_map/ppermute | solution.py:396
  22.7 3.4 %collective-permute-start.6 = (bf16[3,72,512]{2,1,0:T(8,128)(2,1)S(1)}, bf16[3,72,512]{2,1,0:T(8,128)(2,1)S(1)}, u32[]{:S(2)}, u32[]{:S(2)}) collective-permute-start(bf16[3,72,512]{2,1,0:T(8,128)(2,1)S(1)} %pad_maximum_fusion.1.refs_2_), channel_id=1, source_target_pairs={{0,1},{1,0},{2,3},{3,2},{4,5},{5,4},{6,7},{7,6},{8,9},{9,8},{10,11... | collective-permute-start | bytes 663560 | tf_op jit(solution)/shard_map/ppermute | solution.py:396
  22.8 4.8 %copy-start.4 = (bf16[3,72,512]{2,1,0:T(8,128)(2,1)}, bf16[3,72,512]{2,1,0:T(8,128)(2,1)S(1)}, u32[]{:S(2)}) copy-start(bf16[3,72,512]{2,1,0:T(8,128)(2,1)S(1)} %collective-permute-done.4.refs_3_) | copy-start | bytes 663556
  22.8 3.4 %collective-permute-start.7 = (bf16[3,72,512]{2,1,0:T(8,128)(2,1)S(1)}, bf16[3,72,512]{2,1,0:T(8,128)(2,1)S(1)}, u32[]{:S(2)}, u32[]{:S(2)}) collective-permute-start(bf16[3,72,512]{2,1,0:T(8,128)(2,1)S(1)} %collective-permute-done.4.refs_3_), channel_id=1, source_target_pairs={{0,1},{1,0},{2,3},{3,2},{4,5},{5,4},{6,7},{7,6},{8,9},{9,8},{10,11... | collective-permute-start | bytes 663560 | tf_op jit(solution)/shard_map/ppermute | solution.py:396
  23.3 2.9 %collective-permute-start.8 = (bf16[2,72,512]{2,1,0:T(8,128)(2,1)S(1)}, bf16[2,72,512]{2,1,0:T(8,128)(2,1)S(1)}, u32[]{:S(2)}, u32[]{:S(2)}) collective-permute-start(bf16[2,72,512]{2,1,0:T(8,128)(2,1)S(1)} %dynamic-slice_bitcast_fusion.refs_4_), channel_id=1, source_target_pairs={{0,1},{1,0},{2,3},{3,2},{4,5},{5,4},{6,7},{7,6},{8,9},{9,8},{10,11... | collective-permute-start | bytes 442376 | tf_op jit(solution)/shard_map/ppermute | solution.py:396
  26.1 1.4 %copy-start.7 = (bf16[2,72,512]{2,1,0:T(8,128)(2,1)}, bf16[2,72,512]{2,1,0:T(8,128)(2,1)S(1)}, u32[]{:S(2)}) copy-start(bf16[2,72,512]{2,1,0:T(8,128)(2,1)S(1)} %collective-permute-done.5.refs_5_) | copy-start | bytes 442372
  26.1 1.4 %collective-permute-start.9 = (bf16[2,72,512]{2,1,0:T(8,128)(2,1)S(1)}, bf16[2,72,512]{2,1,0:T(8,128)(2,1)S(1)}, u32[]{:S(2)}, u32[]{:S(2)}) collective-permute-start(bf16[2,72,512]{2,1,0:T(8,128)(2,1)S(1)} %collective-permute-done.5.refs_5_), channel_id=1, source_target_pairs={{0,1},{1,0},{2,3},{3,2},{4,5},{5,4},{6,7},{7,6},{8,9},{9,8},{10,11... | collective-permute-start | bytes 442376 | tf_op jit(solution)/shard_map/ppermute | solution.py:396
  26.1 1.4 %copy-start.5 = (bf16[3,72,512]{2,1,0:T(8,128)(2,1)}, bf16[3,72,512]{2,1,0:T(8,128)(2,1)S(1)}, u32[]{:S(2)}) copy-start(bf16[3,72,512]{2,1,0:T(8,128)(2,1)S(1)} %collective-permute-done.6.refs_6_) | copy-start | bytes 663556
  26.2 1.4 %copy-start.6 = (bf16[3,72,512]{2,1,0:T(8,128)(2,1)}, bf16[3,72,512]{2,1,0:T(8,128)(2,1)S(1)}, u32[]{:S(2)}) copy-start(bf16[3,72,512]{2,1,0:T(8,128)(2,1)S(1)} %collective-permute-done.7.refs_7_) | copy-start | bytes 663556
  26.2 1.4 %copy-start.8 = (bf16[2,72,512]{2,1,0:T(8,128)(2,1)}, bf16[2,72,512]{2,1,0:T(8,128)(2,1)S(1)}, u32[]{:S(2)}) copy-start(bf16[2,72,512]{2,1,0:T(8,128)(2,1)S(1)} %collective-permute-done.8.refs_8_) | copy-start | bytes 442372
  27.6 0.7 %copy-start.9 = (bf16[2,72,512]{2,1,0:T(8,128)(2,1)}, bf16[2,72,512]{2,1,0:T(8,128)(2,1)S(1)}, u32[]{:S(2)}) copy-start(bf16[2,72,512]{2,1,0:T(8,128)(2,1)S(1)} %collective-permute-done.9.refs_9_) | copy-start | bytes 442372
